TPU v7x, 256 devices: a whole 4x4x8 slice. The times are simulated.
256 devices in a mesh: blk: 32 (over z, x), grp: 8 (over y, core).
Axes of the slice: x: 4, y: 4, z: 8, core: 2. Of those that a mesh axis runs over, the one named last changes fastest.
Arguments:
- queries: bfloat16 [131072, 512], P(('blk', 'grp')), may hold values from -64 to 64
- keys: bfloat16 [131072, 128], P(('blk', 'grp')), may hold values from -8 to 8
- values: bfloat16 [131072, 128], P(('blk', 'grp')), may hold values from -6 to 6
- selected: int32 [256, 16], replicated, may hold values from 0 to 2047, as said below
- key_in: bfloat16 [4096, 256], replicated, may hold values from -0.09375 to 0.09375
- key_out: bfloat16 [256, 128], replicated, may hold values from -0.375 to 0.375
- value_in: bfloat16 [4096, 256], replicated, may hold values from -0.09375 to 0.09375
- value_out: bfloat16 [256, 128], replicated, may hold values from -0.375 to 0.375
- positions: bfloat16 [2, 32, 128], replicated, may hold values from -5 to 5
- gate_weight: bfloat16 [512, 12], replicated, may hold values from -0.25 to 0.25
Outputs:
- attended: bfloat16 [131072, 512], P(('blk', 'grp'))
Inputs may be any that keep to these rules, and one draw needn't show every extreme that they name: `selected`: row d lists 16 different fine blocks. Write r = 64 and b = d // 8. Entry 0 is the first fine block of group d's own tokens. Every listed block j with j // r different from b has j // r < b, and no two listed blocks share a value of j // r other than b. Blocks with j // r == b may lie after group d's tokens.
All inputs are finite; a program needn't handle non-finite values.
Results may differ from a plain program's by a relative error of at most 0.004.
Values may be sent and summed in bfloat16 or wider, within the bound.
No kernel may reach another device: no remote copies, remote signals or barrier semaphores. Data moves between devices by JAX's collectives and lax.ppermute only.
A program may use at most 64 MiB of HBM per device.

v0:
```python
import jax
import jax.numpy as jnp
from jax import lax
from jax.sharding import PartitionSpec as P

HEAD_DIM = 128
HEADS = 4
CMP_BLOCK = 32
SEL_BLOCK = 64
TOPN = 16
WINDOW = 512


NEG = -1e30


def in_order(blocks, dim):
    blocks = jnp.moveaxis(blocks, 0, dim)
    lengths = blocks.shape
    return blocks.reshape(*lengths[:dim], lengths[dim] * lengths[dim + 1], *lengths[dim + 2 :])


def copy_for_each(array, axis):
    copies = jnp.broadcast_to(array, (lax.axis_size(axis), *array.shape))
    return lax.all_to_all(copies, axis, split_axis=0, concat_axis=0, tiled=True)


def gathered_copies(array, axis, dim):
    return in_order(copy_for_each(array, axis), dim)


def side_by_side(arrays, axis, dim, along):
    both = jnp.concatenate(arrays, axis=along)
    whole, at, outs = (gathered_copies(both, axis, dim), 0, [])
    for a in arrays:
        outs.append(lax.slice_in_dim(whole, at, at + a.shape[along], axis=along))
        at += a.shape[along]
    return tuple(outs)


def in_one_piece(arrays, axis, dim, along):
    widths = [a.shape[along] for a in arrays]
    both = jnp.concatenate(arrays, axis=along)
    whole = lax.all_gather(both, axis, axis=dim, tiled=True)
    return tuple(jnp.split(whole, [sum(widths[:k]) for k in range(1, len(widths))], axis=along))


def from_behind(block, axis, distance):
    devices = range(lax.axis_size(axis))
    route = [(i - distance, i) for i in devices if i - distance in devices]
    return lax.ppermute(block, axis, route)


def compress(tokens, shift, w_in, w_out):
    count = tokens.shape[0] // CMP_BLOCK
    mixed = (
        tokens.astype(jnp.float32).reshape(count, CMP_BLOCK, HEAD_DIM)
        + shift.astype(jnp.float32)[None]
    )
    flat = mixed.astype(jnp.bfloat16).reshape(count, CMP_BLOCK * HEAD_DIM)
    hidden = jax.nn.silu(jnp.dot(flat, w_in, preferred_element_type=jnp.float32)).astype(
        jnp.bfloat16
    )
    return jnp.dot(hidden, w_out, preferred_element_type=jnp.float32).astype(jnp.bfloat16)


def attend(query_rows, query_pos, key_rows, value_rows, key_pos, span):
    scale = HEAD_DIM ** (-0.5)
    scores = (
        jnp.einsum("qhd,kd->qhk", query_rows, key_rows, preferred_element_type=jnp.float32) * scale
    )
    allowed = (
        (key_pos[None, :] <= query_pos[:, None])
        & (key_pos[None, :] > query_pos[:, None] - span)
        & (key_pos[None, :] >= 0)
    )
    scores = jnp.where(allowed[:, None, :], scores, NEG)
    top = jnp.max(scores, axis=2, keepdims=True)
    weights = jnp.exp(scores - top)
    total = jnp.sum(weights, axis=2)
    mixed = jnp.einsum(
        "qhk,kd->qhd", weights.astype(jnp.bfloat16), value_rows, preferred_element_type=jnp.float32
    )
    return mixed / total[..., None]


def make_fold(query_heads, query_pos):
    scale = HEAD_DIM ** (-0.5)
    toks = query_heads.shape[0]

    def fold(carry, piece, start):
        best, total, accum = carry
        piece_keys, piece_values = piece
        count = piece_keys.shape[0]
        key_end = jnp.arange(count, dtype=jnp.int32) * CMP_BLOCK + (CMP_BLOCK - 1)
        block_rows = toks
        while (
            block_rows > 32 and block_rows % 2 == 0 and (HEADS * block_rows * count * 4 > 1 << 24)
        ):
            block_rows = block_rows // 2
        steps = toks // block_rows

        def one(items):
            rows, pos, old_best, old_total, old_accum = items
            scores = (
                jnp.einsum("qhd,kd->qhk", rows, piece_keys, preferred_element_type=jnp.float32)
                * scale
            )
            scores = jnp.where((key_end[None, :] <= pos[:, None])[:, None, :], scores, NEG)
            new_best = jnp.maximum(old_best, jnp.max(scores, axis=2))
            weights = jnp.exp(scores - new_best[..., None])
            factor = jnp.exp(old_best - new_best)
            new_total = old_total * factor + jnp.sum(weights, axis=2)
            product = jnp.einsum(
                "qhk,kd->qhd",
                weights.astype(jnp.bfloat16),
                piece_values,
                preferred_element_type=jnp.float32,
            )
            return (new_best, new_total, old_accum * factor[..., None] + product)

        items = (
            query_heads.reshape(steps, block_rows, HEADS, HEAD_DIM),
            query_pos.reshape(steps, block_rows),
            best.reshape(steps, block_rows, HEADS),
            total.reshape(steps, block_rows, HEADS),
            accum.reshape(steps, block_rows, HEADS, HEAD_DIM),
        )
        new_best, new_total, new_accum = lax.map(one, items)
        return (
            new_best.reshape(toks, HEADS),
            new_total.reshape(toks, HEADS),
            new_accum.reshape(toks, HEADS, HEAD_DIM),
        )

    return fold


def per_device(
    queries, keys, values, selected, key_in, key_out, value_in, value_out, positions, gate_weight
):
    stretches = lax.axis_size("blk")
    group_size = lax.axis_size("grp")
    stretch = lax.axis_index("blk")
    column = lax.axis_index("grp")
    toks = queries.shape[0]
    seq_len = stretches * group_size * toks
    position = stretch * group_size + column
    query_pos = position * toks + jnp.arange(toks, dtype=jnp.int32)
    query_heads = queries.reshape(toks, HEADS, HEAD_DIM)
    row_keys, row_values = side_by_side((keys, values), "grp", 0, 1)
    fold = make_fold(query_heads, query_pos)
    start_state = (
        jnp.zeros((toks, HEADS), jnp.float32),
        jnp.ones((toks, HEADS), jnp.float32),
        jnp.zeros((toks, HEADS, HEAD_DIM), jnp.float32),
    )
    packed = (
        compress(keys, positions[0], key_in, key_out),
        compress(values, positions[1], value_in, value_out),
    )
    best, total, accum = fold(
        start_state, in_one_piece((packed[0], packed[1]), ("blk", "grp"), 0, 1), jnp.int32(0)
    )
    coarse = accum / total[..., None]
    per_row = group_size * toks // SEL_BLOCK
    row_blocks = jnp.concatenate([row_keys, row_values], axis=1).reshape(
        per_row, SEL_BLOCK, 2 * HEAD_DIM
    )
    requests = jnp.take(selected.reshape(stretches, group_size, TOPN), column, axis=1)
    targets = jnp.arange(stretches, dtype=jnp.int32)
    match = (requests // per_row == stretch) & (targets[:, None] != stretch)
    picked = jnp.sum(jnp.where(match, requests % per_row, 0), axis=1)
    outgoing = jnp.take(row_blocks, picked, axis=0)
    incoming = lax.all_to_all(outgoing, "blk", split_axis=0, concat_axis=0, tiled=True)
    mine = lax.dynamic_index_in_dim(selected, position, 0, keepdims=False)
    owners = mine // per_row
    nearby = jnp.take(row_blocks, mine % per_row, axis=0)
    remote = jnp.take(incoming, owners, axis=0)
    fine_rows = jnp.where((owners == stretch)[:, None, None], nearby, remote).reshape(
        TOPN * SEL_BLOCK, 2 * HEAD_DIM
    )
    fine_keys = fine_rows[:, :HEAD_DIM]
    fine_values = fine_rows[:, HEAD_DIM:]
    fine_pos = (
        mine[:, None] * SEL_BLOCK + jnp.arange(SEL_BLOCK, dtype=jnp.int32)[None, :]
    ).reshape(-1)
    reach = (WINDOW + toks - 1) // toks
    moved_keys, moved_values = from_behind((keys, values), ("blk", "grp"), 1)
    key_parts = [moved_keys]
    value_parts = [moved_values]
    wide_keys = jnp.concatenate(key_parts + [keys], axis=0)
    wide_values = jnp.concatenate(value_parts + [values], axis=0)
    wide_pos = position * toks - reach * toks + jnp.arange((reach + 1) * toks, dtype=jnp.int32)
    block_rows = min(toks, 128)
    steps = toks // block_rows

    def both_blocks(index):
        first = index * block_rows
        rows = lax.dynamic_slice_in_dim(query_heads, first, block_rows, 0)
        pos = lax.dynamic_slice_in_dim(query_pos, first, block_rows, 0)
        fine_part = attend(rows, pos, fine_keys, fine_values, fine_pos, seq_len + 1)
        key_start = reach * toks + first - WINDOW
        near_keys = lax.dynamic_slice_in_dim(wide_keys, key_start, block_rows + WINDOW, 0)
        near_values = lax.dynamic_slice_in_dim(wide_values, key_start, block_rows + WINDOW, 0)
        near_pos = lax.dynamic_slice_in_dim(wide_pos, key_start, block_rows + WINDOW, 0)
        local_part = attend(rows, pos, near_keys, near_values, near_pos, WINDOW)
        return (fine_part, local_part)

    fine, local = lax.map(both_blocks, jnp.arange(steps, dtype=jnp.int32))
    fine = fine.reshape(toks, HEADS, HEAD_DIM)
    local = local.reshape(toks, HEADS, HEAD_DIM)
    gates = jax.nn.sigmoid(
        jnp.dot(queries, gate_weight, preferred_element_type=jnp.float32)
    ).reshape(toks, 3, HEADS)
    mixed = (
        gates[:, 0, :, None] * coarse + gates[:, 1, :, None] * fine + gates[:, 2, :, None] * local
    )
    return mixed.astype(jnp.bfloat16).reshape(toks, HEADS * HEAD_DIM)


def solution(mesh):
    return jax.shard_map(
        per_device,
        mesh=mesh,
        in_specs=(
            P(("blk", "grp"), None),
            P(("blk", "grp"), None),
            P(("blk", "grp"), None),
            P(),
            P(),
            P(),
            P(),
            P(),
            P(),
            P(),
        ),
        out_specs=P(("blk", "grp"), None),
        check_vma=False,
    )
```

profile of v0, /device:TPU:1, one launch (start us, length us, event | category | flops | bytes accessed | tf_op | source)
XLA Modules:
  0.0 179.8 jit_solution(15215971414897024461)
XLA Ops:
  6.5 1.1 pad_maximum_fusion
  7.7 1.5 broadcast_in_dim.188
  9.2 7.6 %all-to-all-start = ((bf16[8,512,256]{2,1,0:T(8,128)(2,1)}), bf16[8,512,256]{2,1,0:T(8,128)(2,1)}, u32[]{:S(2)}, u32[]{:S(2)}) async-start(bf16[8,512,256]{2,1,0:T(8,128)(2,1)} %broadcast_in_dim.188), calls=%async_computation | async-start | bytes 4194304 | tf_op jit(solution)/shard_map/all_to_all | solution.py:25
  16.8 3.7 %collective-permute-start = (bf16[512,128]{1,0:T(8,128)(2,1)S(1)}, bf16[512,128]{1,0:T(8,128)(2,1)}, u32[]{:S(2)}, u32[]{:S(2)}) collective-permute-start(bf16[512,128]{1,0:T(8,128)(2,1)S(1)} %copy-done.2), channel_id=1, source_target_pairs={{0,1},{1,2},{2,3},{3,4},{4,5},{5,6},{6,7},{7,8},{8,9},{9,10},{10,1... | collective-permute-start | bytes 393224 | tf_op jit(solution)/shard_map/ppermute | solution.py:51
  20.5 2.1 %collective-permute-start.1 = (bf16[512,128]{1,0:T(8,128)(2,1)S(1)}, bf16[512,128]{1,0:T(8,128)(2,1)S(1)}, u32[]{:S(2)}, u32[]{:S(2)}) collective-permute-start(bf16[512,128]{1,0:T(8,128)(2,1)S(1)} %copy-done.3), channel_id=1, source_target_pairs={{0,1},{1,2},{2,3},{3,4},{4,5},{5,6},{6,7},{7,8},{8,9},{9,10},{10,1... | collective-permute-start | bytes 393224 | tf_op jit(solution)/shard_map/ppermute | solution.py:51
  23.3 2.1 %convolution_convert_fusion.1 = bf16[16,128]{1,0:T(8,128)(2,1)S(1)} fusion(bf16[256,128]{1,0:T(8,128)(2,1)S(1)} %copy-done.16, bf16[4096,256]{1,0:T(8,128)(2,1)} %param.18, f32[16,4096]{1,0:T(8,128)S(1)} %reshape.503, f32[4096]{0:T(1024)S(1)} %get-tuple-element.456), kind=kOutput, calls=%fused_computation.75 | convolution fusion | flops 34756608 | bytes 2445312 | tf_op jit(solution)/shard_map/dot_general | solution.py:64
  25.4 0.6 pad_maximum_fusion.3
  26.3 16.9 %all-to-all-done = bf16[8,512,256]{2,1,0:T(8,128)(2,1)} async-done(((bf16[8,512,256]{2,1,0:T(8,128)(2,1)}), bf16[8,512,256]{2,1,0:T(8,128)(2,1)}, u32[]{:S(2)}, u32[]{:S(2)}) %all-to-all-start) | async-done | bytes 2097184 | tf_op jit(solution)/shard_map/all_to_all | solution.py:25
  43.2 3.3 %gather_fusion.1 = bf16[32,64,256]{2,1,0:T(8,128)(2,1)} fusion(bf16[64,64,256]{2,1,0:T(8,128)(2,1)} %bitcast.6, s32[1024]{0:T(1024)S(1)} %pad_clamp_fusion.1), kind=kCustom, calls=%fused_computation.1 | custom fusion | bytes 2097280 | tf_op jit(solution)/shard_map/jit(_take)/gather | solution.py:174
  46.5 2.5 %broadcast_select_fusion = bf16[32,64,256]{2,1,0:T(8,128)(2,1)} fusion(bf16[32,64,256]{2,1,0:T(8,128)(2,1)} %gather_fusion.1, pred[32]{0:T(512)(128)(4,1)S(1)} %compare_and_fusion), kind=kLoop, calls=%fused_computation.83 | loop fusion | flops 524288 | bytes 2097184 | tf_op jit(solution)/shard_map/jit(_take)/select_n | solution.py:174
  49.0 9.7 %all-to-all-start.1 = ((bf16[32,64,256]{2,1,0:T(8,128)(2,1)}), bf16[32,64,256]{2,1,0:T(8,128)(2,1)}, u32[]{:S(2)}, u32[]{:S(2)}) async-start(bf16[32,64,256]{2,1,0:T(8,128)(2,1)} %broadcast_select_fusion), calls=%async_computation.1 | async-start | bytes 2097152 | tf_op jit(solution)/shard_map/all_to_all | solution.py:175
  59.3 0.6 pad_clamp_fusion
  62.7 1.0 copy.22
  63.9 0.7 broadcast_in_dim.190
  64.6 0.6 broadcast_in_dim.191
  65.2 0.7 broadcast_in_dim.182
  65.9 0.7 broadcast_in_dim.183
  66.6 0.7 broadcast_in_dim.185
  67.3 0.7 broadcast_in_dim.186
  68.0 1.5 copy.17
  69.5 1.6 copy.21
  71.1 0.9 copy.27
  71.9 0.9 pad_maximum_fusion.1
  72.9 0.7 pad_maximum_fusion.2
  73.6 2.3 %gather_fusion = bf16[16,64,256]{2,1,0:T(8,128)(2,1)S(1)} fusion(bf16[64,64,256]{2,1,0:T(8,128)(2,1)} %bitcast.6, s32[1024]{0:T(1024)} %get-tuple-element.462), kind=kCustom, calls=%fused_computation | custom fusion | bytes 1048640 | tf_op jit(solution)/shard_map/jit(_take)/gather | solution.py:178
  75.9 6.9 %all-to-all-done.1 = bf16[32,64,256]{2,1,0:T(8,128)(2,1)} async-done(((bf16[32,64,256]{2,1,0:T(8,128)(2,1)}), bf16[32,64,256]{2,1,0:T(8,128)(2,1)}, u32[]{:S(2)}, u32[]{:S(2)}) %all-to-all-start.1) | async-done | bytes 1048608 | tf_op jit(solution)/shard_map/all_to_all | solution.py:175
  82.8 2.7 %gather_fusion.2 = bf16[16,64,256]{2,1,0:T(8,128)(2,1)} fusion(bf16[32,64,256]{2,1,0:T(8,128)(2,1)} %all-to-all-done.1, s32[1024]{0:T(1024)} %get-tuple-element.461), kind=kCustom, calls=%fused_computation.2 | custom fusion | bytes 1048640 | tf_op jit(solution)/shard_map/jit(_take)/gather | solution.py:179
  85.6 1.8 fusion.57
  87.4 0.7 fusion.76
  88.1 35.4 %while.33 = (s32[]{:T(128)}, f32[4,128,4,128]{3,2,1,0:T(4,128)}, f32[4,128,4,128]{3,2,1,0:T(4,128)}, s32[4]{0:T(128)S(1)}, s32[512]{0:T(512)}, /*index=5*/bf16[5...) while((s32[]{:T(128)}, f32[4,128,4,128]{3,2,1,0:T(4,128)}, ...), condition=%wide.region_10.11_spmd.clone, body=%wide.region_5.10_spmd.clone.sunk | while | flops 445252480 | bytes 15753344 | solution.py:210
  88.1 0.6 dynamic_slice.127
  89.3 0.7 broadcast_add_fusion.4
  90.5 1.6 fusion.112
  92.6 0.7 fusion.114
  93.6 1.4 fusion.109
  95.8 1.1 copy_dynamic-update-slice_fusion.6
  98.2 0.7 broadcast_add_fusion.4
  99.3 1.6 fusion.112
  101.5 0.7 fusion.114
  102.4 1.4 fusion.109
  104.6 1.1 copy_dynamic-update-slice_fusion.6
  107.0 0.7 broadcast_add_fusion.4
  108.1 1.6 fusion.112
  110.3 0.7 fusion.114
  111.2 1.4 fusion.109
  113.5 1.1 copy_dynamic-update-slice_fusion.6
  115.9 0.7 broadcast_add_fusion.4
  117.0 1.6 fusion.112
  119.2 0.7 fusion.114
  120.1 1.4 fusion.109
  122.3 1.1 copy_dynamic-update-slice_fusion.6
  123.5 9.9 %all-gather.2.cloned.1.call-done = bf16[4096,256]{1,0:T(8,128)(2,1)} async-done(((bf16[16,256]{1,0:T(8,128)(2,1)}), bf16[4096,256]{1,0:T(8,128)(2,1)}) %all-gather.2.cloned.1.call-update) | async-done | bytes 2097168 | tf_op jit(solution)/shard_map/all_gather | solution.py:44
  133.4 3.0 %fusion.75 = (bf16[4096,128]{1,0:T(8,128)(2,1)}, bf16[4096,128]{1,0:T(8,128)(2,1)}) fusion(bf16[4096,256]{1,0:T(8,128)(2,1)} %all-gather.2.cloned.1.call-done), kind=kLoop, calls=%fused_computation.155 | loop fusion | bytes 4194304 | tf_op jit(solution)/shard_map/split | solution.py:45
  136.4 32.2 %while.32 = (s32[]{:T(128)}, f32[2,256,4]{1,2,0:T(4,128)S(1)}, f32[2,256,4,128]{3,2,1,0:T(4,128)}, s32[2,256]{1,0:T(2,128)S(1)}, bf16[2,256,4,128]{3,2,1,0:T(4,1...) while((s32[]{:T(128)}, f32[2,256,4]{1,2,0:T(4,128)S(1)}, ...), condition=%wide.region_3.4_spmd.clone, body=%wide.region_0.3_spmd.clone.sunk | while | flops 2194812928 | bytes 71646384 | solution.py:129
  136.4 0.6 broadcast_compare_fusion.7
  137.2 4.8 %fusion.101 = (f32[256,4]{0,1:T(4,128)S(1)}, f32[256,4,4096]{2,0,1:T(8,128)S(1)}) fusion(pred[256,4096]{1,0:T(8,128)(4,1)S(1)} %broadcast_compare_fusion.7, bf16[4096,128]{1,0:T(8,128)(2,1)} %get-tuple-element.679, bf16[1,256,4,128]{3,2,1,0:T(4,128)(2,1)S(1)} %constant_dynamic-slice_fusion.5), kind=kOutput, calls=%fused_computation.7.clone.1 | convolution fusion | flops 1086323712 | bytes 19140608 | tf_op jit(solution)/shard_map/while/body/eval_jaxpr/qhd,kd->qhk/dot_general | solution.py:106
  142.0 5.5 %fusion.104 = f32[1,256,4,128]{3,1,2,0:T(8,128)S(1)} fusion(f32[256,4,4096]{2,0,1:T(8,128)S(1)} %get-tuple-element.581, f32[256,4]{0,1:T(4,128)S(1)} %get-tuple-element.583, pred[256,4096]{1,0:T(8,128)(4,1)S(1)} %broadcast_compare_fusion.7, bf16[4096,128]{1,0:T(8,128)(2,1)S(1)} %copy-done.12, f32[256,4]{0,1:T(4,128)S(1)} %get-tuple-element.584), kind=kOutput, calls=%fused_computation.14.clone.1 | convolution fusion | flops 1090650112 | bytes 19406848 | tf_op jit(solution)/shard_map/while/body/eval_jaxpr/qhk,kd->qhd/dot_general | solution.py:114
  147.9 4.5 %fusion.103 = f32[256,4]{0,1:T(4,128)S(1)} fusion(f32[256,4,4096]{2,0,1:T(8,128)S(1)} %get-tuple-element.581, f32[256,4]{0,1:T(4,128)S(1)} %get-tuple-element.583, pred[256,4096]{1,0:T(8,128)(4,1)S(1)} %broadcast_compare_fusion.7), kind=kLoop, calls=%fused_computation.9.clone.1 | loop fusion | flops 16776192 | bytes 17833984 | tf_op jit(solution)/shard_map/while/body/eval_jaxpr/reduce_sum | solution.py:113
  152.4 0.6 broadcast_compare_fusion.7
  153.2 4.8 %fusion.101 = (f32[256,4]{0,1:T(4,128)S(1)}, f32[256,4,4096]{2,0,1:T(8,128)S(1)}) fusion(pred[256,4096]{1,0:T(8,128)(4,1)S(1)} %broadcast_compare_fusion.7, bf16[4096,128]{1,0:T(8,128)(2,1)} %get-tuple-element.679, bf16[1,256,4,128]{3,2,1,0:T(4,128)(2,1)S(1)} %constant_dynamic-slice_fusion.5), kind=kOutput, calls=%fused_computation.7.clone.1 | convolution fusion | flops 1086323712 | bytes 19140608 | tf_op jit(solution)/shard_map/while/body/eval_jaxpr/qhd,kd->qhk/dot_general | solution.py:106
  158.0 5.5 %fusion.104 = f32[1,256,4,128]{3,1,2,0:T(8,128)S(1)} fusion(f32[256,4,4096]{2,0,1:T(8,128)S(1)} %get-tuple-element.581, f32[256,4]{0,1:T(4,128)S(1)} %get-tuple-element.583, pred[256,4096]{1,0:T(8,128)(4,1)S(1)} %broadcast_compare_fusion.7, bf16[4096,128]{1,0:T(8,128)(2,1)S(1)} %copy-done.12, f32[256,4]{0,1:T(4,128)S(1)} %get-tuple-element.584), kind=kOutput, calls=%fused_computation.14.clone.1 | convolution fusion | flops 1090650112 | bytes 19406848 | tf_op jit(solution)/shard_map/while/body/eval_jaxpr/qhk,kd->qhd/dot_general | solution.py:114
  163.9 4.5 %fusion.103 = f32[256,4]{0,1:T(4,128)S(1)} fusion(f32[256,4,4096]{2,0,1:T(8,128)S(1)} %get-tuple-element.581, f32[256,4]{0,1:T(4,128)S(1)} %get-tuple-element.583, pred[256,4096]{1,0:T(8,128)(4,1)S(1)} %broadcast_compare_fusion.7), kind=kLoop, calls=%fused_computation.9.clone.1 | loop fusion | flops 16776192 | bytes 17833984 | tf_op jit(solution)/shard_map/while/body/eval_jaxpr/reduce_sum | solution.py:113
  168.8 0.6 div.103
  171.3 1.6 fusion.54
  (162 shorter events, 17.2 us)
Async XLA Ops:
  6.5 16.2 %copy-start = (bf16[4096,256]{1,0:T(8,128)(2,1)S(1)}, bf16[4096,256]{1,0:T(8,128)(2,1)}, u32[]{:S(2)}) copy-start(bf16[4096,256]{1,0:T(8,128)(2,1)} %param.20) | copy-start | bytes 6291460
  9.2 7.6 %copy-start.2 = (bf16[512,128]{1,0:T(8,128)(2,1)S(1)}, bf16[512,128]{1,0:T(8,128)(2,1)}, u32[]{:S(2)}) copy-start(bf16[512,128]{1,0:T(8,128)(2,1)} %param.15) | copy-start | bytes 393220
  9.2 11.3 %copy-start.3 = (bf16[512,128]{1,0:T(8,128)(2,1)S(1)}, bf16[512,128]{1,0:T(8,128)(2,1)}, u32[]{:S(2)}) copy-start(bf16[512,128]{1,0:T(8,128)(2,1)} %param.16) | copy-start | bytes 393220
  9.2 13.5 %copy-start.19 = (bf16[2,32,128]{2,1,0:T(8,128)(2,1)S(1)}, bf16[2,32,128]{2,1,0:T(8,128)(2,1)}, u32[]{:S(2)}) copy-start(bf16[2,32,128]{2,1,0:T(8,128)(2,1)} %param.22) | copy-start | bytes 49156
  9.2 13.5 %copy-start.15 = (bf16[256,128]{1,0:T(8,128)(2,1)S(1)}, bf16[256,128]{1,0:T(8,128)(2,1)}, u32[]{:S(2)}) copy-start(bf16[256,128]{1,0:T(8,128)(2,1)} %param.21) | copy-start | bytes 196612
  9.2 34.1 %all-to-all-start = ((bf16[8,512,256]{2,1,0:T(8,128)(2,1)}), bf16[8,512,256]{2,1,0:T(8,128)(2,1)}, u32[]{:S(2)}, u32[]{:S(2)}) async-start(bf16[8,512,256]{2,1,0:T(8,128)(2,1)} %broadcast_in_dim.188), calls=%async_computation | async-start | bytes 4194304 | tf_op jit(solution)/shard_map/all_to_all | solution.py:25
  16.8 6.5 %copy-start.16 = (bf16[256,128]{1,0:T(8,128)(2,1)S(1)}, bf16[256,128]{1,0:T(8,128)(2,1)}, u32[]{:S(2)}) copy-start(bf16[256,128]{1,0:T(8,128)(2,1)} %param.19) | copy-start | bytes 196612
  16.8 116.6 %all-gather.2.cloned.1.call-start = ((), (), s32[]{:S(2)}) async-start(), calls=%async_computation.2 | async-start | bytes 2105344 | tf_op jit(solution)/shard_map/all_gather | solution.py:44
  16.8 55.1 %collective-permute-start = (bf16[512,128]{1,0:T(8,128)(2,1)S(1)}, bf16[512,128]{1,0:T(8,128)(2,1)}, u32[]{:S(2)}, u32[]{:S(2)}) collective-permute-start(bf16[512,128]{1,0:T(8,128)(2,1)S(1)} %copy-done.2), channel_id=1, source_target_pairs={{0,1},{1,2},{2,3},{3,4},{4,5},{5,6},{6,7},{7,8},{8,9},{9,10},{10,1... | collective-permute-start | bytes 393224 | tf_op jit(solution)/shard_map/ppermute | solution.py:51
  20.5 52.4 %collective-permute-start.1 = (bf16[512,128]{1,0:T(8,128)(2,1)S(1)}, bf16[512,128]{1,0:T(8,128)(2,1)S(1)}, u32[]{:S(2)}, u32[]{:S(2)}) collective-permute-start(bf16[512,128]{1,0:T(8,128)(2,1)S(1)} %copy-done.3), channel_id=1, source_target_pairs={{0,1},{1,2},{2,3},{3,4},{4,5},{5,6},{6,7},{7,8},{8,9},{9,10},{10,1... | collective-permute-start | bytes 393224 | tf_op jit(solution)/shard_map/ppermute | solution.py:51
  22.7 3.3 %copy-start.17 = (s32[256,16]{0,1:T(8,128)S(1)}, s32[256,16]{0,1:T(8,128)}, u32[]{:S(2)}) copy-start(s32[256,16]{0,1:T(8,128)} %param.17) | copy-start | bytes 49156
  46.5 12.2 %copy-start.1 = (bf16[512,512]{1,0:T(8,128)(2,1)S(1)}, bf16[512,512]{1,0:T(8,128)(2,1)}, u32[]{:S(2)}) copy-start(bf16[512,512]{1,0:T(8,128)(2,1)} %param.14) | copy-start | bytes 1572868
  46.5 12.2 %copy-start.20 = (bf16[512,12]{0,1:T(8,128)(2,1)S(1)}, bf16[512,12]{0,1:T(8,128)(2,1)}, u32[]{:S(2)}) copy-start(bf16[512,12]{0,1:T(8,128)(2,1)} %param.23) | copy-start | bytes 36868
  46.5 12.5 %copy-start.18 = (s32[256,16]{0,1:T(8,128)S(1)}, s32[256,16]{0,1:T(8,128)}, u32[]{:S(2)}) copy-start(s32[256,16]{0,1:T(8,128)} %param.17) | copy-start | bytes 49156
  49.0 33.8 %all-to-all-start.1 = ((bf16[32,64,256]{2,1,0:T(8,128)(2,1)}), bf16[32,64,256]{2,1,0:T(8,128)(2,1)}, u32[]{:S(2)}, u32[]{:S(2)}) async-start(bf16[32,64,256]{2,1,0:T(8,128)(2,1)} %broadcast_select_fusion), calls=%async_computation.1 | async-start | bytes 2097152 | tf_op jit(solution)/shard_map/all_to_all | solution.py:175
  71.9 13.6 %copy-start.23 = (pred[1024]{0:T(1024)(128)(4,1)S(1)}, pred[1024]{0:T(1024)(128)(4,1)}, u32[]{:S(2)}) copy-start(pred[1024]{0:T(1024)(128)(4,1)} %broadcast_in_dim.191) | copy-start | bytes 3076
  71.9 13.6 %copy-start.24 = (pred[1024]{0:T(1024)(128)(4,1)S(1)}, pred[1024]{0:T(1024)(128)(4,1)}, u32[]{:S(2)}) copy-start(pred[1024]{0:T(1024)(128)(4,1)} %broadcast_in_dim.183) | copy-start | bytes 3076
  73.6 12.0 %copy-start.25 = (pred[1024]{0:T(1024)(128)(4,1)S(1)}, pred[1024]{0:T(1024)(128)(4,1)}, u32[]{:S(2)}) copy-start(pred[1024]{0:T(1024)(128)(4,1)} %broadcast_in_dim.186) | copy-start | bytes 3076
  75.9 12.2 %copy-start.21 = (s32[16]{0:T(128)S(1)}, s32[16]{0:T(128)}, u32[]{:S(2)}) copy-start(s32[16]{0:T(128)} %broadcast_multiply_fusion) | copy-start | bytes 196
  90.5 2.2 %copy-start.14 = (bf16[1024,128]{1,0:T(8,128)(2,1)S(1)}, bf16[1024,128]{1,0:T(8,128)(2,1)}, u32[]{:S(2)}) copy-start(bf16[1024,128]{1,0:T(8,128)(2,1)} %get-tuple-element.648) | copy-start | bytes 786436 | tf_op jit(solution)/shard_map/while
  93.3 2.0 %copy-start.13 = (bf16[1024,128]{1,0:T(8,128)(2,1)S(1)}, bf16[1024,128]{1,0:T(8,128)(2,1)}, u32[]{:S(2)}) copy-start(bf16[1024,128]{1,0:T(8,128)(2,1)} %get-tuple-element.651) | copy-start | bytes 786436 | tf_op jit(solution)/shard_map/while
  99.3 2.2 %copy-start.14 = (bf16[1024,128]{1,0:T(8,128)(2,1)S(1)}, bf16[1024,128]{1,0:T(8,128)(2,1)}, u32[]{:S(2)}) copy-start(bf16[1024,128]{1,0:T(8,128)(2,1)} %get-tuple-element.648) | copy-start | bytes 786436 | tf_op jit(solution)/shard_map/while
  102.2 2.0 %copy-start.13 = (bf16[1024,128]{1,0:T(8,128)(2,1)S(1)}, bf16[1024,128]{1,0:T(8,128)(2,1)}, u32[]{:S(2)}) copy-start(bf16[1024,128]{1,0:T(8,128)(2,1)} %get-tuple-element.651) | copy-start | bytes 786436 | tf_op jit(solution)/shard_map/while
  108.1 2.2 %copy-start.14 = (bf16[1024,128]{1,0:T(8,128)(2,1)S(1)}, bf16[1024,128]{1,0:T(8,128)(2,1)}, u32[]{:S(2)}) copy-start(bf16[1024,128]{1,0:T(8,128)(2,1)} %get-tuple-element.648) | copy-start | bytes 786436 | tf_op jit(solution)/shard_map/while
  111.0 2.1 %copy-start.13 = (bf16[1024,128]{1,0:T(8,128)(2,1)S(1)}, bf16[1024,128]{1,0:T(8,128)(2,1)}, u32[]{:S(2)}) copy-start(bf16[1024,128]{1,0:T(8,128)(2,1)} %get-tuple-element.651) | copy-start | bytes 786436 | tf_op jit(solution)/shard_map/while
  117.0 2.2 %copy-start.14 = (bf16[1024,128]{1,0:T(8,128)(2,1)S(1)}, bf16[1024,128]{1,0:T(8,128)(2,1)}, u32[]{:S(2)}) copy-start(bf16[1024,128]{1,0:T(8,128)(2,1)} %get-tuple-element.648) | copy-start | bytes 786436 | tf_op jit(solution)/shard_map/while
  119.8 2.0 %copy-start.13 = (bf16[1024,128]{1,0:T(8,128)(2,1)S(1)}, bf16[1024,128]{1,0:T(8,128)(2,1)}, u32[]{:S(2)}) copy-start(bf16[1024,128]{1,0:T(8,128)(2,1)} %get-tuple-element.651) | copy-start | bytes 786436 | tf_op jit(solution)/shard_map/while
  123.5 12.9 %copy-start.22 = (f32[2,256,4]{1,2,0:T(4,128)S(1)}, f32[2,256,4]{1,2,0:T(4,128)}, u32[]{:S(2)}) copy-start(f32[2,256,4]{1,2,0:T(4,128)} %custom-call.6) | copy-start | bytes 24580
  136.4 33.0 %copy-start.9 = (f32[512,4]{1,0:T(8,128)S(1)}, f32[512,4]{1,0:T(8,128)}, u32[]{:S(2)}) copy-start(f32[512,4]{1,0:T(8,128)} %copy.17) | copy-start | bytes 24580
  137.2 4.8 %copy-start.12 = (bf16[4096,128]{1,0:T(8,128)(2,1)S(1)}, bf16[4096,128]{1,0:T(8,128)(2,1)}, u32[]{:S(2)}) copy-start(bf16[4096,128]{1,0:T(8,128)(2,1)} %get-tuple-element.680) | copy-start | bytes 3145732 | tf_op jit(solution)/shard_map/while
  142.0 5.5 %copy-start.4 = (f32[2,256,4,128]{3,2,1,0:T(4,128)S(1)}, f32[2,256,4,128]{3,2,1,0:T(4,128)}, u32[]{:S(2)}) copy-start(f32[2,256,4,128]{3,2,1,0:T(4,128)} %get-tuple-element.668) | copy-start | bytes 3145732 | tf_op jit(solution)/shard_map/while
  147.9 4.5 %copy-start.5 = (f32[2,256,4,128]{3,2,1,0:T(4,128)}, f32[2,256,4,128]{3,2,1,0:T(4,128)S(1)}, u32[]{:S(2)}) copy-start(f32[2,256,4,128]{3,2,1,0:T(4,128)S(1)} %copy_dynamic-update-slice_fusion.5) | copy-start | bytes 3145732 | tf_op jit(solution)/shard_map/while
  153.2 4.8 %copy-start.12 = (bf16[4096,128]{1,0:T(8,128)(2,1)S(1)}, bf16[4096,128]{1,0:T(8,128)(2,1)}, u32[]{:S(2)}) copy-start(bf16[4096,128]{1,0:T(8,128)(2,1)} %get-tuple-element.680) | copy-start | bytes 3145732 | tf_op jit(solution)/shard_map/while
  158.0 5.5 %copy-start.4 = (f32[2,256,4,128]{3,2,1,0:T(4,128)S(1)}, f32[2,256,4,128]{3,2,1,0:T(4,128)}, u32[]{:S(2)}) copy-start(f32[2,256,4,128]{3,2,1,0:T(4,128)} %get-tuple-element.668) | copy-start | bytes 3145732 | tf_op jit(solution)/shard_map/while
  163.9 4.5 %copy-start.5 = (f32[2,256,4,128]{3,2,1,0:T(4,128)}, f32[2,256,4,128]{3,2,1,0:T(4,128)S(1)}, u32[]{:S(2)}) copy-start(f32[2,256,4,128]{3,2,1,0:T(4,128)S(1)} %copy_dynamic-update-slice_fusion.5) | copy-start | bytes 3145732 | tf_op jit(solution)/shard_map/while
  168.6 1.4 copy-start.10
  168.6 2.0 %copy-start.11 = (f32[512,4]{1,0:T(8,128)S(1)}, f32[512,4]{1,0:T(8,128)}, u32[]{:S(2)}) copy-start(f32[512,4]{1,0:T(8,128)} %copy.27) | copy-start | bytes 24580
  169.4 1.9 %copy-start.6 = (f32[2,256,4,128]{3,2,1,0:T(4,128)S(1)}, f32[2,256,4,128]{3,2,1,0:T(4,128)}, u32[]{:S(2)}) copy-start(f32[2,256,4,128]{3,2,1,0:T(4,128)} %get-tuple-element.318) | copy-start | bytes 3145732
  169.4 1.9 %copy-start.7 = (f32[4,128,4,128]{3,2,1,0:T(4,128)S(1)}, f32[4,128,4,128]{3,2,1,0:T(4,128)}, u32[]{:S(2)}) copy-start(f32[4,128,4,128]{3,2,1,0:T(4,128)} %get-tuple-element.320) | copy-start | bytes 3145732
  169.4 1.9 %copy-start.8 = (f32[4,128,4,128]{3,2,1,0:T(4,128)S(1)}, f32[4,128,4,128]{3,2,1,0:T(4,128)}, u32[]{:S(2)}) copy-start(f32[4,128,4,128]{3,2,1,0:T(4,128)} %get-tuple-element.321) | copy-start | bytes 3145732
Sparse Core Ops, SparseCore 0:
  26.1 107.2 all-gather.1
where the time goes:
time: 181 us; the launch traced here: 180 us
  matrix products  39.6 us (22%)
  local copies, waits for them, and re-layouts  34.7 us (19%)
  waiting for transfers between devices  33.8 us (19%)
  other arithmetic  31.6 us (17%)
  starting transfers between devices  23 us (13%)
  between operations  13.8 us (8%)
  loops' own time  3.27 us (2%)
    all_to_all x1, waiting for transfers between devices, copy_for_each(): return lax.all_to_all(copies, axis, split_axis=0, concat_axis=0, tiled=True)  16.9 us
    dot_general x8, matrix products, attend(): jnp.einsum('qhd,kd->qhk', query_rows, key_rows, preferred_element_type=jn...  11.9 us
    dot_general x2, matrix products, one(): jnp.einsum('qhk,kd->qhd', weights.astype(jnp.bfloat16), piece_values, pre...  10.9 us
    all_gather x1, waiting for transfers between devices, in_one_piece(): whole = lax.all_gather(both, axis, axis=dim, tiled=True)  9.94 us
    all_to_all x1, starting transfers between devices, per_device(): lax.all_to_all(outgoing, 'blk', split_axis=0, concat_axis=0, tiled=True)  9.71 us
    dot_general x2, matrix products, one(): jnp.einsum('qhd,kd->qhk', rows, piece_keys, preferred_element_type=jnp.fl...  9.52 us
    reduce_sum x2, other arithmetic, one(): new_total = old_total * factor + jnp.sum(weights, axis=2)  8.99 us
    all_to_all x1, starting transfers between devices, copy_for_each(): return lax.all_to_all(copies, axis, split_axis=0, concat_axis=0, tiled=True)  7.6 us
  transfers between devices with their start and end apart: 5, of which 3 were waited for; matrix products, arithmetic and copies ran while one was open for 36% of the time, Pallas kernels for 0%

commit v1 on v0

v1 whole, which is shorter than its diff:
```python
import math

import jax
import jax.numpy as jnp
from jax import lax
from jax.experimental import pallas as pl
from jax.experimental.pallas import tpu as pltpu
from jax.sharding import PartitionSpec as P

HEAD_DIM = 128
HEADS = 4
CMP_BLOCK = 32
SEL_BLOCK = 64
TOPN = 16
WINDOW = 512
NEG = -1e30
SCALE2 = HEAD_DIM**-0.5 * math.log2(math.e)
AXES = ("blk", "grp")
ANY = pl.BlockSpec(memory_space=pl.ANY)
SMEM = pl.BlockSpec(memory_space=pltpu.SMEM)
VMEM = pl.BlockSpec(memory_space=pltpu.VMEM)


def compress(tokens, shift, w_in, w_out):
    count = tokens.shape[0] // CMP_BLOCK
    mixed = (
        tokens.astype(jnp.float32).reshape(count, CMP_BLOCK, HEAD_DIM)
        + shift.astype(jnp.float32)[None]
    )
    flat = mixed.astype(jnp.bfloat16).reshape(count, CMP_BLOCK * HEAD_DIM)
    hidden = jax.nn.silu(jnp.dot(flat, w_in, preferred_element_type=jnp.float32)).astype(
        jnp.bfloat16
    )
    return jnp.dot(hidden, w_out, preferred_element_type=jnp.float32).astype(jnp.bfloat16)


def route(stretches, rows, cores, move):
    pairs = []
    for b in range(stretches):
        for y in range(rows):
            for c in range(cores):
                to_y, to_c = move(y, c)
                pairs.append(((b * rows + y) * cores + c, (b * rows + to_y % rows) * cores + to_c))
    return pairs


def dot_t(a, b):
    return lax.dot_general(a, b, (((1,), (1,)), ((), ())), preferred_element_type=jnp.float32)


def lane_groups(x, op):
    parts = [x[:, i : i + 128] for i in range(0, x.shape[1], 128)]
    while len(parts) > 1:
        parts = [
            op(parts[i], parts[i + 1]) if i + 1 < len(parts) else parts[i]
            for i in range(0, len(parts), 2)
        ]
    return parts[0]


def gates_of(q, gw):
    return jax.nn.sigmoid(jnp.dot(q, gw, preferred_element_type=jnp.float32))


def copy_all(pairs, sem):
    copies = [pltpu.make_async_copy(s, d, sem.at[i]) for i, (s, d) in enumerate(pairs)]
    for c in copies:
        c.start()
    for c in copies:
        c.wait()


def pick_kernel(picked, near, *refs):
    own, from1, from3, far_a, far_b, s_own, s_from1, s_from3, s_far_a, s_far_b = refs[:10]
    out, nearby, rows, sem = refs[10:]
    half = far_a.shape[0]
    pairs = []
    for dc, (o, a, b, fa, fb) in enumerate(
        ((own, from1, from3, far_a, far_b), (s_own, s_from1, s_from3, s_far_a, s_far_b))
    ):
        for dy, ref in ((0, o), (1, a), (3, b)):
            slot = dy * 2 + dc
            pairs.append((ref, rows.at[pl.ds(slot * 8, 8)]))
        slot = 4 + dc
        pairs.append((fa, rows.at[pl.ds(slot * 8, half)]))
        pairs.append((fb, rows.at[pl.ds(slot * 8 + half, half)]))
    copy_all(pairs, sem)
    for i in range(out.shape[0]):
        out[i] = rows[picked[i]]
    for i in range(nearby.shape[0]):
        nearby[i] = rows[near[i]]


def window_kernel(low, q_ref, prev_ref, kv_ref, gw_ref, out_ref):
    toks = q_ref.shape[0]
    q = q_ref[...]
    gates = gates_of(q, gw_ref[...])
    rows = 128
    for first in range(0, toks, rows):
        k = jnp.concatenate([prev_ref[first:, :HEAD_DIM], kv_ref[: first + rows, :HEAD_DIM]], 0)
        v = jnp.concatenate([prev_ref[first:, HEAD_DIM:], kv_ref[: first + rows, HEAD_DIM:]], 0)
        shape = (rows, WINDOW + rows)
        r = lax.broadcasted_iota(jnp.int32, shape, 0)
        c = lax.broadcasted_iota(jnp.int32, shape, 1)
        seen = (c > r) & (c <= r + WINDOW) & (c + first >= low[0])
        for h in range(HEADS):
            qh = q_ref[first : first + rows, h * HEAD_DIM : (h + 1) * HEAD_DIM]
            s = jnp.where(seen, dot_t(qh, k), NEG)
            top = jnp.max(lane_groups(s, jnp.maximum), axis=1, keepdims=True)
            p = jnp.exp2((s - top) * SCALE2)
            total = jnp.sum(lane_groups(p, jnp.add), axis=1, keepdims=True)
            o = jnp.dot(p.astype(jnp.bfloat16), v, preferred_element_type=jnp.float32)
            g = gates[first : first + rows, 2 * HEADS + h : 2 * HEADS + h + 1]
            out_ref[first : first + rows, h * HEAD_DIM : (h + 1) * HEAD_DIM] = o * (g / total)


def coarse_kernel(last, q_ref, gw_ref, part_ref, ends_ref, *refs):
    own, from1, from3, far_a, far_b, s_own, s_from1, s_from3, s_far_a, s_far_b = refs[:10]
    out_ref, kv, s_buf, mx, ls, acc, sem = refs[10:]
    toks = q_ref.shape[0]
    half = far_a.shape[0]
    pairs = []
    for dc, (o, a, b, fa, fb) in enumerate(
        ((own, from1, from3, far_a, far_b), (s_own, s_from1, s_from3, s_far_a, s_far_b))
    ):
        for dy, ref in ((0, o), (1, a), (3, b)):
            pairs.append((ref, kv.at[:, dy * 2 + dc]))
        pairs.append((fa, kv.at[pl.ds(0, half), 4 + dc]))
        pairs.append((fb, kv.at[pl.ds(half, half), 4 + dc]))
    copy_all(pairs, sem)
    zi = last[0]
    base = last[1]
    gates = gates_of(q_ref[...], gw_ref[...])
    chunk = kv.shape[1] * kv.shape[2]
    seen = ends_ref[pl.ds(zi, 1), :] <= base + lax.broadcasted_iota(jnp.int32, (toks, chunk), 0)

    def rows_of(z):
        return kv[z].reshape(chunk, 2 * HEAD_DIM)

    for h in range(HEADS):
        cols = slice(h * HEAD_DIM, (h + 1) * HEAD_DIM)
        qh = q_ref[:, cols]
        mx[...] = jnp.zeros_like(mx)
        ls[...] = jnp.zeros_like(ls)
        acc[...] = jnp.zeros_like(acc)

        def first(z, _):
            s = dot_t(qh, rows_of(z)[:, :HEAD_DIM])
            s_buf[z] = s
            mx[...] = jnp.maximum(mx[...], lane_groups(s, jnp.maximum))
            return 0

        lax.fori_loop(0, zi, first, 0)
        s = jnp.where(seen, dot_t(qh, rows_of(zi)[:, :HEAD_DIM]), NEG)
        s_buf[zi] = s
        top = jnp.max(jnp.maximum(mx[...], lane_groups(s, jnp.maximum)), axis=1, keepdims=True)

        def second(z, _):
            p = jnp.exp2((s_buf[z] - top) * SCALE2)
            ls[...] += lane_groups(p, jnp.add)
            acc[...] += jnp.dot(
                p.astype(jnp.bfloat16), rows_of(z)[:, HEAD_DIM:], preferred_element_type=jnp.float32
            )
            return 0

        lax.fori_loop(0, zi + 1, second, 0)
        total = jnp.exp2(-top * SCALE2) + jnp.sum(ls[...], axis=1, keepdims=True)
        out_ref[:, cols] = part_ref[:, cols] + acc[...] * (gates[:, h : h + 1] / total)


def fine_kernel(owners, near, base, q_ref, gw_ref, part_ref, pos_ref, in_ref, near_ref, out_ref, kv):
    toks = q_ref.shape[0]
    for i in range(TOPN):
        block = jnp.where(near[i] == 1, near_ref[i], in_ref[owners[i]])
        kv[pl.ds(i * SEL_BLOCK, SEL_BLOCK), :] = block
    gates = gates_of(q_ref[...], gw_ref[...])
    rows = 256
    for first in range(0, toks, rows):
        p0 = base[0] + first
        seen = pos_ref[...] <= p0 + lax.broadcasted_iota(jnp.int32, (rows, kv.shape[0]), 0)
        for h in range(HEADS):
            cols = slice(h * HEAD_DIM, (h + 1) * HEAD_DIM)
            s = jnp.where(seen, dot_t(q_ref[first : first + rows, cols], kv[:, :HEAD_DIM]), NEG)
            top = jnp.max(lane_groups(s, jnp.maximum), axis=1, keepdims=True)
            p = jnp.exp2((s - top) * SCALE2)
            total = jnp.sum(lane_groups(p, jnp.add), axis=1, keepdims=True)
            o = jnp.dot(p.astype(jnp.bfloat16), kv[:, HEAD_DIM:], preferred_element_type=jnp.float32)
            g = gates[first : first + rows, HEADS + h : HEADS + h + 1]
            out = part_ref[first : first + rows, cols] + o * (g / total)
            out_ref[first : first + rows, cols] = out.astype(out_ref.dtype)


def params(mib):
    return pltpu.CompilerParams(vmem_limit_bytes=mib << 20)


def solution(mesh):
    stretches = mesh.shape["blk"]
    group_size = mesh.shape["grp"]
    cores = 2
    ys = group_size // cores
    depth = 8
    up = route(stretches, ys, cores, lambda y, c: (y + 1, c))
    down = route(stretches, ys, cores, lambda y, c: (y - 1, c))
    swap = route(stretches, ys, cores, lambda y, c: (y, 1 - c))
    behind = [(i - 1, i) for i in range(1, stretches * group_size)]

    def spread(piece):
        half = piece.shape[0] // 2
        from1 = lax.ppermute(piece, AXES, up)
        from3 = lax.ppermute(piece, AXES, down)
        far_a = lax.ppermute(from1[:half], AXES, up)
        far_b = lax.ppermute(from3[half:], AXES, down)
        mine = (piece, from1, from3, far_a, far_b)
        return mine + tuple(lax.ppermute(p, AXES, swap) for p in mine)

    def per_device(
        queries, keys, values, selected, key_in, key_out, value_in, value_out, positions, gate_weight
    ):
        stretch = lax.axis_index("blk")
        column = lax.axis_index("grp")
        my_y = column // cores
        my_c = column % cores
        toks = queries.shape[0]
        position = stretch * group_size + column
        per_dev = toks // SEL_BLOCK
        per_row = group_size * per_dev

        kv = jnp.concatenate([keys, values], axis=1)
        pieces = spread(kv.reshape(per_dev, SEL_BLOCK, 2 * HEAD_DIM))
        prev = lax.ppermute(kv, AXES, behind)

        packed = jnp.concatenate(
            [
                compress(keys, positions[0], key_in, key_out),
                compress(values, positions[1], value_in, value_out),
            ],
            axis=1,
        )
        ncomp = toks // CMP_BLOCK
        copies = jnp.broadcast_to(packed[None], (stretches, *packed.shape))
        column_comp = lax.all_to_all(copies, "blk", split_axis=0, concat_axis=0, tiled=True)
        per_z = stretches // depth * ncomp
        comp_pieces = spread(column_comp.reshape(depth, per_z, 2 * HEAD_DIM))

        def slot_of(block):
            owner = block // per_dev
            dy = (my_y - owner // cores) % ys
            return (dy * cores + (owner % cores) ^ my_c) * per_dev + block % per_dev

        requests = lax.dynamic_index_in_dim(
            selected.reshape(stretches, group_size, TOPN), column, 1, keepdims=False
        )
        targets = jnp.arange(stretches, dtype=jnp.int32)
        match = (requests // per_row == stretch) & (targets[:, None] != stretch)
        picked = jnp.sum(jnp.where(match, requests % per_row, 0), axis=1)
        mine = lax.dynamic_index_in_dim(selected, position, 0, keepdims=False)
        owners = mine // per_row

        outgoing, nearby = pl.pallas_call(
            pick_kernel,
            in_specs=[SMEM, SMEM] + [ANY] * 10,
            out_specs=[VMEM, VMEM],
            out_shape=[
                jax.ShapeDtypeStruct((stretches, SEL_BLOCK, 2 * HEAD_DIM), jnp.bfloat16),
                jax.ShapeDtypeStruct((TOPN, SEL_BLOCK, 2 * HEAD_DIM), jnp.bfloat16),
            ],
            scratch_shapes=[
                pltpu.VMEM((per_row, SEL_BLOCK, 2 * HEAD_DIM), jnp.bfloat16),
                pltpu.SemaphoreType.DMA((10,)),
            ],
            compiler_params=params(16),
            name="pick",
        )(slot_of(picked), slot_of(mine % per_row), *pieces)
        incoming = lax.all_to_all(outgoing, "blk", split_axis=0, concat_axis=0, tiled=True)

        f32_rows = jax.ShapeDtypeStruct(queries.shape, jnp.float32)
        low = jnp.where(position == 0, toks, 0).astype(jnp.int32).reshape(1)
        local = pl.pallas_call(
            window_kernel,
            in_specs=[SMEM] + [VMEM] * 4,
            out_specs=VMEM,
            out_shape=f32_rows,
            compiler_params=params(24),
            name="window",
        )(low, queries, prev, kv, gate_weight)

        slots = jnp.arange(ys * cores, dtype=jnp.int32)
        column_of = ((my_y - slots // cores) % ys) * cores + ((slots % cores) ^ my_c)
        blks = jnp.arange(stretches, dtype=jnp.int32).reshape(depth, 1, stretches // depth, 1)
        ends = (
            (blks * group_size + column_of[None, :, None, None]) * ncomp
            + jnp.arange(ncomp, dtype=jnp.int32)[None, None, None, :]
        ) * CMP_BLOCK + (CMP_BLOCK - 1)
        ends = ends.reshape(depth, -1)
        base = (position * toks).astype(jnp.int32)
        last = jnp.stack([stretch // (stretches // depth), base]).astype(jnp.int32)
        chunk = ends.shape[1]
        part = pl.pallas_call(
            coarse_kernel,
            in_specs=[SMEM] + [VMEM] * 4 + [ANY] * 10,
            out_specs=VMEM,
            out_shape=f32_rows,
            scratch_shapes=[
                pltpu.VMEM((depth, ys * cores, per_z, 2 * HEAD_DIM), jnp.bfloat16),
                pltpu.VMEM((depth, toks, chunk), jnp.float32),
                pltpu.VMEM((toks, 128), jnp.float32),
                pltpu.VMEM((toks, 128), jnp.float32),
                pltpu.VMEM((toks, 128), jnp.float32),
                pltpu.SemaphoreType.DMA((10,)),
            ],
            compiler_params=params(40),
            name="coarse",
        )(last, queries, gate_weight, local, ends, *comp_pieces)

        fine_pos = (
            mine[:, None] * SEL_BLOCK + jnp.arange(SEL_BLOCK, dtype=jnp.int32)[None, :]
        ).reshape(1, -1)
        return pl.pallas_call(
            fine_kernel,
            in_specs=[SMEM] * 3 + [VMEM] * 6,
            out_specs=VMEM,
            out_shape=jax.ShapeDtypeStruct(queries.shape, jnp.bfloat16),
            scratch_shapes=[pltpu.VMEM((TOPN * SEL_BLOCK, 2 * HEAD_DIM), jnp.bfloat16)],
            compiler_params=params(40),
            name="fine",
        )(
            owners,
            (owners == stretch).astype(jnp.int32),
            base.reshape(1),
            queries,
            gate_weight,
            part,
            fine_pos,
            incoming,
            nearby,
        )

    rows = P(AXES, None)
    return jax.shard_map(
        per_device,
        mesh=mesh,
        in_specs=(rows, rows, rows) + (P(),) * 7,
        out_specs=rows,
        check_vma=False,
    )
```

time: 181 us -> 127 us (0.70)
  the two profiles are of different devices: /device:TPU:1 before, /device:TPU:225 now
where the time goes in v1:
time: 127 us
  starting transfers between devices  51.1 us (40%)
  Pallas kernels  38.7 us (30%)
  local copies, waits for them, and re-layouts  20.3 us (16%)
  waiting for transfers between devices  8.53 us (7%)
  other arithmetic  4.1 us (3%)
  matrix products  3.57 us (3%)
    pallas_call x1, Pallas kernels, per_device(): pl.pallas_call(coarse_kernel, in_specs=[SMEM] + [VMEM] * 4 + [ANY] * 10,...  23.9 us
    ppermute x10, starting transfers between devices, spread(): return mine + tuple((lax.ppermute(p, AXES, swap) for p in mine))  17.9 us
    unnamed x27, local copies, waits for them, and re-layouts  9.74 us
    all_to_all x1, starting transfers between devices, per_device(): lax.all_to_all(outgoing, 'blk', split_axis=0, concat_axis=0, tiled=True)  9.4 us
    all_to_all x1, starting transfers between devices, per_device(): lax.all_to_all(copies, 'blk', split_axis=0, concat_axis=0, tiled=True)  7.97 us
    pallas_call x1, Pallas kernels, per_device(): pl.pallas_call(fine_kernel, in_specs=[SMEM] * 3 + [VMEM] * 6, out_specs=V...  6.63 us
    ppermute x2, waiting for transfers between devices, spread(): from1 = lax.ppermute(piece, AXES, up)  6.4 us
    pallas_call x1, Pallas kernels, per_device(): pl.pallas_call(window_kernel, in_specs=[SMEM] + [VMEM] * 4, out_specs=VME...  6.3 us
  transfers between devices with their start and end apart: 21, of which 4 were waited for; matrix products, arithmetic and copies ran while one was open for 15% of the time, Pallas kernels for 25%

profile of v1, /device:TPU:225, one launch (start us, length us, event | category | flops | bytes accessed | tf_op | source)
XLA Modules:
  0.0 126.5 jit_solution(1216902213327366488)
XLA Ops:
  0.0 1.1 constant_dynamic-update-slice_fusion.1
  1.1 0.9 constant_dynamic-update-slice_fusion.kv_ref
  2.0 1.4 %collective-permute-start.10 = (bf16[8,64,256]{2,1,0:T(8,128)(2,1)S(1)}, bf16[8,64,256]{2,1,0:T(8,128)(2,1)S(1)}, u32[]{:S(2)}, u32[]{:S(2)}) collective-permute-start(bf16[8,64,256]{2,1,0:T(8,128)(2,1)S(1)} %bitcast.34), channel_id=1, source_target_pairs={{0,2},{1,3},{2,4},{3,5},{4,6},{5,7},{6,0},{7,1},{8,10},{9,11},{10,... | collective-permute-start | bytes 786440 | tf_op jit(solution)/shard_map/ppermute | solution.py:210
  3.4 1.5 %collective-permute-start.11 = (bf16[8,64,256]{2,1,0:T(8,128)(2,1)S(1)}, bf16[8,64,256]{2,1,0:T(8,128)(2,1)S(1)}, u32[]{:S(2)}, u32[]{:S(2)}) collective-permute-start(bf16[8,64,256]{2,1,0:T(8,128)(2,1)S(1)} %bitcast.35), channel_id=1, source_target_pairs={{0,6},{1,7},{2,0},{3,1},{4,2},{5,3},{6,4},{7,5},{8,14},{9,15},{10,... | collective-permute-start | bytes 786440 | tf_op jit(solution)/shard_map/ppermute | solution.py:211
  4.9 1.1 collective-permute-start.14
  6.0 1.7 %reshape.158 = f32[16,4096]{1,0:T(8,128)} reshape(bf16[512,128]{1,0:T(8,128)(2,1)} %param.12) | data formatting | bytes 393216 | tf_op jit(solution)/shard_map/reshape | solution.py:27
  7.7 1.0 reshape.155
  8.6 0.7 bitcast_convert_fusion.1
  9.4 1.5 %convolution_convert_fusion = bf16[16,128]{1,0:T(8,128)(2,1)S(1)} fusion(bf16[256,128]{1,0:T(8,128)(2,1)} %param.17, bf16[4096,256]{1,0:T(8,128)(2,1)S(1)} %copy-done, f32[16,4096]{1,0:T(8,128)} %reshape.158, f32[4096]{0:T(1024)S(1)} %get-tuple-element.12), kind=kOutput, calls=%fused_computation | convolution fusion | flops 34756608 | bytes 2445312 | tf_op jit(solution)/shard_map/dot_general | solution.py:34
  10.8 2.1 %convolution_convert_fusion.1 = bf16[16,128]{1,0:T(8,128)(2,1)S(1)} fusion(bf16[256,128]{1,0:T(8,128)(2,1)S(1)} %copy-done.10, bf16[4096,256]{1,0:T(8,128)(2,1)} %param.14, f32[16,4096]{1,0:T(8,128)S(1)} %reshape.155, f32[4096]{0:T(1024)S(1)} %get-tuple-element.11), kind=kOutput, calls=%fused_computation.1 | convolution fusion | flops 34756608 | bytes 2445312 | tf_op jit(solution)/shard_map/dot_general | solution.py:34
  12.9 0.7 broadcast_in_dim.3
  13.7 8.0 %all-to-all-start = ((bf16[32,16,256]{2,1,0:T(8,128)(2,1)}), bf16[32,16,256]{2,1,0:T(8,128)(2,1)S(1)}, u32[]{:S(2)}, u32[]{:S(2)}) async-start(bf16[32,16,256]{2,1,0:T(8,128)(2,1)} %broadcast_in_dim.3), calls=%async_computation | async-start | bytes 524288 | tf_op jit(solution)/shard_map/all_to_all | solution.py:242
  21.7 0.8 copy.16
  22.5 0.9 dynamic-slice_reduce_fusion
  23.4 0.6 fusion.16
  24.0 0.6 constant_dynamic-slice_fusion
  24.6 0.0 collective-permute-done.10.refs_1_
  24.6 0.7 slice.26
  25.3 0.1 collective-permute-start.12
  25.4 0.7 slice.27
  26.0 2.6 %collective-permute-start.13 = (bf16[4,64,256]{2,1,0:T(8,128)(2,1)}, bf16[4,64,256]{2,1,0:T(8,128)(2,1)}, u32[]{:S(2)}, u32[]{:S(2)}) collective-permute-start(bf16[4,64,256]{2,1,0:T(8,128)(2,1)} %slice.27), channel_id=1, source_target_pairs={{0,6},{1,7},{2,0},{3,1},{4,2},{5,3},{6,4},{7,5},{8,14},{9,15},{10,... | collective-permute-start | bytes 393224 | tf_op jit(solution)/shard_map/ppermute | solution.py:213
  28.6 0.8 copy.17
  29.4 1.1 collective-permute-start.15
  30.5 0.0 collective-permute-start.16
  30.6 0.6 collective-permute-done.12.refs_3_
  31.2 1.4 %collective-permute-start.17 = (bf16[4,64,256]{2,1,0:T(8,128)(2,1)S(1)}, bf16[4,64,256]{2,1,0:T(8,128)(2,1)S(1)}, u32[]{:S(2)}, u32[]{:S(2)}) collective-permute-start(bf16[4,64,256]{2,1,0:T(8,128)(2,1)S(1)} %collective-permute-done.12.refs_3_), channel_id=1, source_target_pairs={{0,1},{1,0},{2,3},{3,2},{4,5},{5,4},{6,7},{7,6},{8,9},{9,8},{10,11... | collective-permute-start | bytes 393224 | tf_op jit(solution)/shard_map/ppermute | solution.py:215
  32.6 0.0 collective-permute-start.18
  32.7 0.9 collective-permute-done.17.refs_8_
  33.6 0.6 collective-permute-done.18.refs_9_
  34.2 1.9 %pick.1 = (bf16[32,64,256]{2,1,0:T(8,128)(2,1)S(1)}, bf16[16,64,256]{2,1,0:T(8,128)(2,1)S(1)}) custom-call(s32[32]{0:T(128)S(1)} %fusion.14.picked, s32[16]{0:T(128)S(1)} %get-tuple-element.13.near, bf16[8,64,256]{2,1,0:T(8,128)(2,1)S(1)} %bitcast.37, bf16[8,64,256]{2,1,0:T(8,128)(2,1)S(1)} %collective-permute-done.10.refs_1_, ...), custom_call_target="tpu_custom_call" | custom-call | tf_op jit(solution)/shard_map/pick/pallas_call | solution.py:260
  36.0 1.0 copy-done.4
  37.0 0.8 copy-done.5
  37.8 9.4 %all-to-all-start.1 = ((bf16[32,64,256]{2,1,0:T(8,128)(2,1)}), bf16[32,64,256]{2,1,0:T(8,128)(2,1)}, u32[]{:S(2)}, u32[]{:S(2)}) async-start(bf16[32,64,256]{2,1,0:T(8,128)(2,1)} %copy-done.4), calls=%async_computation.1 | async-start | bytes 2097152 | tf_op jit(solution)/shard_map/all_to_all | solution.py:275
  47.2 3.3 %collective-permute-start = (bf16[512,256]{1,0:T(8,128)(2,1)S(1)}, bf16[512,256]{1,0:T(8,128)(2,1)}, u32[]{:S(2)}, u32[]{:S(2)}) collective-permute-start(bf16[512,256]{1,0:T(8,128)(2,1)S(1)} %constant_dynamic-update-slice_fusion.kv_ref), channel_id=1, source_target_pairs={{0,1},{1,2},{2,3},{3,4},{4,5},{5,6},{6,7},{7,8},{8,9},{9,10},{10,1... | collective-permute-start | bytes 786440 | tf_op jit(solution)/shard_map/ppermute | solution.py:231
  50.5 1.1 collective-permute-start.1
  51.6 1.9 %collective-permute-start.2 = (bf16[8,64,256]{2,1,0:T(8,128)(2,1)S(1)}, bf16[8,64,256]{2,1,0:T(8,128)(2,1)}, u32[]{:S(2)}, u32[]{:S(2)}) collective-permute-start(bf16[8,64,256]{2,1,0:T(8,128)(2,1)S(1)} %bitcast.39), channel_id=1, source_target_pairs={{0,6},{1,7},{2,0},{3,1},{4,2},{5,3},{6,4},{7,5},{8,14},{9,15},{10,... | collective-permute-start | bytes 786440 | tf_op jit(solution)/shard_map/ppermute | solution.py:211
  53.5 0.1 add_multiply_fusion
  53.6 0.1 add.222
  53.7 0.2 add.223
  53.9 0.1 add.225
  54.0 6.4 %collective-permute-done.1.refs_1_ = bf16[8,64,256]{2,1,0:T(8,128)(2,1)S(1)} collective-permute-done((bf16[8,64,256]{2,1,0:T(8,128)(2,1)S(1)}, bf16[8,64,256]{2,1,0:T(8,128)(2,1)S(1)}, u32[]{:S(2)}, u32[]{:S(2)}) %collective-permute-start.1) | collective-permute-done | bytes 262176 | tf_op jit(solution)/shard_map/ppermute | solution.py:210
  60.4 1.4 %collective-permute-start.3 = (bf16[4,64,256]{2,1,0:T(8,128)(2,1)S(1)}, bf16[4,64,256]{2,1,0:T(8,128)(2,1)}, u32[]{:S(2)}, u32[]{:S(2)}) collective-permute-start(bf16[4,64,256]{2,1,0:T(8,128)(2,1)S(1)} %slice.24), channel_id=1, source_target_pairs={{0,2},{1,3},{2,4},{3,5},{4,6},{5,7},{6,0},{7,1},{8,10},{9,11},{10,... | collective-permute-start | bytes 393224 | tf_op jit(solution)/shard_map/ppermute | solution.py:212
  61.8 0.9 slice.25
  62.7 2.6 %collective-permute-start.4 = (bf16[4,64,256]{2,1,0:T(8,128)(2,1)S(1)}, bf16[4,64,256]{2,1,0:T(8,128)(2,1)}, u32[]{:S(2)}, u32[]{:S(2)}) collective-permute-start(bf16[4,64,256]{2,1,0:T(8,128)(2,1)S(1)} %slice.25), channel_id=1, source_target_pairs={{0,6},{1,7},{2,0},{3,1},{4,2},{5,3},{6,4},{7,5},{8,14},{9,15},{10,... | collective-permute-start | bytes 393224 | tf_op jit(solution)/shard_map/ppermute | solution.py:213
  65.4 1.3 %iota_add_fusion = s32[16,64]{1,0:T(8,128)} fusion(s32[16]{0:T(128)} %get-tuple-element.14), kind=kLoop, calls=%fused_computation.26 | loop fusion | flops 1024 | bytes 4160 | tf_op jit(solution)/shard_map/add | solution.py:317
  66.7 0.0 collective-permute-start.5
  66.7 0.5 collective-permute-start.6
  67.2 13.2 %collective-permute-start.7 = (bf16[8,64,256]{2,1,0:T(8,128)(2,1)}, bf16[8,64,256]{2,1,0:T(8,128)(2,1)}, u32[]{:S(2)}, u32[]{:S(2)}) collective-permute-start(bf16[8,64,256]{2,1,0:T(8,128)(2,1)} %collective-permute-done.2.refs_2_), channel_id=1, source_target_pairs={{0,1},{1,0},{2,3},{3,2},{4,5},{5,4},{6,7},{7,6},{8,9},{9,8},{10,11... | collective-permute-start | bytes 786440 | tf_op jit(solution)/shard_map/ppermute | solution.py:215
  80.4 0.0 collective-permute-start.8
  80.4 0.5 collective-permute-start.9
  80.9 1.2 compare_convert_fusion
  82.1 0.9 copy.18.gw_ref
  83.0 1.4 %add.243.pos_ref = s32[1,1024]{1,0:T(1,128)} reshape(s32[16,64]{1,0:T(8,128)} %iota_add_fusion) | data formatting | bytes 8192 | tf_op jit(solution)/shard_map/add | solution.py:317
  84.3 0.1 pad_add_fusion.last
  84.4 6.3 %window.1.part_ref = f32[512,512]{1,0:T(8,128)S(1)} custom-call(s32[1]{0:T(128)} %bitcast.2.low, bf16[512,512]{1,0:T(8,128)(2,1)S(1)} %copy-done.1, bf16[512,256]{1,0:T(8,128)(2,1)} %collective-permute-done.prev_ref, bf16[512,256]{1,0:T(8,128)(2,1)S(1)} %constant_dynamic-update-slice_fusion.kv_ref, bf16[512,12]{1,0:T(8,128)(2,1)S(1)} %copy.18.gw_ref), custom_call_target="tpu_custom_call" | custom-call | tf_op jit(solution)/shard_map/window/pallas_call | solution.py:279
  90.7 0.0 collective-permute-done.9.refs_9_
  90.7 23.9 %coarse.1.part_ref = f32[512,512]{1,0:T(8,128)S(1)} custom-call(s32[2]{0:T(128)S(1)} %pad_add_fusion.last, bf16[512,512]{1,0:T(8,128)(2,1)S(1)} %copy-done.1, bf16[512,12]{1,0:T(8,128)(2,1)S(1)} %copy.18.gw_ref, f32[512,512]{1,0:T(8,128)S(1)} %window.1.part_ref, s32[8,512]{1,0:T(8,128)S(1)} %multiply_add_fusion.ends_ref, bf16[8,64,256]{2,1,0:T(8,128)(2,1)S(1)} %bitcast.41, ...), custom_call_target="tpu_custom_call" | custom-call | tf_op jit(solution)/shard_map/coarse/pallas_call | solution.py:299
  114.7 1.0 copy-done.2
  115.6 1.2 copy-done.3
  116.9 1.0 copy-done.6
  117.9 0.7 copy-done.7
  118.6 0.6 copy-done.8
  119.2 0.7 copy-done.9
  119.9 6.6 %fine.1 = bf16[512,512]{1,0:T(8,128)(2,1)} custom-call(s32[16]{0:T(128)S(1)} %copy-done.9, s32[16]{0:T(128)S(1)} %copy-done.8, s32[1]{0:T(128)} %bitcast.base, bf16[512,512]{1,0:T(8,128)(2,1)S(1)} %copy-done.1, bf16[512,12]{1,0:T(8,128)(2,1)S(1)} %copy.18.gw_ref, f32[512,512]{1,0:T(8,128)S(1)} %copy-done.3, s32[1,1024]{1,0:T(1,128)S(1)} %copy-done.7, ...), custom_call_target="tpu_custom_call" | custom-call | tf_op jit(solution)/shard_map/fine/pallas_call | solution.py:319
  (40 shorter events, 0.2 us)
Async XLA Ops:
  0.0 9.4 %copy-start = (bf16[4096,256]{1,0:T(8,128)(2,1)S(1)}, bf16[4096,256]{1,0:T(8,128)(2,1)}, u32[]{:S(2)}) copy-start(bf16[4096,256]{1,0:T(8,128)(2,1)} %param.16) | copy-start | bytes 6291460
  0.0 10.8 %copy-start.10 = (bf16[256,128]{1,0:T(8,128)(2,1)S(1)}, bf16[256,128]{1,0:T(8,128)(2,1)}, u32[]{:S(2)}) copy-start(bf16[256,128]{1,0:T(8,128)(2,1)} %param.15) | copy-start | bytes 196612
  2.0 22.6 %collective-permute-start.10 = (bf16[8,64,256]{2,1,0:T(8,128)(2,1)S(1)}, bf16[8,64,256]{2,1,0:T(8,128)(2,1)S(1)}, u32[]{:S(2)}, u32[]{:S(2)}) collective-permute-start(bf16[8,64,256]{2,1,0:T(8,128)(2,1)S(1)} %bitcast.34), channel_id=1, source_target_pairs={{0,2},{1,3},{2,4},{3,5},{4,6},{5,7},{6,0},{7,1},{8,10},{9,11},{10,... | collective-permute-start | bytes 786440 | tf_op jit(solution)/shard_map/ppermute | solution.py:210
  3.4 22.0 %collective-permute-start.11 = (bf16[8,64,256]{2,1,0:T(8,128)(2,1)S(1)}, bf16[8,64,256]{2,1,0:T(8,128)(2,1)S(1)}, u32[]{:S(2)}, u32[]{:S(2)}) collective-permute-start(bf16[8,64,256]{2,1,0:T(8,128)(2,1)S(1)} %bitcast.35), channel_id=1, source_target_pairs={{0,6},{1,7},{2,0},{3,1},{4,2},{5,3},{6,4},{7,5},{8,14},{9,15},{10,... | collective-permute-start | bytes 786440 | tf_op jit(solution)/shard_map/ppermute | solution.py:211
  4.9 27.7 %collective-permute-start.14 = (bf16[8,64,256]{2,1,0:T(8,128)(2,1)S(1)}, bf16[8,64,256]{2,1,0:T(8,128)(2,1)S(1)}, u32[]{:S(2)}, u32[]{:S(2)}) collective-permute-start(bf16[8,64,256]{2,1,0:T(8,128)(2,1)S(1)} %bitcast.36), channel_id=1, source_target_pairs={{0,1},{1,0},{2,3},{3,2},{4,5},{5,4},{6,7},{7,6},{8,9},{9,8},{10,11... | collective-permute-start | bytes 786440 | tf_op jit(solution)/shard_map/ppermute | solution.py:215
  13.7 24.1 %all-to-all-start = ((bf16[32,16,256]{2,1,0:T(8,128)(2,1)}), bf16[32,16,256]{2,1,0:T(8,128)(2,1)S(1)}, u32[]{:S(2)}, u32[]{:S(2)}) async-start(bf16[32,16,256]{2,1,0:T(8,128)(2,1)} %broadcast_in_dim.3), calls=%async_computation | async-start | bytes 524288 | tf_op jit(solution)/shard_map/all_to_all | solution.py:242
  23.4 5.2 %copy-start.11 = (s32[16]{0:T(128)}, s32[16]{0:T(128)S(1)}, u32[]{:S(2)}) copy-start(s32[16]{0:T(128)S(1)} %dynamic-slice_reduce_fusion) | copy-start | bytes 196
  25.3 5.9 %collective-permute-start.12 = (bf16[4,64,256]{2,1,0:T(8,128)(2,1)}, bf16[4,64,256]{2,1,0:T(8,128)(2,1)S(1)}, u32[]{:S(2)}, u32[]{:S(2)}) collective-permute-start(bf16[4,64,256]{2,1,0:T(8,128)(2,1)} %slice.26), channel_id=1, source_target_pairs={{0,2},{1,3},{2,4},{3,5},{4,6},{5,7},{6,0},{7,1},{8,10},{9,11},{10,... | collective-permute-start | bytes 393224 | tf_op jit(solution)/shard_map/ppermute | solution.py:212
  26.0 6.6 %collective-permute-start.13 = (bf16[4,64,256]{2,1,0:T(8,128)(2,1)}, bf16[4,64,256]{2,1,0:T(8,128)(2,1)}, u32[]{:S(2)}, u32[]{:S(2)}) collective-permute-start(bf16[4,64,256]{2,1,0:T(8,128)(2,1)} %slice.27), channel_id=1, source_target_pairs={{0,6},{1,7},{2,0},{3,1},{4,2},{5,3},{6,4},{7,5},{8,14},{9,15},{10,... | collective-permute-start | bytes 393224 | tf_op jit(solution)/shard_map/ppermute | solution.py:213
  29.4 3.3 %collective-permute-start.15 = (bf16[8,64,256]{2,1,0:T(8,128)(2,1)S(1)}, bf16[8,64,256]{2,1,0:T(8,128)(2,1)S(1)}, u32[]{:S(2)}, u32[]{:S(2)}) collective-permute-start(bf16[8,64,256]{2,1,0:T(8,128)(2,1)S(1)} %collective-permute-done.10.refs_1_), channel_id=1, source_target_pairs={{0,1},{1,0},{2,3},{3,2},{4,5},{5,4},{6,7},{7,6},{8,9},{9,8},{10,11... | collective-permute-start | bytes 786440 | tf_op jit(solution)/shard_map/ppermute | solution.py:215
  30.5 2.2 %collective-permute-start.16 = (bf16[8,64,256]{2,1,0:T(8,128)(2,1)S(1)}, bf16[8,64,256]{2,1,0:T(8,128)(2,1)S(1)}, u32[]{:S(2)}, u32[]{:S(2)}) collective-permute-start(bf16[8,64,256]{2,1,0:T(8,128)(2,1)S(1)} %collective-permute-done.11.refs_2_), channel_id=1, source_target_pairs={{0,1},{1,0},{2,3},{3,2},{4,5},{5,4},{6,7},{7,6},{8,9},{9,8},{10,11... | collective-permute-start | bytes 786440 | tf_op jit(solution)/shard_map/ppermute | solution.py:215
  31.2 2.4 %collective-permute-start.17 = (bf16[4,64,256]{2,1,0:T(8,128)(2,1)S(1)}, bf16[4,64,256]{2,1,0:T(8,128)(2,1)S(1)}, u32[]{:S(2)}, u32[]{:S(2)}) collective-permute-start(bf16[4,64,256]{2,1,0:T(8,128)(2,1)S(1)} %collective-permute-done.12.refs_3_), channel_id=1, source_target_pairs={{0,1},{1,0},{2,3},{3,2},{4,5},{5,4},{6,7},{7,6},{8,9},{9,8},{10,11... | collective-permute-start | bytes 393224 | tf_op jit(solution)/shard_map/ppermute | solution.py:215
  32.6 1.6 %collective-permute-start.18 = (bf16[4,64,256]{2,1,0:T(8,128)(2,1)}, bf16[4,64,256]{2,1,0:T(8,128)(2,1)S(1)}, u32[]{:S(2)}, u32[]{:S(2)}) collective-permute-start(bf16[4,64,256]{2,1,0:T(8,128)(2,1)} %collective-permute-done.13.refs_4_), channel_id=1, source_target_pairs={{0,1},{1,0},{2,3},{3,2},{4,5},{5,4},{6,7},{7,6},{8,9},{9,8},{10,11... | collective-permute-start | bytes 393224 | tf_op jit(solution)/shard_map/ppermute | solution.py:215
  36.0 1.0 copy-start.4
  37.0 0.8 copy-start.5
  37.8 46.6 %copy-start.1 = (bf16[512,512]{1,0:T(8,128)(2,1)S(1)}, bf16[512,512]{1,0:T(8,128)(2,1)}, u32[]{:S(2)}) copy-start(bf16[512,512]{1,0:T(8,128)(2,1)} %q_ref.5) | copy-start | bytes 1572868
  37.8 77.8 %all-to-all-start.1 = ((bf16[32,64,256]{2,1,0:T(8,128)(2,1)}), bf16[32,64,256]{2,1,0:T(8,128)(2,1)}, u32[]{:S(2)}, u32[]{:S(2)}) async-start(bf16[32,64,256]{2,1,0:T(8,128)(2,1)} %copy-done.4), calls=%async_computation.1 | async-start | bytes 2097152 | tf_op jit(solution)/shard_map/all_to_all | solution.py:275
  47.2 20.0 %collective-permute-start = (bf16[512,256]{1,0:T(8,128)(2,1)S(1)}, bf16[512,256]{1,0:T(8,128)(2,1)}, u32[]{:S(2)}, u32[]{:S(2)}) collective-permute-start(bf16[512,256]{1,0:T(8,128)(2,1)S(1)} %constant_dynamic-update-slice_fusion.kv_ref), channel_id=1, source_target_pairs={{0,1},{1,2},{2,3},{3,4},{4,5},{5,6},{6,7},{7,8},{8,9},{9,10},{10,1... | collective-permute-start | bytes 786440 | tf_op jit(solution)/shard_map/ppermute | solution.py:231
  50.5 9.9 %collective-permute-start.1 = (bf16[8,64,256]{2,1,0:T(8,128)(2,1)S(1)}, bf16[8,64,256]{2,1,0:T(8,128)(2,1)S(1)}, u32[]{:S(2)}, u32[]{:S(2)}) collective-permute-start(bf16[8,64,256]{2,1,0:T(8,128)(2,1)S(1)} %bitcast.38), channel_id=1, source_target_pairs={{0,2},{1,3},{2,4},{3,5},{4,6},{5,7},{6,0},{7,1},{8,10},{9,11},{10,... | collective-permute-start | bytes 786440 | tf_op jit(solution)/shard_map/ppermute | solution.py:210
  51.6 10.2 %collective-permute-start.2 = (bf16[8,64,256]{2,1,0:T(8,128)(2,1)S(1)}, bf16[8,64,256]{2,1,0:T(8,128)(2,1)}, u32[]{:S(2)}, u32[]{:S(2)}) collective-permute-start(bf16[8,64,256]{2,1,0:T(8,128)(2,1)S(1)} %bitcast.39), channel_id=1, source_target_pairs={{0,6},{1,7},{2,0},{3,1},{4,2},{5,3},{6,4},{7,5},{8,14},{9,15},{10,... | collective-permute-start | bytes 786440 | tf_op jit(solution)/shard_map/ppermute | solution.py:211
  60.4 19.9 %collective-permute-start.3 = (bf16[4,64,256]{2,1,0:T(8,128)(2,1)S(1)}, bf16[4,64,256]{2,1,0:T(8,128)(2,1)}, u32[]{:S(2)}, u32[]{:S(2)}) collective-permute-start(bf16[4,64,256]{2,1,0:T(8,128)(2,1)S(1)} %slice.24), channel_id=1, source_target_pairs={{0,2},{1,3},{2,4},{3,5},{4,6},{5,7},{6,0},{7,1},{8,10},{9,11},{10,... | collective-permute-start | bytes 393224 | tf_op jit(solution)/shard_map/ppermute | solution.py:212
  62.7 17.6 %collective-permute-start.4 = (bf16[4,64,256]{2,1,0:T(8,128)(2,1)S(1)}, bf16[4,64,256]{2,1,0:T(8,128)(2,1)}, u32[]{:S(2)}, u32[]{:S(2)}) collective-permute-start(bf16[4,64,256]{2,1,0:T(8,128)(2,1)S(1)} %slice.25), channel_id=1, source_target_pairs={{0,6},{1,7},{2,0},{3,1},{4,2},{5,3},{6,4},{7,5},{8,14},{9,15},{10,... | collective-permute-start | bytes 393224 | tf_op jit(solution)/shard_map/ppermute | solution.py:213
  66.7 24.0 %collective-permute-start.5 = (bf16[8,64,256]{2,1,0:T(8,128)(2,1)S(1)}, bf16[8,64,256]{2,1,0:T(8,128)(2,1)}, u32[]{:S(2)}, u32[]{:S(2)}) collective-permute-start(bf16[8,64,256]{2,1,0:T(8,128)(2,1)S(1)} %bitcast.40), channel_id=1, source_target_pairs={{0,1},{1,0},{2,3},{3,2},{4,5},{5,4},{6,7},{7,6},{8,9},{9,8},{10,11... | collective-permute-start | bytes 786440 | tf_op jit(solution)/shard_map/ppermute | solution.py:215
  66.7 24.0 %collective-permute-start.6 = (bf16[8,64,256]{2,1,0:T(8,128)(2,1)S(1)}, bf16[8,64,256]{2,1,0:T(8,128)(2,1)}, u32[]{:S(2)}, u32[]{:S(2)}) collective-permute-start(bf16[8,64,256]{2,1,0:T(8,128)(2,1)S(1)} %collective-permute-done.1.refs_1_), channel_id=1, source_target_pairs={{0,1},{1,0},{2,3},{3,2},{4,5},{5,4},{6,7},{7,6},{8,9},{9,8},{10,11... | collective-permute-start | bytes 786440 | tf_op jit(solution)/shard_map/ppermute | solution.py:215
  67.2 23.5 %collective-permute-start.7 = (bf16[8,64,256]{2,1,0:T(8,128)(2,1)}, bf16[8,64,256]{2,1,0:T(8,128)(2,1)}, u32[]{:S(2)}, u32[]{:S(2)}) collective-permute-start(bf16[8,64,256]{2,1,0:T(8,128)(2,1)} %collective-permute-done.2.refs_2_), channel_id=1, source_target_pairs={{0,1},{1,0},{2,3},{3,2},{4,5},{5,4},{6,7},{7,6},{8,9},{9,8},{10,11... | collective-permute-start | bytes 786440 | tf_op jit(solution)/shard_map/ppermute | solution.py:215
  80.4 10.3 %collective-permute-start.8 = (bf16[4,64,256]{2,1,0:T(8,128)(2,1)}, bf16[4,64,256]{2,1,0:T(8,128)(2,1)}, u32[]{:S(2)}, u32[]{:S(2)}) collective-permute-start(bf16[4,64,256]{2,1,0:T(8,128)(2,1)} %collective-permute-done.3.refs_3_), channel_id=1, source_target_pairs={{0,1},{1,0},{2,3},{3,2},{4,5},{5,4},{6,7},{7,6},{8,9},{9,8},{10,11... | collective-permute-start | bytes 393224 | tf_op jit(solution)/shard_map/ppermute | solution.py:215
  80.4 10.3 %collective-permute-start.9 = (bf16[4,64,256]{2,1,0:T(8,128)(2,1)}, bf16[4,64,256]{2,1,0:T(8,128)(2,1)}, u32[]{:S(2)}, u32[]{:S(2)}) collective-permute-start(bf16[4,64,256]{2,1,0:T(8,128)(2,1)} %collective-permute-done.4.refs_4_), channel_id=1, source_target_pairs={{0,1},{1,0},{2,3},{3,2},{4,5},{5,4},{6,7},{7,6},{8,9},{9,8},{10,11... | collective-permute-start | bytes 393224 | tf_op jit(solution)/shard_map/ppermute | solution.py:215
  114.7 1.0 copy-start.2
  115.6 1.2 copy-start.3
  116.9 1.0 copy-start.6
  117.9 0.7 copy-start.7
  118.6 0.6 copy-start.8
  119.2 0.7 copy-start.9

commit v2 on v1

v2 whole, which is shorter than its diff:
```python
import math

import jax
import jax.numpy as jnp
from jax import lax
from jax.experimental import pallas as pl
from jax.experimental.pallas import tpu as pltpu
from jax.sharding import PartitionSpec as P

HEAD_DIM = 128
HEADS = 4
CMP_BLOCK = 32
SEL_BLOCK = 64
TOPN = 16
WINDOW = 512
NEG = -1e30
SCALE2 = HEAD_DIM**-0.5 * math.log2(math.e)
AXES = ("blk", "grp")
ANY = pl.BlockSpec(memory_space=pl.ANY)
HBM = pl.BlockSpec(memory_space=pltpu.MemorySpace.HBM)
SMEM = pl.BlockSpec(memory_space=pltpu.SMEM)
VMEM = pl.BlockSpec(memory_space=pltpu.VMEM)


def route(stretches, rows, cores, move):
    pairs = []
    for b in range(stretches):
        for y in range(rows):
            for c in range(cores):
                to_y, to_c = move(y, c)
                pairs.append(((b * rows + y) * cores + c, (b * rows + to_y % rows) * cores + to_c))
    return pairs


def dot_t(a, b):
    return lax.dot_general(a, b, (((1,), (1,)), ((), ())), preferred_element_type=jnp.float32)


def lane_groups(x, op):
    parts = [x[:, i : i + 128] for i in range(0, x.shape[1], 128)]
    while len(parts) > 1:
        parts = [
            op(parts[i], parts[i + 1]) if i + 1 < len(parts) else parts[i]
            for i in range(0, len(parts), 2)
        ]
    return parts[0]


def gates_of(q_ref, gw_ref):
    return jax.nn.sigmoid(dot_t(q_ref[...], gw_ref[...]))


def start_all(pairs, sem):
    copies = [pltpu.make_async_copy(s, d, sem.at[i]) for i, (s, d) in enumerate(pairs)]
    for copy in copies:
        copy.start()
    return copies


def copy_all(pairs, sem):
    for copy in start_all(pairs, sem):
        copy.wait()


def prep_kernel(ids, keys_ref, values_ref, sel_ref, kv_ref, meta_ref, raw, sel_buf, sem):
    copy_all([(keys_ref, raw.at[0]), (values_ref, raw.at[1]), (sel_ref, sel_buf)], sem)
    kv_ref[:, :HEAD_DIM] = raw[0]
    kv_ref[:, HEAD_DIM:] = raw[1]
    sel = sel_buf[...]
    groups = sel.shape[1]
    group = lax.broadcasted_iota(jnp.int32, sel.shape, 1)
    match = ((sel >> 6) == ids[0]) & ((group >> 3) != ids[0])
    slot = slot_of(sel & 63, ids[1])
    meta_ref[:, :groups] = jnp.sum(jnp.where(match, slot, 0), axis=0, keepdims=True)
    mine = jnp.sum(jnp.where(group == ids[0] * 8 + ids[1], sel, 0), axis=1, keepdims=True)
    lane = lax.broadcasted_iota(jnp.int32, (TOPN, 128), 1)
    entry = lax.broadcasted_iota(jnp.int32, (TOPN, 128), 0)
    row = jnp.sum(jnp.where(lane == entry, mine, 0), axis=0, keepdims=True)
    row = jnp.where(lane[:1] == TOPN, ids[0], row)
    meta_ref[:, groups:] = jnp.where(lane[:1] == TOPN + 1, ids[1], row)


def unpack(meta):
    return meta[0, 256 + TOPN], meta[0, 257 + TOPN], [meta[0, 256 + i] for i in range(TOPN)]


def slot_of(block, column):
    owner = block >> 3
    dy = ((column >> 1) - (owner >> 1)) & 3
    return (((dy << 1) + ((owner ^ column) & 1)) << 3) + (block & 7)


def compress_kernel(
    keys_ref, values_ref, pos_ref, k_in, k_out, v_in, v_out, out_ref, raw, pos, wide, flat, w1, w2, sem
):
    toks = keys_ref.shape[0]
    count = toks // CMP_BLOCK
    loads = start_all(
        [
            (keys_ref, raw.at[0]),
            (pos_ref, pos),
            (values_ref, raw.at[1]),
            (k_in, w1.at[0]),
            (k_out, w2.at[0]),
            (v_in, w1.at[1]),
            (v_out, w2.at[1]),
        ],
        sem,
    )
    for load in loads[:3]:
        load.wait()
    for side in range(2):
        shift = pos[side].astype(jnp.float32)
        x = raw[side].astype(jnp.float32).reshape(count, CMP_BLOCK, HEAD_DIM) + shift[None]
        wide[side] = x.reshape(toks, HEAD_DIM)
        for t in range(CMP_BLOCK):
            rows = wide[side, pl.ds(t, count, stride=CMP_BLOCK), :]
            flat[side, :, t * HEAD_DIM : (t + 1) * HEAD_DIM] = rows.astype(jnp.bfloat16)
    for side in range(2):
        for load in loads[3 + 2 * side : 5 + 2 * side]:
            load.wait()
        hidden = jnp.dot(flat[side], w1[side], preferred_element_type=jnp.float32)
        hidden = (hidden * jax.nn.sigmoid(hidden)).astype(jnp.bfloat16)
        comp = jnp.dot(hidden, w2[side], preferred_element_type=jnp.float32).astype(jnp.bfloat16)
        cols = slice(side * HEAD_DIM, (side + 1) * HEAD_DIM)
        out_ref[:, :, cols] = jnp.broadcast_to(comp[None], (out_ref.shape[0], count, HEAD_DIM))


def piece_pairs(pieces, near, far):
    pairs = []
    for dc in range(2):
        o, a, b, fa, fb = pieces[dc * 5 : dc * 5 + 5]
        for dy, ref in ((0, o), (1, a), (3, b)):
            pairs.append((ref, near(dy * 2 + dc)))
        half = fa.shape[0]
        pairs.append((fa, far(4 + dc, 0, half)))
        pairs.append((fb, far(4 + dc, half, half)))
    return pairs


def pick_kernel(meta, *refs):
    pieces = refs[:10]
    out, nearby, rows, sem = refs[10:]
    copy_all(
        piece_pairs(
            pieces,
            lambda slot: rows.at[pl.ds(slot * 8, 8)],
            lambda slot, at, n: rows.at[pl.ds(slot * 8 + at, n)],
        ),
        sem,
    )
    stretch, column, mine = unpack(meta)
    pairs = [(rows.at[meta[0, i * 8 + column]], out.at[i]) for i in range(out.shape[0])]
    for i in range(TOPN):
        pairs.append((rows.at[slot_of(mine[i] & 63, column)], nearby.at[i]))
    copy_all(pairs, sem)


def fill_ones(values):
    values[:, HEAD_DIM:] = jnp.ones((values.shape[0], HEAD_DIM), values.dtype)


def attend(q, keys, values, seen):
    s = dot_t(q, keys)
    if seen is not None:
        s = jnp.where(seen, s, NEG)
    top = jnp.max(lane_groups(s, jnp.maximum), axis=1, keepdims=True)
    p = jnp.exp2((s - top) * SCALE2).astype(jnp.bfloat16)
    o = jnp.dot(p, values, preferred_element_type=jnp.float32)
    return o[:, :HEAD_DIM], o[:, HEAD_DIM:]


def window_kernel(
    meta, q_in, gw_in, kv_in, s_own, s_from1, edge, out, q_ref, gw_ref, out_ref, keys, values, sem
):
    loads = start_all([(q_in, q_ref), (gw_in, gw_ref)], sem.at[pl.ds(4, 2)])
    stretch, column, _ = unpack(meta)
    toks = q_in.shape[0]
    heads = slice(0, HEAD_DIM)
    tails = slice(HEAD_DIM, 2 * HEAD_DIM)

    def fetch(ref, at, i):
        copy_all(
            [
                (ref.at[:, heads], keys.at[pl.ds(at, toks)]),
                (ref.at[:, tails], values.at[pl.ds(at, toks), heads]),
            ],
            sem.at[pl.ds(2 * i, 2)],
        )

    @pl.when(column % 2 == 1)
    def _():
        fetch(s_own, 0, 0)

    @pl.when((column % 2 == 0) & (column > 0))
    def _():
        fetch(s_from1, 0, 0)

    @pl.when(column == 0)
    def _():
        fetch(edge, 0, 0)

    fetch(kv_in, toks, 1)
    fill_ones(values)
    for load in loads:
        load.wait()
    low = jnp.where(stretch * 8 + column == 0, toks, 0)
    gates = gates_of(q_ref, gw_ref)
    rows = 128
    for first in range(0, toks, rows):
        span = slice(first, first + WINDOW + rows)
        r = lax.broadcasted_iota(jnp.int32, (rows, WINDOW + rows), 0)
        c = lax.broadcasted_iota(jnp.int32, (rows, WINDOW + rows), 1)
        seen = (c > r) & (c <= r + WINDOW) & (c + first >= low)
        for h in range(HEADS):
            cols = slice(h * HEAD_DIM, (h + 1) * HEAD_DIM)
            o, total = attend(q_ref[first : first + rows, cols], keys[span], values[span], seen)
            g = gates[first : first + rows, 2 * HEADS + h : 2 * HEADS + h + 1]
            out_ref[first : first + rows, cols] = o * (g / total)
    copy_all([(out_ref, out)], sem.at[pl.ds(6, 1)])


NEAR_SLOTS = ((0, 0), (0, 1), (1, 0), (1, 1), (3, 0), (3, 1))
FAR_SLOTS = ((2, 0), (2, 1))


def coarse_ends(stretch_z, zs, slots, column):
    lane = lax.broadcasted_iota(jnp.int32, (1, zs * len(slots) * 64), 1)
    z = jnp.zeros_like(lane)
    for i in range(1, zs):
        z += (lane >= i * len(slots) * 64).astype(jnp.int32)
    place = (lane >> 6) - z * len(slots)
    owner = jnp.zeros_like(lane)
    for i, (dy, dc) in enumerate(slots):
        theirs = ((((column >> 1) - dy) & 3) << 1) + ((column ^ dc) & 1)
        owner = jnp.where(place == i, theirs, owner)
    blk = ((stretch_z + z) << 2) + ((lane >> 4) & 3)
    return (((blk << 3) + owner) * 16 + (lane & 15)) * CMP_BLOCK + (CMP_BLOCK - 1)


def load_coarse(pairs, keys, values, sem):
    copies = []
    for ref, at in pairs:
        copies.append((ref.at[:, :, :HEAD_DIM], keys.at[at]))
        copies.append((ref.at[:, :, HEAD_DIM:], values.at[(*at, slice(None), slice(0, HEAD_DIM))]))
    loads = start_all(copies, sem)
    values[..., HEAD_DIM:] = jnp.ones((*values.shape[:3], HEAD_DIM), values.dtype)
    return loads


def fold(q, keys, values, seen, old):
    s = dot_t(q, keys)
    if seen is not None:
        s = jnp.where(seen, s, NEG)
    acc, total, best = old
    top = jnp.maximum(best, jnp.max(lane_groups(s, jnp.maximum), axis=1, keepdims=True))
    wide = jnp.concatenate([top] * (s.shape[1] // 128), axis=1)
    p = jnp.exp2((s - wide) * SCALE2).astype(jnp.bfloat16)
    factor = jnp.exp2((best - top) * SCALE2)
    o = jnp.dot(p, values, preferred_element_type=jnp.float32)
    return acc * factor + o[:, :HEAD_DIM], total * factor + o[:, HEAD_DIM:], top


ROWS = 256
PARTS = (slice(0, 128), slice(128, 256), slice(256, 384))


def near_kernel(meta, q_in, own, s_own, from1, s_from1, from3, s_from3, state, q_ref, keys, values, sem):
    q_load = pltpu.make_async_copy(q_in, q_ref, sem.at[12])
    q_load.start()
    stretch, column, _ = unpack(meta)
    toks = q_in.shape[0]
    pieces = (own, s_own, from1, s_from1, from3, s_from3)
    loads = load_coarse([(ref, (slice(None), i)) for i, ref in enumerate(pieces)], keys, values, sem)
    state[:, :, PARTS[0]] = jnp.zeros((HEADS, toks, 128), jnp.float32)
    state[:, :, PARTS[1]] = jnp.ones((HEADS, toks, 128), jnp.float32)
    state[:, :, PARTS[2]] = jnp.zeros((HEADS, toks, 128), jnp.float32)
    for load in [q_load, *loads]:
        load.wait()
    pair = stretch >> 3
    chunk = 2 * len(NEAR_SLOTS) * 64
    ends = coarse_ends(pair << 1, 2, NEAR_SLOTS, column)
    base = (stretch * 8 + column) * toks

    def step(z, masked):
        k = keys[pl.ds(2 * z, 2)].reshape(chunk, HEAD_DIM)
        v = values[pl.ds(2 * z, 2)].reshape(chunk, 2 * HEAD_DIM)
        for first in range(0, toks, ROWS):
            span = slice(first, first + ROWS)
            seen = None
            if masked:
                seen = ends <= base + first + lax.broadcasted_iota(jnp.int32, (ROWS, chunk), 0)
            for h in range(HEADS):
                cols = slice(h * HEAD_DIM, (h + 1) * HEAD_DIM)
                old = tuple(state[h, span, part] for part in PARTS)
                for part, new in zip(PARTS, fold(q_ref[span, cols], k, v, seen, old)):
                    state[h, span, part] = new

    def full(z, carry):
        step(z, False)
        return carry

    lax.fori_loop(0, pair, full, 0)
    step(pair, True)


def fine_kernel(
    meta, q_in, gw_in, part_in, state, a, b, s_a, s_b, near_ref, incoming, *refs
):
    out, q_ref, gw_ref, part_ref, c_keys, c_values, keys, values, done = refs[:9]
    in_sem, c_sem, sem, out_sem = refs[9:]
    toks = q_in.shape[0]
    first_loads = start_all([(q_in, q_ref), (gw_in, gw_ref), (part_in, part_ref)], in_sem)
    stretch, column, mine = unpack(meta)
    group = stretch * 8 + column
    half = a.shape[0]
    low, high = slice(0, half), slice(half, 2 * half)
    pairs = [(a, (low, 0)), (b, (high, 0)), (s_a, (low, 1)), (s_b, (high, 1))]
    loads = load_coarse(pairs, c_keys, c_values, c_sem)

    def fetch(i, run):
        owner = mine[i] >> 6
        place = pl.ds(i * SEL_BLOCK, SEL_BLOCK)

        def both(ref):
            to = values.at[place, pl.ds(0, HEAD_DIM)]
            run(pltpu.make_async_copy(ref.at[:, pl.ds(0, HEAD_DIM)], keys.at[place], sem.at[i]))
            run(pltpu.make_async_copy(ref.at[:, pl.ds(HEAD_DIM, HEAD_DIM)], to, sem.at[TOPN + i]))

        @pl.when(owner != stretch)
        def _():
            both(incoming.at[owner])

        @pl.when(owner == stretch)
        def _():
            both(near_ref.at[i])

    for i in range(TOPN):
        fetch(i, lambda copy: copy.start())
    fill_ones(values)
    lane = lax.broadcasted_iota(jnp.int32, (1, 2 * SEL_BLOCK), 1)
    pos = jnp.concatenate(
        [
            jnp.where(
                lane < SEL_BLOCK,
                mine[i] * SEL_BLOCK + lane,
                (mine[i + 1] - 1) * SEL_BLOCK + lane,
            )
            for i in range(0, TOPN, 2)
        ],
        axis=1,
    )
    for load in first_loads:
        load.wait()
    gates = gates_of(q_ref, gw_ref)
    chunk = 2 * half * len(FAR_SLOTS) * 64
    ends = coarse_ends(0, 2 * half, FAR_SLOTS, column)
    for load in loads:
        load.wait()
    for i in range(TOPN):
        fetch(i, lambda copy: copy.wait())
    c_k = c_keys[...].reshape(chunk, HEAD_DIM)
    c_v = c_values[...].reshape(chunk, 2 * HEAD_DIM)
    writes = []
    for first in range(0, toks, ROWS):
        span = slice(first, first + ROWS)
        base = group * toks + first
        place = base + lax.broadcasted_iota(jnp.int32, (ROWS, keys.shape[0]), 0)
        seen = pos <= place
        c_seen = ends <= place
        for h in range(HEADS):
            cols = slice(h * HEAD_DIM, (h + 1) * HEAD_DIM)
            old = tuple(state[h, span, part] for part in PARTS)
            acc, c_total, _ = fold(q_ref[span, cols], c_k, c_v, c_seen, old)
            o, total = attend(q_ref[span, cols], keys[...], values[...], seen)
            out_h = part_ref[span, cols] + acc * (gates[span, h : h + 1] / c_total)
            out_h += o * (gates[span, HEADS + h : HEADS + h + 1] / total)
            done[span, cols] = out_h.astype(done.dtype)
        write = pltpu.make_async_copy(done.at[span], out.at[span], out_sem.at[first // ROWS])
        write.start()
        writes.append(write)
    for write in writes:
        write.wait()


def hbm(x):
    return pltpu.with_memory_space_constraint(x, pltpu.MemorySpace.HBM)


def params(mib):
    return pltpu.CompilerParams(vmem_limit_bytes=mib << 20)


def solution(mesh):
    stretches = mesh.shape["blk"]
    group_size = mesh.shape["grp"]
    cores = 2
    ys = group_size // cores
    depth = 8
    up = route(stretches, ys, cores, lambda y, c: (y + 1, c))
    down = route(stretches, ys, cores, lambda y, c: (y - 1, c))
    swap = route(stretches, ys, cores, lambda y, c: (y, 1 - c))
    behind = [(i * group_size - 1, i * group_size) for i in range(1, stretches)]

    def cross(piece):
        return lax.ppermute(piece, AXES, swap)

    def spread(piece, ahead):
        half = piece.shape[0] // 2
        from1 = lax.ppermute(piece, AXES, up)
        from3 = lax.ppermute(piece, AXES, down)
        crossed = cross(piece)
        from1, from3, ahead = lax.optimization_barrier((from1, from3, ahead))
        far = (lax.ppermute(from1[:half], AXES, up), lax.ppermute(from3[half:], AXES, down))
        near = (piece, crossed, from1, cross(from1), from3, cross(from3))
        return near, far, ahead

    def per_device(
        queries, keys, values, selected, key_in, key_out, value_in, value_out, positions, gate_weight
    ):
        ids = jnp.stack([lax.axis_index("blk"), lax.axis_index("grp")]).astype(jnp.int32)
        ids, sel, keys, values, key_in, key_out, value_in, value_out, positions, queries, gate_weight = (
            hbm(x)
            for x in (
                ids,
                selected.T,
                keys,
                values,
                key_in,
                key_out,
                value_in,
                value_out,
                positions,
                queries,
                gate_weight.T,
            )
        )
        toks = queries.shape[0]
        per_dev = toks // SEL_BLOCK
        per_row = group_size * per_dev
        ncomp = toks // CMP_BLOCK
        per_z = stretches // depth * ncomp
        f32_rows = jax.ShapeDtypeStruct(queries.shape, jnp.float32)
        blocks = (SEL_BLOCK, 2 * HEAD_DIM)

        kv, meta = pl.pallas_call(
            prep_kernel,
            in_specs=[SMEM] + [HBM] * 3,
            out_specs=[VMEM] * 2,
            out_shape=[
                jax.ShapeDtypeStruct((toks, 2 * HEAD_DIM), jnp.bfloat16),
                jax.ShapeDtypeStruct((1, stretches * group_size + 128), jnp.int32),
            ],
            scratch_shapes=[
                pltpu.VMEM((2, toks, HEAD_DIM), jnp.bfloat16),
                pltpu.VMEM((TOPN, stretches * group_size), jnp.int32),
                pltpu.SemaphoreType.DMA((3,)),
            ],
            compiler_params=params(8),
            name="prep",
        )(ids, keys, values, sel)
        meta = hbm(meta)
        copies = pl.pallas_call(
            compress_kernel,
            in_specs=[HBM] * 7,
            out_specs=VMEM,
            out_shape=jax.ShapeDtypeStruct((stretches, ncomp, 2 * HEAD_DIM), jnp.bfloat16),
            scratch_shapes=[
                pltpu.VMEM((2, toks, HEAD_DIM), jnp.bfloat16),
                pltpu.VMEM(positions.shape, jnp.bfloat16),
                pltpu.VMEM((2, toks, HEAD_DIM), jnp.float32),
                pltpu.VMEM((2, ncomp, CMP_BLOCK * HEAD_DIM), jnp.bfloat16),
                pltpu.VMEM((2, *key_in.shape), jnp.bfloat16),
                pltpu.VMEM((2, *key_out.shape), jnp.bfloat16),
                pltpu.SemaphoreType.DMA((7,)),
            ],
            compiler_params=params(16),
            name="compress",
        )(keys, values, positions, key_in, key_out, value_in, value_out)
        near, far, copies = spread(kv.reshape(per_dev, *blocks), copies)
        edge = lax.ppermute(near[0], AXES, behind)
        s_own, s_from1 = near[1], near[3]
        copies, edge, _ = lax.optimization_barrier((copies, edge, (far, near[1], near[3], near[5])))
        column_comp = lax.all_to_all(copies, "blk", split_axis=0, concat_axis=0, tiled=True)
        outgoing, nearby = pl.pallas_call(
            pick_kernel,
            in_specs=[SMEM] + [ANY] * 10,
            out_specs=[HBM, HBM],
            out_shape=[
                jax.ShapeDtypeStruct((stretches, *blocks), jnp.bfloat16),
                jax.ShapeDtypeStruct((TOPN, *blocks), jnp.bfloat16),
            ],
            scratch_shapes=[
                pltpu.VMEM((per_row, *blocks), jnp.bfloat16),
                pltpu.SemaphoreType.DMA((stretches + TOPN,)),
            ],
            compiler_params=params(16),
            name="pick",
        )(meta, near[0], near[2], near[4], *far, near[1], near[3], near[5], *map(cross, far))
        incoming = lax.all_to_all(outgoing, "blk", split_axis=0, concat_axis=0, tiled=True)

        q_of = pltpu.VMEM(queries.shape, jnp.bfloat16)
        gw_of = pltpu.VMEM(gate_weight.shape, jnp.bfloat16)
        keys_of = pltpu.VMEM((2 * toks, HEAD_DIM), jnp.bfloat16)
        values_of = pltpu.VMEM((2 * toks, 2 * HEAD_DIM), jnp.bfloat16)
        flat = (toks, 2 * HEAD_DIM)
        local = pl.pallas_call(
            window_kernel,
            in_specs=[SMEM] + [HBM] * 2 + [ANY] * 4,
            out_specs=HBM,
            out_shape=f32_rows,
            scratch_shapes=[
                q_of,
                gw_of,
                pltpu.VMEM(queries.shape, jnp.float32),
                keys_of,
                values_of,
                pltpu.SemaphoreType.DMA((7,)),
            ],
            compiler_params=params(16),
            name="window",
        )(
            meta,
            queries,
            gate_weight,
            kv,
            s_own.reshape(flat),
            s_from1.reshape(flat),
            edge.reshape(flat),
        )

        column_comp = column_comp.reshape(depth, per_z, 2 * HEAD_DIM)
        comp_near, comp_far, local = spread(column_comp, local)

        def coarse_scratch(count):
            return [
                pltpu.VMEM((depth, count, per_z, HEAD_DIM), jnp.bfloat16),
                pltpu.VMEM((depth, count, per_z, 2 * HEAD_DIM), jnp.bfloat16),
            ]

        state = pl.pallas_call(
            near_kernel,
            in_specs=[SMEM] + [HBM] + [ANY] * 6,
            out_specs=VMEM,
            out_shape=jax.ShapeDtypeStruct((HEADS, toks, 3 * HEAD_DIM), jnp.float32),
            scratch_shapes=[q_of] + coarse_scratch(len(NEAR_SLOTS)) + [pltpu.SemaphoreType.DMA((13,))],
            compiler_params=params(20),
            name="near",
        )(meta, queries, *comp_near)
        comp_far, state = lax.optimization_barrier((comp_far, state))
        return pl.pallas_call(
            fine_kernel,
            in_specs=[SMEM] + [HBM] * 3 + [VMEM] + [HBM] * 5 + [ANY],
            out_specs=HBM,
            out_shape=jax.ShapeDtypeStruct(queries.shape, jnp.bfloat16),
            scratch_shapes=[q_of, gw_of, pltpu.VMEM(queries.shape, jnp.float32)]
            + coarse_scratch(len(FAR_SLOTS))
            + [
                keys_of,
                values_of,
                pltpu.VMEM(queries.shape, jnp.bfloat16),
                pltpu.SemaphoreType.DMA((3,)),
                pltpu.SemaphoreType.DMA((8,)),
                pltpu.SemaphoreType.DMA((2 * TOPN,)),
                pltpu.SemaphoreType.DMA((toks // ROWS,)),
            ],
            compiler_params=params(20),
            name="fine",
        )(
            meta,
            queries,
            gate_weight,
            hbm(local),
            state,
            *map(hbm, comp_far),
            *(hbm(cross(piece)) for piece in comp_far),
            hbm(nearby),
            incoming,
        )

    rows = P(AXES, None)
    return jax.shard_map(
        per_device,
        mesh=mesh,
        in_specs=(rows, rows, rows) + (P(),) * 7,
        out_specs=rows,
        check_vma=False,
    )
```

time: 127 us -> 86.5 us (0.68)
  the two profiles are of different devices: /device:TPU:225 before, /device:TPU:2 now
where the time goes in v2:
time: 86.5 us; the launch traced here: 86 us
  starting transfers between devices  34.9 us (40%)
  Pallas kernels  28.1 us (32%)
  waiting for transfers between devices  20.2 us (23%)
  local copies, waits for them, and re-layouts  1.82 us (2%)
    all_to_all x1, starting transfers between devices, per_device(): lax.all_to_all(copies, 'blk', split_axis=0, concat_axis=0, tiled=True)  11.3 us
    pallas_call x1, Pallas kernels, per_device(): pl.pallas_call(fine_kernel, in_specs=[SMEM] + [HBM] * 3 + [VMEM] + [HBM]...  9.92 us
    all_to_all x1, waiting for transfers between devices, per_device(): lax.all_to_all(outgoing, 'blk', split_axis=0, concat_axis=0, tiled=True)  7.62 us
    all_to_all x1, starting transfers between devices, per_device(): lax.all_to_all(outgoing, 'blk', split_axis=0, concat_axis=0, tiled=True)  5.95 us
    all_to_all x1, waiting for transfers between devices, per_device(): lax.all_to_all(copies, 'blk', split_axis=0, concat_axis=0, tiled=True)  5.77 us
    ppermute x2, starting transfers between devices, spread(): lax.ppermute(from3[half:], AXES, down)  5.67 us
    pallas_call x1, Pallas kernels, per_device(): pl.pallas_call(window_kernel, in_specs=[SMEM] + [HBM] * 2 + [ANY] * 4, ou...  4.93 us
    pallas_call x1, Pallas kernels, per_device(): pl.pallas_call(near_kernel, in_specs=[SMEM] + [HBM] + [ANY] * 6, out_spec...  4.35 us
  transfers between devices with their start and end apart: 21, of which 8 were waited for; matrix products, arithmetic and copies ran while one was open for 0% of the time, Pallas kernels for 19%

profile of v2, /device:TPU:2, one launch (start us, length us, event | category | flops | bytes accessed | tf_op | source)
XLA Modules:
  0.0 86.0 jit_solution(3688262649813256030)
XLA Ops:
  0.0 0.6 pad_add_fusion.ids
  0.6 1.8 %prep.1 = (bf16[512,256]{1,0:T(8,128)(2,1)S(1)}, s32[1,384]{1,0:T(1,128)S(1)}) custom-call(s32[2]{0:T(128)} %pad_add_fusion.ids, bf16[512,128]{1,0:T(8,128)(2,1)} %keys_ref.3, bf16[512,128]{1,0:T(8,128)(2,1)} %values_ref.3, s32[16,256]{1,0:T(8,128)} %bitcast.23), custom_call_target="tpu_custom_call" | custom-call | tf_op jit(solution)/shard_map/prep/pallas_call | solution.py:446
  2.4 0.0 copy-start.2
  2.4 1.7 %collective-permute-start = (bf16[8,64,256]{2,1,0:T(8,128)(2,1)S(1)}, bf16[8,64,256]{2,1,0:T(8,128)(2,1)S(1)}, u32[]{:S(2)}, u32[]{:S(2)}) collective-permute-start(bf16[8,64,256]{2,1,0:T(8,128)(2,1)S(1)} %bitcast.13), channel_id=1, source_target_pairs={{0,2},{1,3},{2,4},{3,5},{4,6},{5,7},{6,0},{7,1},{8,10},{9,11},{10,... | collective-permute-start | bytes 786440 | tf_op jit(solution)/shard_map/ppermute | solution.py:410
  4.0 1.7 %collective-permute-start.1 = (bf16[8,64,256]{2,1,0:T(8,128)(2,1)S(1)}, bf16[8,64,256]{2,1,0:T(8,128)(2,1)S(1)}, u32[]{:S(2)}, u32[]{:S(2)}) collective-permute-start(bf16[8,64,256]{2,1,0:T(8,128)(2,1)S(1)} %bitcast.14), channel_id=1, source_target_pairs={{0,6},{1,7},{2,0},{3,1},{4,2},{5,3},{6,4},{7,5},{8,14},{9,15},{10,... | collective-permute-start | bytes 786440 | tf_op jit(solution)/shard_map/ppermute | solution.py:411
  5.7 0.0 copy-done.2
  5.7 0.0 collective-permute-start.5
  5.7 1.3 %collective-permute-start.2 = (bf16[8,64,256]{2,1,0:T(8,128)(2,1)S(1)}, bf16[8,64,256]{2,1,0:T(8,128)(2,1)S(1)}, u32[]{:S(2)}, u32[]{:S(2)}) collective-permute-start(bf16[8,64,256]{2,1,0:T(8,128)(2,1)S(1)} %bitcast.16), channel_id=1, source_target_pairs={{7,8},{15,16},{23,24},{31,32},{39,40},{47,48},{55,56},{63,64},{71,... | collective-permute-start | bytes 786440 | tf_op jit(solution)/shard_map/ppermute | solution.py:481
  7.0 4.1 %compress.1 = bf16[32,16,256]{2,1,0:T(8,128)(2,1)} custom-call(bf16[512,128]{1,0:T(8,128)(2,1)} %keys_ref.3, bf16[512,128]{1,0:T(8,128)(2,1)} %values_ref.3, bf16[2,32,128]{2,1,0:T(8,128)(2,1)} %pos_ref.1, bf16[4096,256]{1,0:T(8,128)(2,1)} %k_in.1, bf16[256,128]{1,0:T(8,128)(2,1)} %k_out.1, bf16[4096,256]{1,0:T(8,128)(2,1)} %v_in.1, bf16[256,128]{1,0:T(8,128)(2,1)} %v_out.1), custom_call_target="tpu_custom_call" | custom-call | tf_op jit(solution)/shard_map/compress/pallas_call | solution.py:463
  11.1 0.7 collective-permute-done.refs_1_
  11.8 0.0 collective-permute-done.1.refs_2_
  11.8 0.0 collective-permute-start.6
  11.8 0.5 collective-permute-start.7
  12.4 1.7 %collective-permute-start.3 = (bf16[4,64,256]{2,1,0:T(8,128)(2,1)S(1)}, bf16[4,64,256]{2,1,0:T(8,128)(2,1)S(1)}, u32[]{:S(2)}, u32[]{:S(2)}) collective-permute-start(bf16[4,64,256]{2,1,0:T(8,128)(2,1)S(1)} %slice.12), channel_id=1, source_target_pairs={{0,2},{1,3},{2,4},{3,5},{4,6},{5,7},{6,0},{7,1},{8,10},{9,11},{10,... | collective-permute-start | bytes 393224 | tf_op jit(solution)/shard_map/ppermute | solution.py:414
  14.0 0.0 collective-permute-done.5.refs_5_
  14.0 2.4 %collective-permute-start.4 = (bf16[4,64,256]{2,1,0:T(8,128)(2,1)S(1)}, bf16[4,64,256]{2,1,0:T(8,128)(2,1)S(1)}, u32[]{:S(2)}, u32[]{:S(2)}) collective-permute-start(bf16[4,64,256]{2,1,0:T(8,128)(2,1)S(1)} %slice.13), channel_id=1, source_target_pairs={{0,6},{1,7},{2,0},{3,1},{4,2},{5,3},{6,4},{7,5},{8,14},{9,15},{10,... | collective-permute-start | bytes 393224 | tf_op jit(solution)/shard_map/ppermute | solution.py:414
  16.5 0.0 collective-permute-done.2
  16.5 4.0 %collective-permute-done.3.refs_3_ = bf16[4,64,256]{2,1,0:T(8,128)(2,1)S(1)} collective-permute-done((bf16[4,64,256]{2,1,0:T(8,128)(2,1)S(1)}, bf16[4,64,256]{2,1,0:T(8,128)(2,1)S(1)}, u32[]{:S(2)}, u32[]{:S(2)}) %collective-permute-start.3) | collective-permute-done | bytes 131104 | tf_op jit(solution)/shard_map/ppermute | solution.py:414
  20.4 0.0 collective-permute-done.4.refs_4_
  20.4 0.0 collective-permute-done.6.refs_6_
  20.4 0.0 collective-permute-done.7.refs_7_
  20.4 11.3 %all-to-all-start = ((bf16[32,16,256]{2,1,0:T(8,128)(2,1)}), bf16[32,16,256]{2,1,0:T(8,128)(2,1)S(1)}, u32[]{:S(2)}, u32[]{:S(2)}) async-start(bf16[32,16,256]{2,1,0:T(8,128)(2,1)} %compress.1), calls=%async_computation | async-start | bytes 524288 | tf_op jit(solution)/shard_map/all_to_all | solution.py:484
  31.8 0.1 collective-permute-start.17
  31.9 0.5 collective-permute-start.18
  32.4 0.8 collective-permute-done.17.refs_8_
  33.2 0.2 collective-permute-done.18.refs_9_
  33.4 3.0 %pick.1 = (bf16[32,64,256]{2,1,0:T(8,128)(2,1)}, bf16[16,64,256]{2,1,0:T(8,128)(2,1)S(1)}) custom-call(s32[1,384]{1,0:T(1,128)} %copy-done.2, bf16[8,64,256]{2,1,0:T(8,128)(2,1)S(1)} %bitcast.17, bf16[8,64,256]{2,1,0:T(8,128)(2,1)S(1)} %collective-permute-done.refs_1_, bf16[8,64,256]{2,1,0:T(8,128)(2,1)S(1)} %collective-permute-done.1.refs_2_, ...), custom_call_target="tpu_custom_call" | custom-call | tf_op jit(solution)/shard_map/pick/pallas_call | solution.py:485
  36.4 0.0 copy-start.1
  36.4 0.8 copy-done.1
  37.2 5.8 %all-to-all-done = bf16[32,16,256]{2,1,0:T(8,128)(2,1)S(1)} async-done(((bf16[32,16,256]{2,1,0:T(8,128)(2,1)}), bf16[32,16,256]{2,1,0:T(8,128)(2,1)S(1)}, u32[]{:S(2)}, u32[]{:S(2)}) %all-to-all-start) | async-done | bytes 262176 | tf_op jit(solution)/shard_map/all_to_all | solution.py:484
  43.0 6.0 %all-to-all-start.1 = ((bf16[32,64,256]{2,1,0:T(8,128)(2,1)}), bf16[32,64,256]{2,1,0:T(8,128)(2,1)}, u32[]{:S(2)}, u32[]{:S(2)}) async-start(bf16[32,64,256]{2,1,0:T(8,128)(2,1)} %get-tuple-element.34), calls=%async_computation.1 | async-start | bytes 2097152 | tf_op jit(solution)/shard_map/all_to_all | solution.py:500
  49.0 1.0 %collective-permute-start.8 = (bf16[8,64,256]{2,1,0:T(8,128)(2,1)S(1)}, bf16[8,64,256]{2,1,0:T(8,128)(2,1)S(1)}, u32[]{:S(2)}, u32[]{:S(2)}) collective-permute-start(bf16[8,64,256]{2,1,0:T(8,128)(2,1)S(1)} %bitcast.9), channel_id=1, source_target_pairs={{0,2},{1,3},{2,4},{3,5},{4,6},{5,7},{6,0},{7,1},{8,10},{9,11},{10,... | collective-permute-start | bytes 786440 | tf_op jit(solution)/shard_map/ppermute | solution.py:410
  50.0 2.3 %collective-permute-start.9 = (bf16[8,64,256]{2,1,0:T(8,128)(2,1)S(1)}, bf16[8,64,256]{2,1,0:T(8,128)(2,1)S(1)}, u32[]{:S(2)}, u32[]{:S(2)}) collective-permute-start(bf16[8,64,256]{2,1,0:T(8,128)(2,1)S(1)} %bitcast.10), channel_id=1, source_target_pairs={{0,6},{1,7},{2,0},{3,1},{4,2},{5,3},{6,4},{7,5},{8,14},{9,15},{10,... | collective-permute-start | bytes 786440 | tf_op jit(solution)/shard_map/ppermute | solution.py:411
  52.3 4.9 %window.1.part_in = f32[512,512]{1,0:T(8,128)S(1)} custom-call(s32[1,384]{1,0:T(1,128)} %copy-done.2, bf16[512,512]{1,0:T(8,128)(2,1)} %q_in.5, bf16[12,512]{1,0:T(8,128)(2,1)} %bitcast.21, bf16[512,256]{1,0:T(8,128)(2,1)S(1)} %get-tuple-element.21.kv_in, bf16[512,256]{1,0:T(8,128)(2,1)S(1)} %bitcast.18, bf16[512,256]{1,0:T(8,128)(2,1)S(1)} %bitcast.19, ...), custom_call_target="tpu_custom_call" | custom-call | tf_op jit(solution)/shard_map/window/pallas_call | solution.py:507
  57.2 0.0 copy-start
  57.2 1.0 %copy-done = f32[512,512]{1,0:T(8,128)} copy-done((f32[512,512]{1,0:T(8,128)}, f32[512,512]{1,0:T(8,128)S(1)}, u32[]{:S(2)}) %copy-start) | copy-done | bytes 1048600
  58.2 0.0 collective-permute-start.12
  58.2 0.0 collective-permute-done.8.from1
  58.2 0.0 collective-permute-done.9.from3
  58.2 0.5 collective-permute-start.13
  58.7 0.1 collective-permute-start.14
  58.8 0.1 collective-permute-start.10
  58.9 3.2 %collective-permute-start.11 = (bf16[4,64,256]{2,1,0:T(8,128)(2,1)S(1)}, bf16[4,64,256]{2,1,0:T(8,128)(2,1)S(1)}, u32[]{:S(2)}, u32[]{:S(2)}) collective-permute-start(bf16[4,64,256]{2,1,0:T(8,128)(2,1)S(1)} %slice.15), channel_id=1, source_target_pairs={{0,6},{1,7},{2,0},{3,1},{4,2},{5,3},{6,4},{7,5},{8,14},{9,15},{10,... | collective-permute-start | bytes 393224 | tf_op jit(solution)/shard_map/ppermute | solution.py:414
  62.1 0.0 collective-permute-done.12.s_own
  62.1 0.0 collective-permute-done.13.s_from1
  62.1 0.0 collective-permute-done.14.s_from3
  62.1 4.4 %near.1.state = f32[4,512,384]{2,1,0:T(8,128)S(1)} custom-call(s32[1,384]{1,0:T(1,128)} %copy-done.2, bf16[512,512]{1,0:T(8,128)(2,1)} %q_in.5, bf16[8,64,256]{2,1,0:T(8,128)(2,1)S(1)} %bitcast.12, bf16[8,64,256]{2,1,0:T(8,128)(2,1)S(1)} %collective-permute-done.12.s_own, bf16[8,64,256]{2,1,0:T(8,128)(2,1)S(1)} %collective-permute-done.8.from1, ...), custom_call_target="tpu_custom_call" | custom-call | tf_op jit(solution)/shard_map/near/pallas_call | solution.py:541
  66.5 0.0 collective-permute-done.10.a
  66.5 0.0 copy-start.3
  66.5 0.0 collective-permute-done.11.b
  66.5 0.0 copy-start.4
  66.5 0.1 collective-permute-start.15
  66.6 0.5 collective-permute-start.16
  67.1 0.8 collective-permute-done.15.s_a
  68.0 0.0 copy-done.4
  68.0 0.0 copy-start.5
  68.0 0.3 collective-permute-done.16.s_b
  68.3 0.0 copy-start.6
  68.3 7.6 %all-to-all-done.1.incoming = bf16[32,64,256]{2,1,0:T(8,128)(2,1)} async-done(((bf16[32,64,256]{2,1,0:T(8,128)(2,1)}), bf16[32,64,256]{2,1,0:T(8,128)(2,1)}, u32[]{:S(2)}, u32[]{:S(2)}) %all-to-all-start.1) | async-done | bytes 1048608 | tf_op jit(solution)/shard_map/all_to_all | solution.py:500
  75.9 0.0 copy-done.3
  75.9 0.0 copy-done.5
  75.9 0.0 copy-done.6
  75.9 9.9 %fine.1 = bf16[512,512]{1,0:T(8,128)(2,1)} custom-call(s32[1,384]{1,0:T(1,128)} %copy-done.2, bf16[512,512]{1,0:T(8,128)(2,1)} %q_in.5, bf16[12,512]{1,0:T(8,128)(2,1)} %bitcast.22, f32[512,512]{1,0:T(8,128)} %copy-done, f32[4,512,384]{2,1,0:T(8,128)S(1)} %near.1.state, bf16[4,64,256]{2,1,0:T(8,128)(2,1)} %copy-done.3, bf16[4,64,256]{2,1,0:T(8,128)(2,1)} %copy-done.4, ...), custom_call_target="tpu_custom_call" | custom-call | tf_op jit(solution)/shard_map/fine/pallas_call | solution.py:551
  (4 shorter events, 0.0 us)
Async XLA Ops:
  2.4 3.3 %copy-start.2 = (s32[1,384]{1,0:T(1,128)}, s32[1,384]{1,0:T(1,128)S(1)}, u32[]{:S(2)}) copy-start(s32[1,384]{1,0:T(1,128)S(1)} %get-tuple-element.20.meta) | copy-start | bytes 4612
  2.4 9.4 %collective-permute-start = (bf16[8,64,256]{2,1,0:T(8,128)(2,1)S(1)}, bf16[8,64,256]{2,1,0:T(8,128)(2,1)S(1)}, u32[]{:S(2)}, u32[]{:S(2)}) collective-permute-start(bf16[8,64,256]{2,1,0:T(8,128)(2,1)S(1)} %bitcast.13), channel_id=1, source_target_pairs={{0,2},{1,3},{2,4},{3,5},{4,6},{5,7},{6,0},{7,1},{8,10},{9,11},{10,... | collective-permute-start | bytes 786440 | tf_op jit(solution)/shard_map/ppermute | solution.py:410
  4.0 7.8 %collective-permute-start.1 = (bf16[8,64,256]{2,1,0:T(8,128)(2,1)S(1)}, bf16[8,64,256]{2,1,0:T(8,128)(2,1)S(1)}, u32[]{:S(2)}, u32[]{:S(2)}) collective-permute-start(bf16[8,64,256]{2,1,0:T(8,128)(2,1)S(1)} %bitcast.14), channel_id=1, source_target_pairs={{0,6},{1,7},{2,0},{3,1},{4,2},{5,3},{6,4},{7,5},{8,14},{9,15},{10,... | collective-permute-start | bytes 786440 | tf_op jit(solution)/shard_map/ppermute | solution.py:411
  5.7 8.3 %collective-permute-start.5 = (bf16[8,64,256]{2,1,0:T(8,128)(2,1)S(1)}, bf16[8,64,256]{2,1,0:T(8,128)(2,1)S(1)}, u32[]{:S(2)}, u32[]{:S(2)}) collective-permute-start(bf16[8,64,256]{2,1,0:T(8,128)(2,1)S(1)} %bitcast.15), channel_id=1, source_target_pairs={{0,1},{1,0},{2,3},{3,2},{4,5},{5,4},{6,7},{7,6},{8,9},{9,8},{10,11... | collective-permute-start | bytes 786440 | tf_op jit(solution)/shard_map/ppermute | solution.py:406
  5.7 10.8 %collective-permute-start.2 = (bf16[8,64,256]{2,1,0:T(8,128)(2,1)S(1)}, bf16[8,64,256]{2,1,0:T(8,128)(2,1)S(1)}, u32[]{:S(2)}, u32[]{:S(2)}) collective-permute-start(bf16[8,64,256]{2,1,0:T(8,128)(2,1)S(1)} %bitcast.16), channel_id=1, source_target_pairs={{7,8},{15,16},{23,24},{31,32},{39,40},{47,48},{55,56},{63,64},{71,... | collective-permute-start | bytes 786440 | tf_op jit(solution)/shard_map/ppermute | solution.py:481
  11.8 8.6 %collective-permute-start.6 = (bf16[8,64,256]{2,1,0:T(8,128)(2,1)S(1)}, bf16[8,64,256]{2,1,0:T(8,128)(2,1)S(1)}, u32[]{:S(2)}, u32[]{:S(2)}) collective-permute-start(bf16[8,64,256]{2,1,0:T(8,128)(2,1)S(1)} %collective-permute-done.refs_1_), channel_id=1, source_target_pairs={{0,1},{1,0},{2,3},{3,2},{4,5},{5,4},{6,7},{7,6},{8,9},{9,8},{10,11... | collective-permute-start | bytes 786440 | tf_op jit(solution)/shard_map/ppermute | solution.py:406
  11.8 8.6 %collective-permute-start.7 = (bf16[8,64,256]{2,1,0:T(8,128)(2,1)S(1)}, bf16[8,64,256]{2,1,0:T(8,128)(2,1)S(1)}, u32[]{:S(2)}, u32[]{:S(2)}) collective-permute-start(bf16[8,64,256]{2,1,0:T(8,128)(2,1)S(1)} %collective-permute-done.1.refs_2_), channel_id=1, source_target_pairs={{0,1},{1,0},{2,3},{3,2},{4,5},{5,4},{6,7},{7,6},{8,9},{9,8},{10,11... | collective-permute-start | bytes 786440 | tf_op jit(solution)/shard_map/ppermute | solution.py:406
  12.4 8.1 %collective-permute-start.3 = (bf16[4,64,256]{2,1,0:T(8,128)(2,1)S(1)}, bf16[4,64,256]{2,1,0:T(8,128)(2,1)S(1)}, u32[]{:S(2)}, u32[]{:S(2)}) collective-permute-start(bf16[4,64,256]{2,1,0:T(8,128)(2,1)S(1)} %slice.12), channel_id=1, source_target_pairs={{0,2},{1,3},{2,4},{3,5},{4,6},{5,7},{6,0},{7,1},{8,10},{9,11},{10,... | collective-permute-start | bytes 393224 | tf_op jit(solution)/shard_map/ppermute | solution.py:414
  14.0 6.4 %collective-permute-start.4 = (bf16[4,64,256]{2,1,0:T(8,128)(2,1)S(1)}, bf16[4,64,256]{2,1,0:T(8,128)(2,1)S(1)}, u32[]{:S(2)}, u32[]{:S(2)}) collective-permute-start(bf16[4,64,256]{2,1,0:T(8,128)(2,1)S(1)} %slice.13), channel_id=1, source_target_pairs={{0,6},{1,7},{2,0},{3,1},{4,2},{5,3},{6,4},{7,5},{8,14},{9,15},{10,... | collective-permute-start | bytes 393224 | tf_op jit(solution)/shard_map/ppermute | solution.py:414
  20.4 22.5 %all-to-all-start = ((bf16[32,16,256]{2,1,0:T(8,128)(2,1)}), bf16[32,16,256]{2,1,0:T(8,128)(2,1)S(1)}, u32[]{:S(2)}, u32[]{:S(2)}) async-start(bf16[32,16,256]{2,1,0:T(8,128)(2,1)} %compress.1), calls=%async_computation | async-start | bytes 524288 | tf_op jit(solution)/shard_map/all_to_all | solution.py:484
  31.8 1.4 %collective-permute-start.17 = (bf16[4,64,256]{2,1,0:T(8,128)(2,1)S(1)}, bf16[4,64,256]{2,1,0:T(8,128)(2,1)S(1)}, u32[]{:S(2)}, u32[]{:S(2)}) collective-permute-start(bf16[4,64,256]{2,1,0:T(8,128)(2,1)S(1)} %collective-permute-done.3.refs_3_), channel_id=1, source_target_pairs={{0,1},{1,0},{2,3},{3,2},{4,5},{5,4},{6,7},{7,6},{8,9},{9,8},{10,11... | collective-permute-start | bytes 393224 | tf_op jit(solution)/shard_map/ppermute | solution.py:406
  31.9 1.5 %collective-permute-start.18 = (bf16[4,64,256]{2,1,0:T(8,128)(2,1)S(1)}, bf16[4,64,256]{2,1,0:T(8,128)(2,1)S(1)}, u32[]{:S(2)}, u32[]{:S(2)}) collective-permute-start(bf16[4,64,256]{2,1,0:T(8,128)(2,1)S(1)} %collective-permute-done.4.refs_4_), channel_id=1, source_target_pairs={{0,1},{1,0},{2,3},{3,2},{4,5},{5,4},{6,7},{7,6},{8,9},{9,8},{10,11... | collective-permute-start | bytes 393224 | tf_op jit(solution)/shard_map/ppermute | solution.py:406
  36.4 0.8 copy-start.1
  43.0 32.9 %all-to-all-start.1 = ((bf16[32,64,256]{2,1,0:T(8,128)(2,1)}), bf16[32,64,256]{2,1,0:T(8,128)(2,1)}, u32[]{:S(2)}, u32[]{:S(2)}) async-start(bf16[32,64,256]{2,1,0:T(8,128)(2,1)} %get-tuple-element.34), calls=%async_computation.1 | async-start | bytes 2097152 | tf_op jit(solution)/shard_map/all_to_all | solution.py:500
  49.0 9.2 %collective-permute-start.8 = (bf16[8,64,256]{2,1,0:T(8,128)(2,1)S(1)}, bf16[8,64,256]{2,1,0:T(8,128)(2,1)S(1)}, u32[]{:S(2)}, u32[]{:S(2)}) collective-permute-start(bf16[8,64,256]{2,1,0:T(8,128)(2,1)S(1)} %bitcast.9), channel_id=1, source_target_pairs={{0,2},{1,3},{2,4},{3,5},{4,6},{5,7},{6,0},{7,1},{8,10},{9,11},{10,... | collective-permute-start | bytes 786440 | tf_op jit(solution)/shard_map/ppermute | solution.py:410
  50.0 8.2 %collective-permute-start.9 = (bf16[8,64,256]{2,1,0:T(8,128)(2,1)S(1)}, bf16[8,64,256]{2,1,0:T(8,128)(2,1)S(1)}, u32[]{:S(2)}, u32[]{:S(2)}) collective-permute-start(bf16[8,64,256]{2,1,0:T(8,128)(2,1)S(1)} %bitcast.10), channel_id=1, source_target_pairs={{0,6},{1,7},{2,0},{3,1},{4,2},{5,3},{6,4},{7,5},{8,14},{9,15},{10,... | collective-permute-start | bytes 786440 | tf_op jit(solution)/shard_map/ppermute | solution.py:411
  57.2 1.0 %copy-start = (f32[512,512]{1,0:T(8,128)}, f32[512,512]{1,0:T(8,128)S(1)}, u32[]{:S(2)}) copy-start(f32[512,512]{1,0:T(8,128)S(1)} %window.1.part_in) | copy-start | bytes 3145732
  58.2 4.0 %collective-permute-start.12 = (bf16[8,64,256]{2,1,0:T(8,128)(2,1)S(1)}, bf16[8,64,256]{2,1,0:T(8,128)(2,1)S(1)}, u32[]{:S(2)}, u32[]{:S(2)}) collective-permute-start(bf16[8,64,256]{2,1,0:T(8,128)(2,1)S(1)} %bitcast.11), channel_id=1, source_target_pairs={{0,1},{1,0},{2,3},{3,2},{4,5},{5,4},{6,7},{7,6},{8,9},{9,8},{10,11... | collective-permute-start | bytes 786440 | tf_op jit(solution)/shard_map/ppermute | solution.py:406
  58.2 4.0 %collective-permute-start.13 = (bf16[8,64,256]{2,1,0:T(8,128)(2,1)S(1)}, bf16[8,64,256]{2,1,0:T(8,128)(2,1)S(1)}, u32[]{:S(2)}, u32[]{:S(2)}) collective-permute-start(bf16[8,64,256]{2,1,0:T(8,128)(2,1)S(1)} %collective-permute-done.8.from1), channel_id=1, source_target_pairs={{0,1},{1,0},{2,3},{3,2},{4,5},{5,4},{6,7},{7,6},{8,9},{9,8},{10,11... | collective-permute-start | bytes 786440 | tf_op jit(solution)/shard_map/ppermute | solution.py:406
  58.7 3.4 %collective-permute-start.14 = (bf16[8,64,256]{2,1,0:T(8,128)(2,1)S(1)}, bf16[8,64,256]{2,1,0:T(8,128)(2,1)S(1)}, u32[]{:S(2)}, u32[]{:S(2)}) collective-permute-start(bf16[8,64,256]{2,1,0:T(8,128)(2,1)S(1)} %collective-permute-done.9.from3), channel_id=1, source_target_pairs={{0,1},{1,0},{2,3},{3,2},{4,5},{5,4},{6,7},{7,6},{8,9},{9,8},{10,11... | collective-permute-start | bytes 786440 | tf_op jit(solution)/shard_map/ppermute | solution.py:406
  58.8 7.7 %collective-permute-start.10 = (bf16[4,64,256]{2,1,0:T(8,128)(2,1)S(1)}, bf16[4,64,256]{2,1,0:T(8,128)(2,1)S(1)}, u32[]{:S(2)}, u32[]{:S(2)}) collective-permute-start(bf16[4,64,256]{2,1,0:T(8,128)(2,1)S(1)} %slice.14), channel_id=1, source_target_pairs={{0,2},{1,3},{2,4},{3,5},{4,6},{5,7},{6,0},{7,1},{8,10},{9,11},{10,... | collective-permute-start | bytes 393224 | tf_op jit(solution)/shard_map/ppermute | solution.py:414
  58.9 7.6 %collective-permute-start.11 = (bf16[4,64,256]{2,1,0:T(8,128)(2,1)S(1)}, bf16[4,64,256]{2,1,0:T(8,128)(2,1)S(1)}, u32[]{:S(2)}, u32[]{:S(2)}) collective-permute-start(bf16[4,64,256]{2,1,0:T(8,128)(2,1)S(1)} %slice.15), channel_id=1, source_target_pairs={{0,6},{1,7},{2,0},{3,1},{4,2},{5,3},{6,4},{7,5},{8,14},{9,15},{10,... | collective-permute-start | bytes 393224 | tf_op jit(solution)/shard_map/ppermute | solution.py:414
  66.5 9.4 %copy-start.3 = (bf16[4,64,256]{2,1,0:T(8,128)(2,1)}, bf16[4,64,256]{2,1,0:T(8,128)(2,1)S(1)}, u32[]{:S(2)}) copy-start(bf16[4,64,256]{2,1,0:T(8,128)(2,1)S(1)} %collective-permute-done.10.a) | copy-start | bytes 393220
  66.5 1.4 %copy-start.4 = (bf16[4,64,256]{2,1,0:T(8,128)(2,1)}, bf16[4,64,256]{2,1,0:T(8,128)(2,1)S(1)}, u32[]{:S(2)}) copy-start(bf16[4,64,256]{2,1,0:T(8,128)(2,1)S(1)} %collective-permute-done.11.b) | copy-start | bytes 393220
  66.5 1.4 %collective-permute-start.15 = (bf16[4,64,256]{2,1,0:T(8,128)(2,1)S(1)}, bf16[4,64,256]{2,1,0:T(8,128)(2,1)S(1)}, u32[]{:S(2)}, u32[]{:S(2)}) collective-permute-start(bf16[4,64,256]{2,1,0:T(8,128)(2,1)S(1)} %collective-permute-done.10.a), channel_id=1, source_target_pairs={{0,1},{1,0},{2,3},{3,2},{4,5},{5,4},{6,7},{7,6},{8,9},{9,8},{10,11... | collective-permute-start | bytes 393224 | tf_op jit(solution)/shard_map/ppermute | solution.py:406
  66.6 1.7 %collective-permute-start.16 = (bf16[4,64,256]{2,1,0:T(8,128)(2,1)S(1)}, bf16[4,64,256]{2,1,0:T(8,128)(2,1)S(1)}, u32[]{:S(2)}, u32[]{:S(2)}) collective-permute-start(bf16[4,64,256]{2,1,0:T(8,128)(2,1)S(1)} %collective-permute-done.11.b), channel_id=1, source_target_pairs={{0,1},{1,0},{2,3},{3,2},{4,5},{5,4},{6,7},{7,6},{8,9},{9,8},{10,11... | collective-permute-start | bytes 393224 | tf_op jit(solution)/shard_map/ppermute | solution.py:406
  68.0 7.9 %copy-start.5 = (bf16[4,64,256]{2,1,0:T(8,128)(2,1)}, bf16[4,64,256]{2,1,0:T(8,128)(2,1)S(1)}, u32[]{:S(2)}) copy-start(bf16[4,64,256]{2,1,0:T(8,128)(2,1)S(1)} %collective-permute-done.15.s_a) | copy-start | bytes 393220
  68.3 7.6 %copy-start.6 = (bf16[4,64,256]{2,1,0:T(8,128)(2,1)}, bf16[4,64,256]{2,1,0:T(8,128)(2,1)S(1)}, u32[]{:S(2)}) copy-start(bf16[4,64,256]{2,1,0:T(8,128)(2,1)S(1)} %collective-permute-done.16.s_b) | copy-start | bytes 393220

commit v3 on v2

--- a/solution.py
+++ b/solution.py
@@ -126,29 +126,9 @@
         out_ref[:, :, cols] = jnp.broadcast_to(comp[None], (out_ref.shape[0], count, HEAD_DIM))
 
 
-def piece_pairs(pieces, near, far):
-    pairs = []
-    for dc in range(2):
-        o, a, b, fa, fb = pieces[dc * 5 : dc * 5 + 5]
-        for dy, ref in ((0, o), (1, a), (3, b)):
-            pairs.append((ref, near(dy * 2 + dc)))
-        half = fa.shape[0]
-        pairs.append((fa, far(4 + dc, 0, half)))
-        pairs.append((fb, far(4 + dc, half, half)))
-    return pairs
-
-
 def pick_kernel(meta, *refs):
-    pieces = refs[:10]
-    out, nearby, rows, sem = refs[10:]
-    copy_all(
-        piece_pairs(
-            pieces,
-            lambda slot: rows.at[pl.ds(slot * 8, 8)],
-            lambda slot, at, n: rows.at[pl.ds(slot * 8 + at, n)],
-        ),
-        sem,
-    )
+    out, nearby, rows, sem = refs[8:]
+    copy_all([(ref, rows.at[pl.ds(i * 8, 8)]) for i, ref in enumerate(refs[:8])], sem)
     stretch, column, mine = unpack(meta)
     pairs = [(rows.at[meta[0, i * 8 + column]], out.at[i]) for i in range(out.shape[0])]
     for i in range(TOPN):
@@ -156,8 +136,8 @@
     copy_all(pairs, sem)
 
 
-def fill_ones(values):
-    values[:, HEAD_DIM:] = jnp.ones((values.shape[0], HEAD_DIM), values.dtype)
+def ones_beside(kv):
+    kv[..., 2 * HEAD_DIM :] = jnp.ones((*kv.shape[:-1], HEAD_DIM), kv.dtype)
 
 
 def attend(q, keys, values, seen):
@@ -171,37 +151,29 @@
 
 
 def window_kernel(
-    meta, q_in, gw_in, kv_in, s_own, s_from1, edge, out, q_ref, gw_ref, out_ref, keys, values, sem
+    meta, q_in, gw_in, kv_in, s_own, s_from1, edge, out, q_ref, gw_ref, out_ref, both, sem
 ):
-    loads = start_all([(q_in, q_ref), (gw_in, gw_ref)], sem.at[pl.ds(4, 2)])
+    toks = q_in.shape[0]
+    near, here = pl.ds(0, toks), pl.ds(toks, toks)
+    front = pl.ds(0, 2 * HEAD_DIM)
+    loads = start_all(
+        [(q_in, q_ref), (gw_in, gw_ref), (kv_in, both.at[here, front])], sem.at[pl.ds(2, 3)]
+    )
     stretch, column, _ = unpack(meta)
-    toks = q_in.shape[0]
-    heads = slice(0, HEAD_DIM)
-    tails = slice(HEAD_DIM, 2 * HEAD_DIM)
-
-    def fetch(ref, at, i):
-        copy_all(
-            [
-                (ref.at[:, heads], keys.at[pl.ds(at, toks)]),
-                (ref.at[:, tails], values.at[pl.ds(at, toks), heads]),
-            ],
-            sem.at[pl.ds(2 * i, 2)],
-        )
 
     @pl.when(column % 2 == 1)
     def _():
-        fetch(s_own, 0, 0)
+        copy_all([(s_own, both.at[near, front])], sem)
 
     @pl.when((column % 2 == 0) & (column > 0))
     def _():
-        fetch(s_from1, 0, 0)
+        copy_all([(s_from1, both.at[near, front])], sem)
 
     @pl.when(column == 0)
     def _():
-        fetch(edge, 0, 0)
-
-    fetch(kv_in, toks, 1)
-    fill_ones(values)
+        copy_all([(edge, both.at[near, front])], sem)
+
+    ones_beside(both)
     for load in loads:
         load.wait()
     low = jnp.where(stretch * 8 + column == 0, toks, 0)
@@ -214,14 +186,15 @@
         seen = (c > r) & (c <= r + WINDOW) & (c + first >= low)
         for h in range(HEADS):
             cols = slice(h * HEAD_DIM, (h + 1) * HEAD_DIM)
-            o, total = attend(q_ref[first : first + rows, cols], keys[span], values[span], seen)
+            o, total = attend(
+                q_ref[first : first + rows, cols], both[span, :HEAD_DIM], both[span, HEAD_DIM:], seen
+            )
             g = gates[first : first + rows, 2 * HEADS + h : 2 * HEADS + h + 1]
             out_ref[first : first + rows, cols] = o * (g / total)
-    copy_all([(out_ref, out)], sem.at[pl.ds(6, 1)])
-
-
-NEAR_SLOTS = ((0, 0), (0, 1), (1, 0), (1, 1), (3, 0), (3, 1))
-FAR_SLOTS = ((2, 0), (2, 1))
+    copy_all([(out_ref, out)], sem)
+
+
+SLOTS = ((0, 0), (0, 1), (1, 0), (1, 1), (2, 0), (2, 1), (3, 0), (3, 1))
 
 
 def coarse_ends(stretch_z, zs, slots, column):
@@ -238,16 +211,6 @@
     return (((blk << 3) + owner) * 16 + (lane & 15)) * CMP_BLOCK + (CMP_BLOCK - 1)
 
 
-def load_coarse(pairs, keys, values, sem):
-    copies = []
-    for ref, at in pairs:
-        copies.append((ref.at[:, :, :HEAD_DIM], keys.at[at]))
-        copies.append((ref.at[:, :, HEAD_DIM:], values.at[(*at, slice(None), slice(0, HEAD_DIM))]))
-    loads = start_all(copies, sem)
-    values[..., HEAD_DIM:] = jnp.ones((*values.shape[:3], HEAD_DIM), values.dtype)
-    return loads
-
-
 def fold(q, keys, values, seen, old):
     s = dot_t(q, keys)
     if seen is not None:
@@ -261,30 +224,33 @@
     return acc * factor + o[:, :HEAD_DIM], total * factor + o[:, HEAD_DIM:], top
 
 
-ROWS = 256
+ROWS = 128
+WIDE = 256
+STEP = 4
 PARTS = (slice(0, 128), slice(128, 256), slice(256, 384))
 
 
-def near_kernel(meta, q_in, own, s_own, from1, s_from1, from3, s_from3, state, q_ref, keys, values, sem):
-    q_load = pltpu.make_async_copy(q_in, q_ref, sem.at[12])
-    q_load.start()
+def coarse_kernel(meta, q_in, gw_in, local_in, *refs):
+    pieces = refs[: len(SLOTS)]
+    out_ref, q_ref, gw_ref, local, kv, state, sem = refs[len(SLOTS) :]
     stretch, column, _ = unpack(meta)
     toks = q_in.shape[0]
-    pieces = (own, s_own, from1, s_from1, from3, s_from3)
-    loads = load_coarse([(ref, (slice(None), i)) for i, ref in enumerate(pieces)], keys, values, sem)
+    pairs = [(ref, kv.at[:, i, :, pl.ds(0, 2 * HEAD_DIM)]) for i, ref in enumerate(pieces)]
+    loads = start_all([(q_in, q_ref), (gw_in, gw_ref), *pairs, (local_in, local)], sem)
+    ones_beside(kv)
     state[:, :, PARTS[0]] = jnp.zeros((HEADS, toks, 128), jnp.float32)
     state[:, :, PARTS[1]] = jnp.ones((HEADS, toks, 128), jnp.float32)
     state[:, :, PARTS[2]] = jnp.zeros((HEADS, toks, 128), jnp.float32)
-    for load in [q_load, *loads]:
+    for load in loads[:-1]:
         load.wait()
-    pair = stretch >> 3
-    chunk = 2 * len(NEAR_SLOTS) * 64
-    ends = coarse_ends(pair << 1, 2, NEAR_SLOTS, column)
+    last = stretch >> 4
+    chunk = STEP * len(SLOTS) * 64
+    ends = coarse_ends(last * STEP, STEP, SLOTS, column)
     base = (stretch * 8 + column) * toks
 
     def step(z, masked):
-        k = keys[pl.ds(2 * z, 2)].reshape(chunk, HEAD_DIM)
-        v = values[pl.ds(2 * z, 2)].reshape(chunk, 2 * HEAD_DIM)
+        both = kv[pl.ds(STEP * z, STEP)].reshape(chunk, 3 * HEAD_DIM)
+        k, v = both[:, :HEAD_DIM], both[:, HEAD_DIM:]
         for first in range(0, toks, ROWS):
             span = slice(first, first + ROWS)
             seen = None
@@ -300,44 +266,40 @@
         step(z, False)
         return carry
 
-    lax.fori_loop(0, pair, full, 0)
-    step(pair, True)
+    lax.fori_loop(0, last, full, 0)
+    step(last, True)
+    loads[-1].wait()
+    gates = gates_of(q_ref, gw_ref)
+    for h in range(HEADS):
+        cols = slice(h * HEAD_DIM, (h + 1) * HEAD_DIM)
+        acc, total = state[h, :, PARTS[0]], state[h, :, PARTS[1]]
+        out_ref[:, cols] = local[:, cols] + acc * (gates[:, h : h + 1] / total)
 
 
 def fine_kernel(
-    meta, q_in, gw_in, part_in, state, a, b, s_a, s_b, near_ref, incoming, *refs
+    meta, q_in, gw_in, part_ref, near_ref, incoming, *refs
 ):
-    out, q_ref, gw_ref, part_ref, c_keys, c_values, keys, values, done = refs[:9]
-    in_sem, c_sem, sem, out_sem = refs[9:]
+    out, q_ref, gw_ref, kv, done, in_sem, sem, out_sem = refs
     toks = q_in.shape[0]
-    first_loads = start_all([(q_in, q_ref), (gw_in, gw_ref), (part_in, part_ref)], in_sem)
+    loads = start_all([(q_in, q_ref), (gw_in, gw_ref)], in_sem)
     stretch, column, mine = unpack(meta)
     group = stretch * 8 + column
-    half = a.shape[0]
-    low, high = slice(0, half), slice(half, 2 * half)
-    pairs = [(a, (low, 0)), (b, (high, 0)), (s_a, (low, 1)), (s_b, (high, 1))]
-    loads = load_coarse(pairs, c_keys, c_values, c_sem)
 
     def fetch(i, run):
         owner = mine[i] >> 6
-        place = pl.ds(i * SEL_BLOCK, SEL_BLOCK)
-
-        def both(ref):
-            to = values.at[place, pl.ds(0, HEAD_DIM)]
-            run(pltpu.make_async_copy(ref.at[:, pl.ds(0, HEAD_DIM)], keys.at[place], sem.at[i]))
-            run(pltpu.make_async_copy(ref.at[:, pl.ds(HEAD_DIM, HEAD_DIM)], to, sem.at[TOPN + i]))
+        place = kv.at[pl.ds(i * SEL_BLOCK, SEL_BLOCK), pl.ds(0, 2 * HEAD_DIM)]
 
         @pl.when(owner != stretch)
         def _():
-            both(incoming.at[owner])
+            run(pltpu.make_async_copy(incoming.at[owner], place, sem.at[i]))
 
         @pl.when(owner == stretch)
         def _():
-            both(near_ref.at[i])
+            run(pltpu.make_async_copy(near_ref.at[i], place, sem.at[i]))
 
     for i in range(TOPN):
         fetch(i, lambda copy: copy.start())
-    fill_ones(values)
+    ones_beside(kv)
     lane = lax.broadcasted_iota(jnp.int32, (1, 2 * SEL_BLOCK), 1)
     pos = jnp.concatenate(
         [
@@ -350,33 +312,22 @@
         ],
         axis=1,
     )
-    for load in first_loads:
+    for load in loads:
         load.wait()
     gates = gates_of(q_ref, gw_ref)
-    chunk = 2 * half * len(FAR_SLOTS) * 64
-    ends = coarse_ends(0, 2 * half, FAR_SLOTS, column)
-    for load in loads:
-        load.wait()
     for i in range(TOPN):
         fetch(i, lambda copy: copy.wait())
-    c_k = c_keys[...].reshape(chunk, HEAD_DIM)
-    c_v = c_values[...].reshape(chunk, 2 * HEAD_DIM)
     writes = []
-    for first in range(0, toks, ROWS):
-        span = slice(first, first + ROWS)
-        base = group * toks + first
-        place = base + lax.broadcasted_iota(jnp.int32, (ROWS, keys.shape[0]), 0)
+    for first in range(0, toks, WIDE):
+        span = slice(first, first + WIDE)
+        place = group * toks + first + lax.broadcasted_iota(jnp.int32, (WIDE, kv.shape[0]), 0)
         seen = pos <= place
-        c_seen = ends <= place
         for h in range(HEADS):
             cols = slice(h * HEAD_DIM, (h + 1) * HEAD_DIM)
-            old = tuple(state[h, span, part] for part in PARTS)
-            acc, c_total, _ = fold(q_ref[span, cols], c_k, c_v, c_seen, old)
-            o, total = attend(q_ref[span, cols], keys[...], values[...], seen)
-            out_h = part_ref[span, cols] + acc * (gates[span, h : h + 1] / c_total)
-            out_h += o * (gates[span, HEADS + h : HEADS + h + 1] / total)
-            done[span, cols] = out_h.astype(done.dtype)
-        write = pltpu.make_async_copy(done.at[span], out.at[span], out_sem.at[first // ROWS])
+            o, total = attend(q_ref[span, cols], kv[:, :HEAD_DIM], kv[:, HEAD_DIM:], seen)
+            g = gates[span, HEADS + h : HEADS + h + 1]
+            done[span, cols] = (part_ref[span, cols] + o * (g / total)).astype(done.dtype)
+        write = pltpu.make_async_copy(done.at[span], out.at[span], out_sem.at[first // WIDE])
         write.start()
         writes.append(write)
     for write in writes:
@@ -399,21 +350,15 @@
     depth = 8
     up = route(stretches, ys, cores, lambda y, c: (y + 1, c))
     down = route(stretches, ys, cores, lambda y, c: (y - 1, c))
+    across = route(stretches, ys, cores, lambda y, c: (y + 2, c))
     swap = route(stretches, ys, cores, lambda y, c: (y, 1 - c))
     behind = [(i * group_size - 1, i * group_size) for i in range(1, stretches)]
 
     def cross(piece):
         return lax.ppermute(piece, AXES, swap)
 
-    def spread(piece, ahead):
-        half = piece.shape[0] // 2
-        from1 = lax.ppermute(piece, AXES, up)
-        from3 = lax.ppermute(piece, AXES, down)
-        crossed = cross(piece)
-        from1, from3, ahead = lax.optimization_barrier((from1, from3, ahead))
-        far = (lax.ppermute(from1[:half], AXES, up), lax.ppermute(from3[half:], AXES, down))
-        near = (piece, crossed, from1, cross(from1), from3, cross(from3))
-        return near, far, ahead
+    def spread(piece):
+        return [lax.ppermute(piece, AXES, path) for path in (up, down, across)]
 
     def per_device(
         queries, keys, values, selected, key_in, key_out, value_in, value_out, positions, gate_weight
@@ -477,14 +422,17 @@
             compiler_params=params(16),
             name="compress",
         )(keys, values, positions, key_in, key_out, value_in, value_out)
-        near, far, copies = spread(kv.reshape(per_dev, *blocks), copies)
-        edge = lax.ppermute(near[0], AXES, behind)
-        s_own, s_from1 = near[1], near[3]
-        copies, edge, _ = lax.optimization_barrier((copies, edge, (far, near[1], near[3], near[5])))
+        own = kv.reshape(per_dev, *blocks)
+        s_own = cross(own)
+        from1, from3, far = spread(own)
+        edge = lax.ppermute(own, AXES, behind)
+        copies, edge, s_own = lax.optimization_barrier((copies, edge, s_own))
         column_comp = lax.all_to_all(copies, "blk", split_axis=0, concat_axis=0, tiled=True)
+        s_from1, s_from3, s_far = cross(from1), cross(from3), cross(far)
+
         outgoing, nearby = pl.pallas_call(
             pick_kernel,
-            in_specs=[SMEM] + [ANY] * 10,
+            in_specs=[SMEM] + [ANY] * 8,
             out_specs=[HBM, HBM],
             out_shape=[
                 jax.ShapeDtypeStruct((stretches, *blocks), jnp.bfloat16),
@@ -496,13 +444,12 @@
             ],
             compiler_params=params(16),
             name="pick",
-        )(meta, near[0], near[2], near[4], *far, near[1], near[3], near[5], *map(cross, far))
+        )(meta, own, s_own, from1, s_from1, far, s_far, from3, s_from3)
         incoming = lax.all_to_all(outgoing, "blk", split_axis=0, concat_axis=0, tiled=True)
 
         q_of = pltpu.VMEM(queries.shape, jnp.bfloat16)
         gw_of = pltpu.VMEM(gate_weight.shape, jnp.bfloat16)
-        keys_of = pltpu.VMEM((2 * toks, HEAD_DIM), jnp.bfloat16)
-        values_of = pltpu.VMEM((2 * toks, 2 * HEAD_DIM), jnp.bfloat16)
+        kv_of = pltpu.VMEM((2 * toks, 3 * HEAD_DIM), jnp.bfloat16)
         flat = (toks, 2 * HEAD_DIM)
         local = pl.pallas_call(
             window_kernel,
@@ -513,9 +460,8 @@
                 q_of,
                 gw_of,
                 pltpu.VMEM(queries.shape, jnp.float32),
-                keys_of,
-                values_of,
-                pltpu.SemaphoreType.DMA((7,)),
+                kv_of,
+                pltpu.SemaphoreType.DMA((5,)),
             ],
             compiler_params=params(16),
             name="window",
@@ -529,54 +475,45 @@
             edge.reshape(flat),
         )
 
-        column_comp = column_comp.reshape(depth, per_z, 2 * HEAD_DIM)
-        comp_near, comp_far, local = spread(column_comp, local)
-
-        def coarse_scratch(count):
-            return [
-                pltpu.VMEM((depth, count, per_z, HEAD_DIM), jnp.bfloat16),
-                pltpu.VMEM((depth, count, per_z, 2 * HEAD_DIM), jnp.bfloat16),
-            ]
-
-        state = pl.pallas_call(
-            near_kernel,
-            in_specs=[SMEM] + [HBM] + [ANY] * 6,
+        own_comp = column_comp.reshape(depth, per_z, 2 * HEAD_DIM)
+        comp1, comp3, comp_far = spread(own_comp)
+        comp1, comp3, local = lax.optimization_barrier((comp1, comp3, local))
+        pieces = (own_comp, comp1, comp_far, comp3)
+
+        part = pl.pallas_call(
+            coarse_kernel,
+            in_specs=[SMEM] + [HBM] * 3 + [ANY] * 8,
             out_specs=VMEM,
-            out_shape=jax.ShapeDtypeStruct((HEADS, toks, 3 * HEAD_DIM), jnp.float32),
-            scratch_shapes=[q_of] + coarse_scratch(len(NEAR_SLOTS)) + [pltpu.SemaphoreType.DMA((13,))],
-            compiler_params=params(20),
-            name="near",
-        )(meta, queries, *comp_near)
-        comp_far, state = lax.optimization_barrier((comp_far, state))
+            out_shape=f32_rows,
+            scratch_shapes=[
+                q_of,
+                gw_of,
+                pltpu.VMEM(queries.shape, jnp.float32),
+                pltpu.VMEM((depth, group_size, per_z, 3 * HEAD_DIM), jnp.bfloat16),
+                pltpu.VMEM((HEADS, toks, 3 * HEAD_DIM), jnp.float32),
+                pltpu.SemaphoreType.DMA((11,)),
+            ],
+            compiler_params=params(24),
+            name="coarse",
+        )(meta, queries, gate_weight, hbm(local), *(x for piece in pieces for x in (piece, cross(piece))))
+
         return pl.pallas_call(
             fine_kernel,
-            in_specs=[SMEM] + [HBM] * 3 + [VMEM] + [HBM] * 5 + [ANY],
+            in_specs=[SMEM] + [HBM] * 2 + [VMEM, HBM, ANY],
             out_specs=HBM,
             out_shape=jax.ShapeDtypeStruct(queries.shape, jnp.bfloat16),
-            scratch_shapes=[q_of, gw_of, pltpu.VMEM(queries.shape, jnp.float32)]
-            + coarse_scratch(len(FAR_SLOTS))
-            + [
-                keys_of,
-                values_of,
+            scratch_shapes=[
+                q_of,
+                gw_of,
+                kv_of,
                 pltpu.VMEM(queries.shape, jnp.bfloat16),
-                pltpu.SemaphoreType.DMA((3,)),
-                pltpu.SemaphoreType.DMA((8,)),
-                pltpu.SemaphoreType.DMA((2 * TOPN,)),
-                pltpu.SemaphoreType.DMA((toks // ROWS,)),
+                pltpu.SemaphoreType.DMA((2,)),
+                pltpu.SemaphoreType.DMA((TOPN,)),
+                pltpu.SemaphoreType.DMA((toks // WIDE,)),
             ],
             compiler_params=params(20),
             name="fine",
-        )(
-            meta,
-            queries,
-            gate_weight,
-            hbm(local),
-            state,
-            *map(hbm, comp_far),
-            *(hbm(cross(piece)) for piece in comp_far),
-            hbm(nearby),
-            incoming,
-        )
+        )(meta, queries, gate_weight, part, hbm(nearby), incoming)
 
     rows = P(AXES, None)
     return jax.shard_map(

time: 86.5 us -> 78.5 us (0.908)
  the two profiles are of different devices: /device:TPU:2 before, /device:TPU:129 now
where the time goes in v3:
time: 78.5 us; the launch traced here: 78 us
  starting transfers between devices  36.4 us (46%)
  Pallas kernels  34.5 us (44%)
  waiting for transfers between devices  4.43 us (6%)
  local copies, waits for them, and re-layouts  1.74 us (2%)
    pallas_call x1, Pallas kernels, per_device(): pl.pallas_call(coarse_kernel, in_specs=[SMEM] + [HBM] * 3 + [ANY] * 8, ou...  15.1 us
    ppermute x8, starting transfers between devices, cross(): return lax.ppermute(piece, AXES, swap)  9.66 us
    ppermute x6, starting transfers between devices, spread(): return [lax.ppermute(piece, AXES, path) for path in (up, down, across)]  9.09 us
    all_to_all x1, starting transfers between devices, per_device(): lax.all_to_all(copies, 'blk', split_axis=0, concat_axis=0, tiled=True)  8.99 us
    all_to_all x1, starting transfers between devices, per_device(): lax.all_to_all(outgoing, 'blk', split_axis=0, concat_axis=0, tiled=True)  8.03 us
    pallas_call x1, Pallas kernels, per_device(): pl.pallas_call(fine_kernel, in_specs=[SMEM] + [HBM] * 2 + [VMEM, HBM, ANY...  6.22 us
    pallas_call x1, Pallas kernels, per_device(): pl.pallas_call(window_kernel, in_specs=[SMEM] + [HBM] * 2 + [ANY] * 4, ou...  4.91 us
    pallas_call x1, Pallas kernels, per_device(): pl.pallas_call(compress_kernel, in_specs=[HBM] * 7, out_specs=VMEM, out_s...  4.12 us
  transfers between devices with their start and end apart: 17, of which 8 were waited for; matrix products, arithmetic and copies ran while one was open for 0% of the time, Pallas kernels for 34%

profile of v3, /device:TPU:129, one launch (start us, length us, event | category | flops | bytes accessed | tf_op | source)
XLA Modules:
  0.0 78.0 jit_solution(10749875754160574806)
XLA Ops:
  0.0 0.6 pad_add_fusion.ids
  0.6 1.8 %prep.1 = (bf16[512,256]{1,0:T(8,128)(2,1)S(1)}, s32[1,384]{1,0:T(1,128)S(1)}) custom-call(s32[2]{0:T(128)} %pad_add_fusion.ids, bf16[512,128]{1,0:T(8,128)(2,1)} %keys_ref.3, bf16[512,128]{1,0:T(8,128)(2,1)} %values_ref.3, s32[16,256]{1,0:T(8,128)} %bitcast.26), custom_call_target="tpu_custom_call" | custom-call | tf_op jit(solution)/shard_map/prep/pallas_call | solution.py:391
  2.4 0.0 copy-start.2
  2.4 0.7 collective-permute-start
  3.1 1.4 %collective-permute-start.1 = (bf16[8,64,256]{2,1,0:T(8,128)(2,1)S(1)}, bf16[8,64,256]{2,1,0:T(8,128)(2,1)S(1)}, u32[]{:S(2)}, u32[]{:S(2)}) collective-permute-start(bf16[8,64,256]{2,1,0:T(8,128)(2,1)S(1)} %bitcast.15), channel_id=1, source_target_pairs={{0,1},{1,0},{2,3},{3,2},{4,5},{5,4},{6,7},{7,6},{8,9},{9,8},{10,11... | collective-permute-start | bytes 786440 | tf_op jit(solution)/shard_map/ppermute | solution.py:358
  4.5 0.7 collective-permute-start.4
  5.2 0.0 copy-done.2
  5.2 4.7 %collective-permute-start.11 = (bf16[8,64,256]{2,1,0:T(8,128)(2,1)S(1)}, bf16[8,64,256]{2,1,0:T(8,128)(2,1)S(1)}, u32[]{:S(2)}, u32[]{:S(2)}) collective-permute-start(bf16[8,64,256]{2,1,0:T(8,128)(2,1)S(1)} %bitcast.17), channel_id=1, source_target_pairs={{0,4},{1,5},{2,6},{3,7},{4,0},{5,1},{6,2},{7,3},{8,12},{9,13},{10,... | collective-permute-start | bytes 786440 | tf_op jit(solution)/shard_map/ppermute | solution.py:361
  9.9 0.0 collective-permute-start.13
  9.9 4.1 %compress.1 = bf16[32,16,256]{2,1,0:T(8,128)(2,1)} custom-call(bf16[512,128]{1,0:T(8,128)(2,1)} %keys_ref.3, bf16[512,128]{1,0:T(8,128)(2,1)} %values_ref.3, bf16[2,32,128]{2,1,0:T(8,128)(2,1)} %pos_ref.1, bf16[4096,256]{1,0:T(8,128)(2,1)} %k_in.1, bf16[256,128]{1,0:T(8,128)(2,1)} %k_out.1, bf16[4096,256]{1,0:T(8,128)(2,1)} %v_in.1, bf16[256,128]{1,0:T(8,128)(2,1)} %v_out.1), custom_call_target="tpu_custom_call" | custom-call | tf_op jit(solution)/shard_map/compress/pallas_call | solution.py:408
  14.0 0.0 collective-permute-done
  14.0 0.0 collective-permute-done.1.refs_1_
  14.0 9.0 %all-to-all-start = ((bf16[32,16,256]{2,1,0:T(8,128)(2,1)}), bf16[32,16,256]{2,1,0:T(8,128)(2,1)S(1)}, u32[]{:S(2)}, u32[]{:S(2)}) async-start(bf16[32,16,256]{2,1,0:T(8,128)(2,1)} %compress.1), calls=%async_computation | async-start | bytes 524288 | tf_op jit(solution)/shard_map/all_to_all | solution.py:430
  23.0 0.4 collective-permute-done.4.refs_2_
  23.4 1.2 %collective-permute-start.5 = (bf16[8,64,256]{2,1,0:T(8,128)(2,1)S(1)}, bf16[8,64,256]{2,1,0:T(8,128)(2,1)S(1)}, u32[]{:S(2)}, u32[]{:S(2)}) collective-permute-start(bf16[8,64,256]{2,1,0:T(8,128)(2,1)S(1)} %collective-permute-done.4.refs_2_), channel_id=1, source_target_pairs={{0,1},{1,0},{2,3},{3,2},{4,5},{5,4},{6,7},{7,6},{8,9},{9,8},{10,11... | collective-permute-start | bytes 786440 | tf_op jit(solution)/shard_map/ppermute | solution.py:358
  24.7 0.0 collective-permute-done.11.refs_4_
  24.7 0.1 collective-permute-start.12
  24.8 0.0 collective-permute-done.13.refs_6_
  24.8 0.4 collective-permute-start.14
  25.2 0.6 collective-permute-done.5.refs_3_
  25.8 0.4 collective-permute-done.12.refs_5_
  26.2 0.4 collective-permute-done.14.refs_7_
  26.6 2.4 %pick.1 = (bf16[32,64,256]{2,1,0:T(8,128)(2,1)}, bf16[16,64,256]{2,1,0:T(8,128)(2,1)S(1)}) custom-call(s32[1,384]{1,0:T(1,128)} %copy-done.2, bf16[8,64,256]{2,1,0:T(8,128)(2,1)S(1)} %bitcast.19, bf16[8,64,256]{2,1,0:T(8,128)(2,1)S(1)} %collective-permute-done.1.refs_1_, bf16[8,64,256]{2,1,0:T(8,128)(2,1)S(1)} %collective-permute-done.4.refs_2_, ...), custom_call_target="tpu_custom_call" | custom-call | tf_op jit(solution)/shard_map/pick/pallas_call | solution.py:433
  28.9 0.0 copy-start.1
  28.9 0.8 copy-done.1
  29.7 1.2 %all-to-all-done = bf16[32,16,256]{2,1,0:T(8,128)(2,1)S(1)} async-done(((bf16[32,16,256]{2,1,0:T(8,128)(2,1)}), bf16[32,16,256]{2,1,0:T(8,128)(2,1)S(1)}, u32[]{:S(2)}, u32[]{:S(2)}) %all-to-all-start) | async-done | bytes 262176 | tf_op jit(solution)/shard_map/all_to_all | solution.py:430
  30.9 8.0 %all-to-all-start.1 = ((bf16[32,64,256]{2,1,0:T(8,128)(2,1)}), bf16[32,64,256]{2,1,0:T(8,128)(2,1)S(1)}, u32[]{:S(2)}, u32[]{:S(2)}) async-start(bf16[32,64,256]{2,1,0:T(8,128)(2,1)} %get-tuple-element.24), calls=%async_computation.1 | async-start | bytes 2097152 | tf_op jit(solution)/shard_map/all_to_all | solution.py:448
  38.9 1.8 %collective-permute-start.2 = (bf16[8,64,256]{2,1,0:T(8,128)(2,1)S(1)}, bf16[8,64,256]{2,1,0:T(8,128)(2,1)S(1)}, u32[]{:S(2)}, u32[]{:S(2)}) collective-permute-start(bf16[8,64,256]{2,1,0:T(8,128)(2,1)S(1)} %bitcast.9), channel_id=1, source_target_pairs={{0,2},{1,3},{2,4},{3,5},{4,6},{5,7},{6,0},{7,1},{8,10},{9,11},{10,... | collective-permute-start | bytes 786440 | tf_op jit(solution)/shard_map/ppermute | solution.py:361
  40.8 0.9 %collective-permute-start.3 = (bf16[8,64,256]{2,1,0:T(8,128)(2,1)S(1)}, bf16[8,64,256]{2,1,0:T(8,128)(2,1)S(1)}, u32[]{:S(2)}, u32[]{:S(2)}) collective-permute-start(bf16[8,64,256]{2,1,0:T(8,128)(2,1)S(1)} %bitcast.10), channel_id=1, source_target_pairs={{0,6},{1,7},{2,0},{3,1},{4,2},{5,3},{6,4},{7,5},{8,14},{9,15},{10,... | collective-permute-start | bytes 786440 | tf_op jit(solution)/shard_map/ppermute | solution.py:361
  41.7 0.9 %collective-permute-start.8 = (bf16[8,64,256]{2,1,0:T(8,128)(2,1)S(1)}, bf16[8,64,256]{2,1,0:T(8,128)(2,1)S(1)}, u32[]{:S(2)}, u32[]{:S(2)}) collective-permute-start(bf16[8,64,256]{2,1,0:T(8,128)(2,1)S(1)} %bitcast.11), channel_id=1, source_target_pairs={{0,4},{1,5},{2,6},{3,7},{4,0},{5,1},{6,2},{7,3},{8,12},{9,13},{10,... | collective-permute-start | bytes 786440 | tf_op jit(solution)/shard_map/ppermute | solution.py:361
  42.6 4.9 %window.1.local_in = f32[512,512]{1,0:T(8,128)S(1)} custom-call(s32[1,384]{1,0:T(1,128)} %copy-done.2, bf16[512,512]{1,0:T(8,128)(2,1)} %q_in.5, bf16[12,512]{1,0:T(8,128)(2,1)} %bitcast.23, bf16[512,256]{1,0:T(8,128)(2,1)S(1)} %get-tuple-element.16.kv_in, bf16[512,256]{1,0:T(8,128)(2,1)S(1)} %bitcast.20, bf16[512,256]{1,0:T(8,128)(2,1)S(1)} %bitcast.21, ...), custom_call_target="tpu_custom_call" | custom-call | tf_op jit(solution)/shard_map/window/pallas_call | solution.py:454
  47.6 0.0 copy-start
  47.6 1.0 %copy-done = f32[512,512]{1,0:T(8,128)} copy-done((f32[512,512]{1,0:T(8,128)}, f32[512,512]{1,0:T(8,128)S(1)}, u32[]{:S(2)}) %copy-start) | copy-done | bytes 1048600
  48.5 2.4 %collective-permute-start.6 = (bf16[8,64,256]{2,1,0:T(8,128)(2,1)S(1)}, bf16[8,64,256]{2,1,0:T(8,128)(2,1)S(1)}, u32[]{:S(2)}, u32[]{:S(2)}) collective-permute-start(bf16[8,64,256]{2,1,0:T(8,128)(2,1)S(1)} %bitcast.12), channel_id=1, source_target_pairs={{0,1},{1,0},{2,3},{3,2},{4,5},{5,4},{6,7},{7,6},{8,9},{9,8},{10,11... | collective-permute-start | bytes 786440 | tf_op jit(solution)/shard_map/ppermute | solution.py:358
  51.0 0.0 collective-permute-done.2.refs_2_
  51.0 0.0 collective-permute-done.3.refs_6_
  51.0 3.6 %collective-permute-start.7 = (bf16[8,64,256]{2,1,0:T(8,128)(2,1)S(1)}, bf16[8,64,256]{2,1,0:T(8,128)(2,1)S(1)}, u32[]{:S(2)}, u32[]{:S(2)}) collective-permute-start(bf16[8,64,256]{2,1,0:T(8,128)(2,1)S(1)} %collective-permute-done.2.refs_2_), channel_id=1, source_target_pairs={{0,1},{1,0},{2,3},{3,2},{4,5},{5,4},{6,7},{7,6},{8,9},{9,8},{10,11... | collective-permute-start | bytes 786440 | tf_op jit(solution)/shard_map/ppermute | solution.py:358
  54.6 0.0 collective-permute-done.8.refs_4_
  54.6 0.1 collective-permute-start.9
  54.7 0.4 collective-permute-start.10
  55.1 0.0 collective-permute-done.6.refs_1_
  55.1 0.6 collective-permute-done.7.refs_3_
  55.7 0.4 collective-permute-done.9.refs_5_
  56.1 0.4 collective-permute-done.10.refs_7_
  56.5 15.1 %coarse.1.part_ref = f32[512,512]{1,0:T(8,128)S(1)} custom-call(s32[1,384]{1,0:T(1,128)} %copy-done.2, bf16[512,512]{1,0:T(8,128)(2,1)} %q_in.5, bf16[12,512]{1,0:T(8,128)(2,1)} %bitcast.24, f32[512,512]{1,0:T(8,128)} %copy-done, bf16[8,64,256]{2,1,0:T(8,128)(2,1)S(1)} %bitcast.13, bf16[8,64,256]{2,1,0:T(8,128)(2,1)S(1)} %collective-permute-done.6.refs_1_, ...), custom_call_target="tpu_custom_call" | custom-call | tf_op jit(solution)/shard_map/coarse/pallas_call | solution.py:483
  71.6 0.0 all-to-all-done.1.incoming
  71.6 6.2 %fine.1 = bf16[512,512]{1,0:T(8,128)(2,1)} custom-call(s32[1,384]{1,0:T(1,128)} %copy-done.2, bf16[512,512]{1,0:T(8,128)(2,1)} %q_in.5, bf16[12,512]{1,0:T(8,128)(2,1)} %bitcast.25, f32[512,512]{1,0:T(8,128)S(1)} %coarse.1.part_ref, bf16[16,64,256]{2,1,0:T(8,128)(2,1)} %copy-done.1, bf16[32,64,256]{2,1,0:T(8,128)(2,1)S(1)} %all-to-all-done.1.incoming), custom_call_target="tpu_custom_call" | custom-call | tf_op jit(solution)/shard_map/fine/pallas_call | solution.py:500
Async XLA Ops:
  2.4 2.8 %copy-start.2 = (s32[1,384]{1,0:T(1,128)}, s32[1,384]{1,0:T(1,128)S(1)}, u32[]{:S(2)}) copy-start(s32[1,384]{1,0:T(1,128)S(1)} %get-tuple-element.15.meta) | copy-start | bytes 4612
  2.4 11.6 %collective-permute-start = (bf16[8,64,256]{2,1,0:T(8,128)(2,1)S(1)}, bf16[8,64,256]{2,1,0:T(8,128)(2,1)S(1)}, u32[]{:S(2)}, u32[]{:S(2)}) collective-permute-start(bf16[8,64,256]{2,1,0:T(8,128)(2,1)S(1)} %bitcast.14), channel_id=1, source_target_pairs={{7,8},{15,16},{23,24},{31,32},{39,40},{47,48},{55,56},{63,64},{71,... | collective-permute-start | bytes 786440 | tf_op jit(solution)/shard_map/ppermute | solution.py:428
  3.1 10.9 %collective-permute-start.1 = (bf16[8,64,256]{2,1,0:T(8,128)(2,1)S(1)}, bf16[8,64,256]{2,1,0:T(8,128)(2,1)S(1)}, u32[]{:S(2)}, u32[]{:S(2)}) collective-permute-start(bf16[8,64,256]{2,1,0:T(8,128)(2,1)S(1)} %bitcast.15), channel_id=1, source_target_pairs={{0,1},{1,0},{2,3},{3,2},{4,5},{5,4},{6,7},{7,6},{8,9},{9,8},{10,11... | collective-permute-start | bytes 786440 | tf_op jit(solution)/shard_map/ppermute | solution.py:358
  4.5 19.0 %collective-permute-start.4 = (bf16[8,64,256]{2,1,0:T(8,128)(2,1)S(1)}, bf16[8,64,256]{2,1,0:T(8,128)(2,1)S(1)}, u32[]{:S(2)}, u32[]{:S(2)}) collective-permute-start(bf16[8,64,256]{2,1,0:T(8,128)(2,1)S(1)} %bitcast.16), channel_id=1, source_target_pairs={{0,2},{1,3},{2,4},{3,5},{4,6},{5,7},{6,0},{7,1},{8,10},{9,11},{10,... | collective-permute-start | bytes 786440 | tf_op jit(solution)/shard_map/ppermute | solution.py:361
  5.2 19.5 %collective-permute-start.11 = (bf16[8,64,256]{2,1,0:T(8,128)(2,1)S(1)}, bf16[8,64,256]{2,1,0:T(8,128)(2,1)S(1)}, u32[]{:S(2)}, u32[]{:S(2)}) collective-permute-start(bf16[8,64,256]{2,1,0:T(8,128)(2,1)S(1)} %bitcast.17), channel_id=1, source_target_pairs={{0,4},{1,5},{2,6},{3,7},{4,0},{5,1},{6,2},{7,3},{8,12},{9,13},{10,... | collective-permute-start | bytes 786440 | tf_op jit(solution)/shard_map/ppermute | solution.py:361
  9.9 14.9 %collective-permute-start.13 = (bf16[8,64,256]{2,1,0:T(8,128)(2,1)S(1)}, bf16[8,64,256]{2,1,0:T(8,128)(2,1)S(1)}, u32[]{:S(2)}, u32[]{:S(2)}) collective-permute-start(bf16[8,64,256]{2,1,0:T(8,128)(2,1)S(1)} %bitcast.18), channel_id=1, source_target_pairs={{0,6},{1,7},{2,0},{3,1},{4,2},{5,3},{6,4},{7,5},{8,14},{9,15},{10,... | collective-permute-start | bytes 786440 | tf_op jit(solution)/shard_map/ppermute | solution.py:361
  14.0 16.9 %all-to-all-start = ((bf16[32,16,256]{2,1,0:T(8,128)(2,1)}), bf16[32,16,256]{2,1,0:T(8,128)(2,1)S(1)}, u32[]{:S(2)}, u32[]{:S(2)}) async-start(bf16[32,16,256]{2,1,0:T(8,128)(2,1)} %compress.1), calls=%async_computation | async-start | bytes 524288 | tf_op jit(solution)/shard_map/all_to_all | solution.py:430
  23.4 2.4 %collective-permute-start.5 = (bf16[8,64,256]{2,1,0:T(8,128)(2,1)S(1)}, bf16[8,64,256]{2,1,0:T(8,128)(2,1)S(1)}, u32[]{:S(2)}, u32[]{:S(2)}) collective-permute-start(bf16[8,64,256]{2,1,0:T(8,128)(2,1)S(1)} %collective-permute-done.4.refs_2_), channel_id=1, source_target_pairs={{0,1},{1,0},{2,3},{3,2},{4,5},{5,4},{6,7},{7,6},{8,9},{9,8},{10,11... | collective-permute-start | bytes 786440 | tf_op jit(solution)/shard_map/ppermute | solution.py:358
  24.7 1.5 %collective-permute-start.12 = (bf16[8,64,256]{2,1,0:T(8,128)(2,1)S(1)}, bf16[8,64,256]{2,1,0:T(8,128)(2,1)S(1)}, u32[]{:S(2)}, u32[]{:S(2)}) collective-permute-start(bf16[8,64,256]{2,1,0:T(8,128)(2,1)S(1)} %collective-permute-done.11.refs_4_), channel_id=1, source_target_pairs={{0,1},{1,0},{2,3},{3,2},{4,5},{5,4},{6,7},{7,6},{8,9},{9,8},{10,11... | collective-permute-start | bytes 786440 | tf_op jit(solution)/shard_map/ppermute | solution.py:358
  24.8 1.8 %collective-permute-start.14 = (bf16[8,64,256]{2,1,0:T(8,128)(2,1)S(1)}, bf16[8,64,256]{2,1,0:T(8,128)(2,1)S(1)}, u32[]{:S(2)}, u32[]{:S(2)}) collective-permute-start(bf16[8,64,256]{2,1,0:T(8,128)(2,1)S(1)} %collective-permute-done.13.refs_6_), channel_id=1, source_target_pairs={{0,1},{1,0},{2,3},{3,2},{4,5},{5,4},{6,7},{7,6},{8,9},{9,8},{10,11... | collective-permute-start | bytes 786440 | tf_op jit(solution)/shard_map/ppermute | solution.py:358
  28.9 0.8 %copy-start.1 = (bf16[16,64,256]{2,1,0:T(8,128)(2,1)}, bf16[16,64,256]{2,1,0:T(8,128)(2,1)S(1)}, u32[]{:S(2)}) copy-start(bf16[16,64,256]{2,1,0:T(8,128)(2,1)S(1)} %get-tuple-element.23.near_ref) | copy-start | bytes 1572868
  30.9 40.7 %all-to-all-start.1 = ((bf16[32,64,256]{2,1,0:T(8,128)(2,1)}), bf16[32,64,256]{2,1,0:T(8,128)(2,1)S(1)}, u32[]{:S(2)}, u32[]{:S(2)}) async-start(bf16[32,64,256]{2,1,0:T(8,128)(2,1)} %get-tuple-element.24), calls=%async_computation.1 | async-start | bytes 2097152 | tf_op jit(solution)/shard_map/all_to_all | solution.py:448
  38.9 12.0 %collective-permute-start.2 = (bf16[8,64,256]{2,1,0:T(8,128)(2,1)S(1)}, bf16[8,64,256]{2,1,0:T(8,128)(2,1)S(1)}, u32[]{:S(2)}, u32[]{:S(2)}) collective-permute-start(bf16[8,64,256]{2,1,0:T(8,128)(2,1)S(1)} %bitcast.9), channel_id=1, source_target_pairs={{0,2},{1,3},{2,4},{3,5},{4,6},{5,7},{6,0},{7,1},{8,10},{9,11},{10,... | collective-permute-start | bytes 786440 | tf_op jit(solution)/shard_map/ppermute | solution.py:361
  40.8 10.2 %collective-permute-start.3 = (bf16[8,64,256]{2,1,0:T(8,128)(2,1)S(1)}, bf16[8,64,256]{2,1,0:T(8,128)(2,1)S(1)}, u32[]{:S(2)}, u32[]{:S(2)}) collective-permute-start(bf16[8,64,256]{2,1,0:T(8,128)(2,1)S(1)} %bitcast.10), channel_id=1, source_target_pairs={{0,6},{1,7},{2,0},{3,1},{4,2},{5,3},{6,4},{7,5},{8,14},{9,15},{10,... | collective-permute-start | bytes 786440 | tf_op jit(solution)/shard_map/ppermute | solution.py:361
  41.7 12.9 %collective-permute-start.8 = (bf16[8,64,256]{2,1,0:T(8,128)(2,1)S(1)}, bf16[8,64,256]{2,1,0:T(8,128)(2,1)S(1)}, u32[]{:S(2)}, u32[]{:S(2)}) collective-permute-start(bf16[8,64,256]{2,1,0:T(8,128)(2,1)S(1)} %bitcast.11), channel_id=1, source_target_pairs={{0,4},{1,5},{2,6},{3,7},{4,0},{5,1},{6,2},{7,3},{8,12},{9,13},{10,... | collective-permute-start | bytes 786440 | tf_op jit(solution)/shard_map/ppermute | solution.py:361
  47.6 1.0 %copy-start = (f32[512,512]{1,0:T(8,128)}, f32[512,512]{1,0:T(8,128)S(1)}, u32[]{:S(2)}) copy-start(f32[512,512]{1,0:T(8,128)S(1)} %window.1.local_in) | copy-start | bytes 3145732
  48.5 6.6 %collective-permute-start.6 = (bf16[8,64,256]{2,1,0:T(8,128)(2,1)S(1)}, bf16[8,64,256]{2,1,0:T(8,128)(2,1)S(1)}, u32[]{:S(2)}, u32[]{:S(2)}) collective-permute-start(bf16[8,64,256]{2,1,0:T(8,128)(2,1)S(1)} %bitcast.12), channel_id=1, source_target_pairs={{0,1},{1,0},{2,3},{3,2},{4,5},{5,4},{6,7},{7,6},{8,9},{9,8},{10,11... | collective-permute-start | bytes 786440 | tf_op jit(solution)/shard_map/ppermute | solution.py:358
  51.0 4.8 %collective-permute-start.7 = (bf16[8,64,256]{2,1,0:T(8,128)(2,1)S(1)}, bf16[8,64,256]{2,1,0:T(8,128)(2,1)S(1)}, u32[]{:S(2)}, u32[]{:S(2)}) collective-permute-start(bf16[8,64,256]{2,1,0:T(8,128)(2,1)S(1)} %collective-permute-done.2.refs_2_), channel_id=1, source_target_pairs={{0,1},{1,0},{2,3},{3,2},{4,5},{5,4},{6,7},{7,6},{8,9},{9,8},{10,11... | collective-permute-start | bytes 786440 | tf_op jit(solution)/shard_map/ppermute | solution.py:358
  54.6 1.5 %collective-permute-start.9 = (bf16[8,64,256]{2,1,0:T(8,128)(2,1)S(1)}, bf16[8,64,256]{2,1,0:T(8,128)(2,1)S(1)}, u32[]{:S(2)}, u32[]{:S(2)}) collective-permute-start(bf16[8,64,256]{2,1,0:T(8,128)(2,1)S(1)} %collective-permute-done.8.refs_4_), channel_id=1, source_target_pairs={{0,1},{1,0},{2,3},{3,2},{4,5},{5,4},{6,7},{7,6},{8,9},{9,8},{10,11... | collective-permute-start | bytes 786440 | tf_op jit(solution)/shard_map/ppermute | solution.py:358
  54.7 1.8 %collective-permute-start.10 = (bf16[8,64,256]{2,1,0:T(8,128)(2,1)S(1)}, bf16[8,64,256]{2,1,0:T(8,128)(2,1)S(1)}, u32[]{:S(2)}, u32[]{:S(2)}) collective-permute-start(bf16[8,64,256]{2,1,0:T(8,128)(2,1)S(1)} %collective-permute-done.3.refs_6_), channel_id=1, source_target_pairs={{0,1},{1,0},{2,3},{3,2},{4,5},{5,4},{6,7},{7,6},{8,9},{9,8},{10,11... | collective-permute-start | bytes 786440 | tf_op jit(solution)/shard_map/ppermute | solution.py:358

commit v4 on v3

--- a/solution.py
+++ b/solution.py
@@ -151,7 +151,7 @@
 
 
 def window_kernel(
-    meta, q_in, gw_in, kv_in, s_own, s_from1, edge, out, q_ref, gw_ref, out_ref, both, sem
+    meta, q_in, gw_in, kv_in, s_own, s_from1, edge, out_ref, q_ref, gw_ref, both, sem
 ):
     toks = q_in.shape[0]
     near, here = pl.ds(0, toks), pl.ds(toks, toks)
@@ -191,7 +191,6 @@
             )
             g = gates[first : first + rows, 2 * HEADS + h : 2 * HEADS + h + 1]
             out_ref[first : first + rows, cols] = o * (g / total)
-    copy_all([(out_ref, out)], sem)
 
 
 SLOTS = ((0, 0), (0, 1), (1, 0), (1, 1), (2, 0), (2, 1), (3, 0), (3, 1))
@@ -224,7 +223,7 @@
     return acc * factor + o[:, :HEAD_DIM], total * factor + o[:, HEAD_DIM:], top
 
 
-ROWS = 128
+ROWS = 256
 WIDE = 256
 STEP = 4
 PARTS = (slice(0, 128), slice(128, 256), slice(256, 384))
@@ -454,12 +453,11 @@
         local = pl.pallas_call(
             window_kernel,
             in_specs=[SMEM] + [HBM] * 2 + [ANY] * 4,
-            out_specs=HBM,
+            out_specs=VMEM,
             out_shape=f32_rows,
             scratch_shapes=[
                 q_of,
                 gw_of,
-                pltpu.VMEM(queries.shape, jnp.float32),
                 kv_of,
                 pltpu.SemaphoreType.DMA((5,)),
             ],
@@ -482,7 +480,7 @@
 
         part = pl.pallas_call(
             coarse_kernel,
-            in_specs=[SMEM] + [HBM] * 3 + [ANY] * 8,
+            in_specs=[SMEM] + [HBM] * 2 + [ANY] * 9,
             out_specs=VMEM,
             out_shape=f32_rows,
             scratch_shapes=[
@@ -495,7 +493,7 @@
             ],
             compiler_params=params(24),
             name="coarse",
-        )(meta, queries, gate_weight, hbm(local), *(x for piece in pieces for x in (piece, cross(piece))))
+        )(meta, queries, gate_weight, local, *(x for piece in pieces for x in (piece, cross(piece))))
 
         return pl.pallas_call(
             fine_kernel,

time: 78.5 us -> 78.2 us (level)
  starting transfers between devices: 36.4 us -> 37.5 us
  local copies, waits for them, and re-layouts: 1.74 us -> 0.79 us
    ppermute x8, starting transfers between devices: 9.66 us -> 10.7 us  [cross(): return lax.ppermute(piece, AXES, swap)]
    unnamed x6 -> x4, local copies, waits for them, and re-layouts: 1.74 us -> 0.79 us
where the time goes in v4:
time: 78.2 us; the launch traced here: 77.7 us
  starting transfers between devices  37.5 us (48%)
  Pallas kernels  34.1 us (44%)
  waiting for transfers between devices  4.41 us (6%)
  local copies, waits for them, and re-layouts  0.79 us (1%)
    pallas_call x1, Pallas kernels, per_device(): pl.pallas_call(coarse_kernel, in_specs=[SMEM] + [HBM] * 2 + [ANY] * 9, ou...  14.7 us
    ppermute x8, starting transfers between devices, cross(): return lax.ppermute(piece, AXES, swap)  10.7 us
    ppermute x6, starting transfers between devices, spread(): return [lax.ppermute(piece, AXES, path) for path in (up, down, across)]  9.09 us
    all_to_all x1, starting transfers between devices, per_device(): lax.all_to_all(copies, 'blk', split_axis=0, concat_axis=0, tiled=True)  8.99 us
    all_to_all x1, starting transfers between devices, per_device(): lax.all_to_all(outgoing, 'blk', split_axis=0, concat_axis=0, tiled=True)  8.04 us
    pallas_call x1, Pallas kernels, per_device(): pl.pallas_call(fine_kernel, in_specs=[SMEM] + [HBM] * 2 + [VMEM, HBM, ANY...  6.23 us
    pallas_call x1, Pallas kernels, per_device(): pl.pallas_call(window_kernel, in_specs=[SMEM] + [HBM] * 2 + [ANY] * 4, ou...  4.83 us
    pallas_call x1, Pallas kernels, per_device(): pl.pallas_call(compress_kernel, in_specs=[HBM] * 7, out_specs=VMEM, out_s...  4.12 us
  transfers between devices with their start and end apart: 17, of which 8 were waited for; matrix products, arithmetic and copies ran while one was open for 0% of the time, Pallas kernels for 34%

profile of v4, /device:TPU:129, one launch (start us, length us, event | category | flops | bytes accessed | tf_op | source)
XLA Modules:
  0.0 77.7 jit_solution(4456084222138959680)
XLA Ops:
  0.0 0.6 pad_add_fusion.ids
  0.6 1.8 %prep.1 = (bf16[512,256]{1,0:T(8,128)(2,1)S(1)}, s32[1,384]{1,0:T(1,128)S(1)}) custom-call(s32[2]{0:T(128)} %pad_add_fusion.ids, bf16[512,128]{1,0:T(8,128)(2,1)} %keys_ref.3, bf16[512,128]{1,0:T(8,128)(2,1)} %values_ref.3, s32[16,256]{1,0:T(8,128)} %bitcast.26), custom_call_target="tpu_custom_call" | custom-call | tf_op jit(solution)/shard_map/prep/pallas_call | solution.py:390
  2.5 0.0 copy-start.1
  2.5 0.7 collective-permute-start
  3.1 1.4 %collective-permute-start.1 = (bf16[8,64,256]{2,1,0:T(8,128)(2,1)S(1)}, bf16[8,64,256]{2,1,0:T(8,128)(2,1)S(1)}, u32[]{:S(2)}, u32[]{:S(2)}) collective-permute-start(bf16[8,64,256]{2,1,0:T(8,128)(2,1)S(1)} %bitcast.15), channel_id=1, source_target_pairs={{0,1},{1,0},{2,3},{3,2},{4,5},{5,4},{6,7},{7,6},{8,9},{9,8},{10,11... | collective-permute-start | bytes 786440 | tf_op jit(solution)/shard_map/ppermute | solution.py:357
  4.5 0.7 collective-permute-start.4
  5.2 0.0 copy-done.1
  5.2 4.7 %collective-permute-start.11 = (bf16[8,64,256]{2,1,0:T(8,128)(2,1)S(1)}, bf16[8,64,256]{2,1,0:T(8,128)(2,1)S(1)}, u32[]{:S(2)}, u32[]{:S(2)}) collective-permute-start(bf16[8,64,256]{2,1,0:T(8,128)(2,1)S(1)} %bitcast.17), channel_id=1, source_target_pairs={{0,4},{1,5},{2,6},{3,7},{4,0},{5,1},{6,2},{7,3},{8,12},{9,13},{10,... | collective-permute-start | bytes 786440 | tf_op jit(solution)/shard_map/ppermute | solution.py:360
  9.9 0.0 collective-permute-start.13
  9.9 4.1 %compress.1 = bf16[32,16,256]{2,1,0:T(8,128)(2,1)} custom-call(bf16[512,128]{1,0:T(8,128)(2,1)} %keys_ref.3, bf16[512,128]{1,0:T(8,128)(2,1)} %values_ref.3, bf16[2,32,128]{2,1,0:T(8,128)(2,1)} %pos_ref.1, bf16[4096,256]{1,0:T(8,128)(2,1)} %k_in.1, bf16[256,128]{1,0:T(8,128)(2,1)} %k_out.1, bf16[4096,256]{1,0:T(8,128)(2,1)} %v_in.1, bf16[256,128]{1,0:T(8,128)(2,1)} %v_out.1), custom_call_target="tpu_custom_call" | custom-call | tf_op jit(solution)/shard_map/compress/pallas_call | solution.py:407
  14.1 0.0 collective-permute-done
  14.1 0.0 collective-permute-done.1.refs_1_
  14.1 9.0 %all-to-all-start = ((bf16[32,16,256]{2,1,0:T(8,128)(2,1)}), bf16[32,16,256]{2,1,0:T(8,128)(2,1)S(1)}, u32[]{:S(2)}, u32[]{:S(2)}) async-start(bf16[32,16,256]{2,1,0:T(8,128)(2,1)} %compress.1), calls=%async_computation | async-start | bytes 524288 | tf_op jit(solution)/shard_map/all_to_all | solution.py:429
  23.1 0.4 collective-permute-done.4.refs_2_
  23.5 1.2 %collective-permute-start.5 = (bf16[8,64,256]{2,1,0:T(8,128)(2,1)S(1)}, bf16[8,64,256]{2,1,0:T(8,128)(2,1)S(1)}, u32[]{:S(2)}, u32[]{:S(2)}) collective-permute-start(bf16[8,64,256]{2,1,0:T(8,128)(2,1)S(1)} %collective-permute-done.4.refs_2_), channel_id=1, source_target_pairs={{0,1},{1,0},{2,3},{3,2},{4,5},{5,4},{6,7},{7,6},{8,9},{9,8},{10,11... | collective-permute-start | bytes 786440 | tf_op jit(solution)/shard_map/ppermute | solution.py:357
  24.7 0.0 collective-permute-done.11.refs_4_
  24.7 0.1 collective-permute-start.12
  24.8 0.0 collective-permute-done.13.refs_6_
  24.8 0.4 collective-permute-start.14
  25.2 0.6 collective-permute-done.5.refs_3_
  25.9 0.4 collective-permute-done.12.refs_5_
  26.2 0.4 collective-permute-done.14.refs_7_
  26.6 2.4 %pick.1 = (bf16[32,64,256]{2,1,0:T(8,128)(2,1)}, bf16[16,64,256]{2,1,0:T(8,128)(2,1)S(1)}) custom-call(s32[1,384]{1,0:T(1,128)} %copy-done.1, bf16[8,64,256]{2,1,0:T(8,128)(2,1)S(1)} %bitcast.19, bf16[8,64,256]{2,1,0:T(8,128)(2,1)S(1)} %collective-permute-done.1.refs_1_, bf16[8,64,256]{2,1,0:T(8,128)(2,1)S(1)} %collective-permute-done.4.refs_2_, ...), custom_call_target="tpu_custom_call" | custom-call | tf_op jit(solution)/shard_map/pick/pallas_call | solution.py:432
  29.0 0.0 copy-start
  29.0 0.8 %copy-done = bf16[16,64,256]{2,1,0:T(8,128)(2,1)} copy-done((bf16[16,64,256]{2,1,0:T(8,128)(2,1)}, bf16[16,64,256]{2,1,0:T(8,128)(2,1)S(1)}, u32[]{:S(2)}) %copy-start) | copy-done | bytes 524312
  29.8 1.2 %all-to-all-done = bf16[32,16,256]{2,1,0:T(8,128)(2,1)S(1)} async-done(((bf16[32,16,256]{2,1,0:T(8,128)(2,1)}), bf16[32,16,256]{2,1,0:T(8,128)(2,1)S(1)}, u32[]{:S(2)}, u32[]{:S(2)}) %all-to-all-start) | async-done | bytes 262176 | tf_op jit(solution)/shard_map/all_to_all | solution.py:429
  31.0 8.0 %all-to-all-start.1 = ((bf16[32,64,256]{2,1,0:T(8,128)(2,1)}), bf16[32,64,256]{2,1,0:T(8,128)(2,1)S(1)}, u32[]{:S(2)}, u32[]{:S(2)}) async-start(bf16[32,64,256]{2,1,0:T(8,128)(2,1)} %get-tuple-element.24), calls=%async_computation.1 | async-start | bytes 2097152 | tf_op jit(solution)/shard_map/all_to_all | solution.py:447
  39.0 1.8 %collective-permute-start.2 = (bf16[8,64,256]{2,1,0:T(8,128)(2,1)S(1)}, bf16[8,64,256]{2,1,0:T(8,128)(2,1)S(1)}, u32[]{:S(2)}, u32[]{:S(2)}) collective-permute-start(bf16[8,64,256]{2,1,0:T(8,128)(2,1)S(1)} %bitcast.9), channel_id=1, source_target_pairs={{0,2},{1,3},{2,4},{3,5},{4,6},{5,7},{6,0},{7,1},{8,10},{9,11},{10,... | collective-permute-start | bytes 786440 | tf_op jit(solution)/shard_map/ppermute | solution.py:360
  40.8 0.9 %collective-permute-start.3 = (bf16[8,64,256]{2,1,0:T(8,128)(2,1)S(1)}, bf16[8,64,256]{2,1,0:T(8,128)(2,1)S(1)}, u32[]{:S(2)}, u32[]{:S(2)}) collective-permute-start(bf16[8,64,256]{2,1,0:T(8,128)(2,1)S(1)} %bitcast.10), channel_id=1, source_target_pairs={{0,6},{1,7},{2,0},{3,1},{4,2},{5,3},{6,4},{7,5},{8,14},{9,15},{10,... | collective-permute-start | bytes 786440 | tf_op jit(solution)/shard_map/ppermute | solution.py:360
  41.8 0.9 %collective-permute-start.8 = (bf16[8,64,256]{2,1,0:T(8,128)(2,1)S(1)}, bf16[8,64,256]{2,1,0:T(8,128)(2,1)S(1)}, u32[]{:S(2)}, u32[]{:S(2)}) collective-permute-start(bf16[8,64,256]{2,1,0:T(8,128)(2,1)S(1)} %bitcast.11), channel_id=1, source_target_pairs={{0,4},{1,5},{2,6},{3,7},{4,0},{5,1},{6,2},{7,3},{8,12},{9,13},{10,... | collective-permute-start | bytes 786440 | tf_op jit(solution)/shard_map/ppermute | solution.py:360
  42.7 4.8 %window.1.local_in = f32[512,512]{1,0:T(8,128)S(1)} custom-call(s32[1,384]{1,0:T(1,128)} %copy-done.1, bf16[512,512]{1,0:T(8,128)(2,1)} %q_in.5, bf16[12,512]{1,0:T(8,128)(2,1)} %bitcast.23, bf16[512,256]{1,0:T(8,128)(2,1)S(1)} %get-tuple-element.16.kv_in, bf16[512,256]{1,0:T(8,128)(2,1)S(1)} %bitcast.20, bf16[512,256]{1,0:T(8,128)(2,1)S(1)} %bitcast.21, ...), custom_call_target="tpu_custom_call" | custom-call | tf_op jit(solution)/shard_map/window/pallas_call | solution.py:453
  47.6 2.7 %collective-permute-start.6 = (bf16[8,64,256]{2,1,0:T(8,128)(2,1)S(1)}, bf16[8,64,256]{2,1,0:T(8,128)(2,1)S(1)}, u32[]{:S(2)}, u32[]{:S(2)}) collective-permute-start(bf16[8,64,256]{2,1,0:T(8,128)(2,1)S(1)} %bitcast.12), channel_id=1, source_target_pairs={{0,1},{1,0},{2,3},{3,2},{4,5},{5,4},{6,7},{7,6},{8,9},{9,8},{10,11... | collective-permute-start | bytes 786440 | tf_op jit(solution)/shard_map/ppermute | solution.py:357
  50.2 0.0 collective-permute-done.2.refs_2_
  50.2 0.0 collective-permute-done.3.refs_6_
  50.2 4.4 %collective-permute-start.7 = (bf16[8,64,256]{2,1,0:T(8,128)(2,1)S(1)}, bf16[8,64,256]{2,1,0:T(8,128)(2,1)S(1)}, u32[]{:S(2)}, u32[]{:S(2)}) collective-permute-start(bf16[8,64,256]{2,1,0:T(8,128)(2,1)S(1)} %collective-permute-done.2.refs_2_), channel_id=1, source_target_pairs={{0,1},{1,0},{2,3},{3,2},{4,5},{5,4},{6,7},{7,6},{8,9},{9,8},{10,11... | collective-permute-start | bytes 786440 | tf_op jit(solution)/shard_map/ppermute | solution.py:357
  54.6 0.0 collective-permute-done.8.refs_4_
  54.6 0.1 collective-permute-start.9
  54.7 0.4 collective-permute-start.10
  55.2 0.0 collective-permute-done.6.refs_1_
  55.2 0.6 collective-permute-done.7.refs_3_
  55.8 0.4 collective-permute-done.9.refs_5_
  56.2 0.4 collective-permute-done.10.refs_7_
  56.6 14.7 %coarse.1.part_ref = f32[512,512]{1,0:T(8,128)S(1)} custom-call(s32[1,384]{1,0:T(1,128)} %copy-done.1, bf16[512,512]{1,0:T(8,128)(2,1)} %q_in.5, bf16[12,512]{1,0:T(8,128)(2,1)} %bitcast.24, f32[512,512]{1,0:T(8,128)S(1)} %window.1.local_in, bf16[8,64,256]{2,1,0:T(8,128)(2,1)S(1)} %bitcast.13, bf16[8,64,256]{2,1,0:T(8,128)(2,1)S(1)} %collective-permute-done.6.refs_1_, ...), custom_call_target="tpu_custom_call" | custom-call | tf_op jit(solution)/shard_map/coarse/pallas_call | solution.py:481
  71.3 0.0 all-to-all-done.1.incoming
  71.3 6.2 %fine.1 = bf16[512,512]{1,0:T(8,128)(2,1)} custom-call(s32[1,384]{1,0:T(1,128)} %copy-done.1, bf16[512,512]{1,0:T(8,128)(2,1)} %q_in.5, bf16[12,512]{1,0:T(8,128)(2,1)} %bitcast.25, f32[512,512]{1,0:T(8,128)S(1)} %coarse.1.part_ref, bf16[16,64,256]{2,1,0:T(8,128)(2,1)} %copy-done, bf16[32,64,256]{2,1,0:T(8,128)(2,1)S(1)} %all-to-all-done.1.incoming), custom_call_target="tpu_custom_call" | custom-call | tf_op jit(solution)/shard_map/fine/pallas_call | solution.py:498
Async XLA Ops:
  2.5 2.8 %copy-start.1 = (s32[1,384]{1,0:T(1,128)}, s32[1,384]{1,0:T(1,128)S(1)}, u32[]{:S(2)}) copy-start(s32[1,384]{1,0:T(1,128)S(1)} %get-tuple-element.15.meta) | copy-start | bytes 4612
  2.5 11.6 %collective-permute-start = (bf16[8,64,256]{2,1,0:T(8,128)(2,1)S(1)}, bf16[8,64,256]{2,1,0:T(8,128)(2,1)S(1)}, u32[]{:S(2)}, u32[]{:S(2)}) collective-permute-start(bf16[8,64,256]{2,1,0:T(8,128)(2,1)S(1)} %bitcast.14), channel_id=1, source_target_pairs={{7,8},{15,16},{23,24},{31,32},{39,40},{47,48},{55,56},{63,64},{71,... | collective-permute-start | bytes 786440 | tf_op jit(solution)/shard_map/ppermute | solution.py:427
  3.1 10.9 %collective-permute-start.1 = (bf16[8,64,256]{2,1,0:T(8,128)(2,1)S(1)}, bf16[8,64,256]{2,1,0:T(8,128)(2,1)S(1)}, u32[]{:S(2)}, u32[]{:S(2)}) collective-permute-start(bf16[8,64,256]{2,1,0:T(8,128)(2,1)S(1)} %bitcast.15), channel_id=1, source_target_pairs={{0,1},{1,0},{2,3},{3,2},{4,5},{5,4},{6,7},{7,6},{8,9},{9,8},{10,11... | collective-permute-start | bytes 786440 | tf_op jit(solution)/shard_map/ppermute | solution.py:357
  4.5 19.0 %collective-permute-start.4 = (bf16[8,64,256]{2,1,0:T(8,128)(2,1)S(1)}, bf16[8,64,256]{2,1,0:T(8,128)(2,1)S(1)}, u32[]{:S(2)}, u32[]{:S(2)}) collective-permute-start(bf16[8,64,256]{2,1,0:T(8,128)(2,1)S(1)} %bitcast.16), channel_id=1, source_target_pairs={{0,2},{1,3},{2,4},{3,5},{4,6},{5,7},{6,0},{7,1},{8,10},{9,11},{10,... | collective-permute-start | bytes 786440 | tf_op jit(solution)/shard_map/ppermute | solution.py:360
  5.2 19.5 %collective-permute-start.11 = (bf16[8,64,256]{2,1,0:T(8,128)(2,1)S(1)}, bf16[8,64,256]{2,1,0:T(8,128)(2,1)S(1)}, u32[]{:S(2)}, u32[]{:S(2)}) collective-permute-start(bf16[8,64,256]{2,1,0:T(8,128)(2,1)S(1)} %bitcast.17), channel_id=1, source_target_pairs={{0,4},{1,5},{2,6},{3,7},{4,0},{5,1},{6,2},{7,3},{8,12},{9,13},{10,... | collective-permute-start | bytes 786440 | tf_op jit(solution)/shard_map/ppermute | solution.py:360
  9.9 14.9 %collective-permute-start.13 = (bf16[8,64,256]{2,1,0:T(8,128)(2,1)S(1)}, bf16[8,64,256]{2,1,0:T(8,128)(2,1)S(1)}, u32[]{:S(2)}, u32[]{:S(2)}) collective-permute-start(bf16[8,64,256]{2,1,0:T(8,128)(2,1)S(1)} %bitcast.18), channel_id=1, source_target_pairs={{0,6},{1,7},{2,0},{3,1},{4,2},{5,3},{6,4},{7,5},{8,14},{9,15},{10,... | collective-permute-start | bytes 786440 | tf_op jit(solution)/shard_map/ppermute | solution.py:360
  14.1 16.9 %all-to-all-start = ((bf16[32,16,256]{2,1,0:T(8,128)(2,1)}), bf16[32,16,256]{2,1,0:T(8,128)(2,1)S(1)}, u32[]{:S(2)}, u32[]{:S(2)}) async-start(bf16[32,16,256]{2,1,0:T(8,128)(2,1)} %compress.1), calls=%async_computation | async-start | bytes 524288 | tf_op jit(solution)/shard_map/all_to_all | solution.py:429
  23.5 2.4 %collective-permute-start.5 = (bf16[8,64,256]{2,1,0:T(8,128)(2,1)S(1)}, bf16[8,64,256]{2,1,0:T(8,128)(2,1)S(1)}, u32[]{:S(2)}, u32[]{:S(2)}) collective-permute-start(bf16[8,64,256]{2,1,0:T(8,128)(2,1)S(1)} %collective-permute-done.4.refs_2_), channel_id=1, source_target_pairs={{0,1},{1,0},{2,3},{3,2},{4,5},{5,4},{6,7},{7,6},{8,9},{9,8},{10,11... | collective-permute-start | bytes 786440 | tf_op jit(solution)/shard_map/ppermute | solution.py:357
  24.7 1.5 %collective-permute-start.12 = (bf16[8,64,256]{2,1,0:T(8,128)(2,1)S(1)}, bf16[8,64,256]{2,1,0:T(8,128)(2,1)S(1)}, u32[]{:S(2)}, u32[]{:S(2)}) collective-permute-start(bf16[8,64,256]{2,1,0:T(8,128)(2,1)S(1)} %collective-permute-done.11.refs_4_), channel_id=1, source_target_pairs={{0,1},{1,0},{2,3},{3,2},{4,5},{5,4},{6,7},{7,6},{8,9},{9,8},{10,11... | collective-permute-start | bytes 786440 | tf_op jit(solution)/shard_map/ppermute | solution.py:357
  24.8 1.8 %collective-permute-start.14 = (bf16[8,64,256]{2,1,0:T(8,128)(2,1)S(1)}, bf16[8,64,256]{2,1,0:T(8,128)(2,1)S(1)}, u32[]{:S(2)}, u32[]{:S(2)}) collective-permute-start(bf16[8,64,256]{2,1,0:T(8,128)(2,1)S(1)} %collective-permute-done.13.refs_6_), channel_id=1, source_target_pairs={{0,1},{1,0},{2,3},{3,2},{4,5},{5,4},{6,7},{7,6},{8,9},{9,8},{10,11... | collective-permute-start | bytes 786440 | tf_op jit(solution)/shard_map/ppermute | solution.py:357
  29.0 0.8 %copy-start = (bf16[16,64,256]{2,1,0:T(8,128)(2,1)}, bf16[16,64,256]{2,1,0:T(8,128)(2,1)S(1)}, u32[]{:S(2)}) copy-start(bf16[16,64,256]{2,1,0:T(8,128)(2,1)S(1)} %get-tuple-element.23.near_ref) | copy-start | bytes 1572868
  31.0 40.4 %all-to-all-start.1 = ((bf16[32,64,256]{2,1,0:T(8,128)(2,1)}), bf16[32,64,256]{2,1,0:T(8,128)(2,1)S(1)}, u32[]{:S(2)}, u32[]{:S(2)}) async-start(bf16[32,64,256]{2,1,0:T(8,128)(2,1)} %get-tuple-element.24), calls=%async_computation.1 | async-start | bytes 2097152 | tf_op jit(solution)/shard_map/all_to_all | solution.py:447
  39.0 11.2 %collective-permute-start.2 = (bf16[8,64,256]{2,1,0:T(8,128)(2,1)S(1)}, bf16[8,64,256]{2,1,0:T(8,128)(2,1)S(1)}, u32[]{:S(2)}, u32[]{:S(2)}) collective-permute-start(bf16[8,64,256]{2,1,0:T(8,128)(2,1)S(1)} %bitcast.9), channel_id=1, source_target_pairs={{0,2},{1,3},{2,4},{3,5},{4,6},{5,7},{6,0},{7,1},{8,10},{9,11},{10,... | collective-permute-start | bytes 786440 | tf_op jit(solution)/shard_map/ppermute | solution.py:360
  40.8 9.4 %collective-permute-start.3 = (bf16[8,64,256]{2,1,0:T(8,128)(2,1)S(1)}, bf16[8,64,256]{2,1,0:T(8,128)(2,1)S(1)}, u32[]{:S(2)}, u32[]{:S(2)}) collective-permute-start(bf16[8,64,256]{2,1,0:T(8,128)(2,1)S(1)} %bitcast.10), channel_id=1, source_target_pairs={{0,6},{1,7},{2,0},{3,1},{4,2},{5,3},{6,4},{7,5},{8,14},{9,15},{10,... | collective-permute-start | bytes 786440 | tf_op jit(solution)/shard_map/ppermute | solution.py:360
  41.8 12.9 %collective-permute-start.8 = (bf16[8,64,256]{2,1,0:T(8,128)(2,1)S(1)}, bf16[8,64,256]{2,1,0:T(8,128)(2,1)S(1)}, u32[]{:S(2)}, u32[]{:S(2)}) collective-permute-start(bf16[8,64,256]{2,1,0:T(8,128)(2,1)S(1)} %bitcast.11), channel_id=1, source_target_pairs={{0,4},{1,5},{2,6},{3,7},{4,0},{5,1},{6,2},{7,3},{8,12},{9,13},{10,... | collective-permute-start | bytes 786440 | tf_op jit(solution)/shard_map/ppermute | solution.py:360
  47.6 7.6 %collective-permute-start.6 = (bf16[8,64,256]{2,1,0:T(8,128)(2,1)S(1)}, bf16[8,64,256]{2,1,0:T(8,128)(2,1)S(1)}, u32[]{:S(2)}, u32[]{:S(2)}) collective-permute-start(bf16[8,64,256]{2,1,0:T(8,128)(2,1)S(1)} %bitcast.12), channel_id=1, source_target_pairs={{0,1},{1,0},{2,3},{3,2},{4,5},{5,4},{6,7},{7,6},{8,9},{9,8},{10,11... | collective-permute-start | bytes 786440 | tf_op jit(solution)/shard_map/ppermute | solution.py:357
  50.2 5.6 %collective-permute-start.7 = (bf16[8,64,256]{2,1,0:T(8,128)(2,1)S(1)}, bf16[8,64,256]{2,1,0:T(8,128)(2,1)S(1)}, u32[]{:S(2)}, u32[]{:S(2)}) collective-permute-start(bf16[8,64,256]{2,1,0:T(8,128)(2,1)S(1)} %collective-permute-done.2.refs_2_), channel_id=1, source_target_pairs={{0,1},{1,0},{2,3},{3,2},{4,5},{5,4},{6,7},{7,6},{8,9},{9,8},{10,11... | collective-permute-start | bytes 786440 | tf_op jit(solution)/shard_map/ppermute | solution.py:357
  54.6 1.5 %collective-permute-start.9 = (bf16[8,64,256]{2,1,0:T(8,128)(2,1)S(1)}, bf16[8,64,256]{2,1,0:T(8,128)(2,1)S(1)}, u32[]{:S(2)}, u32[]{:S(2)}) collective-permute-start(bf16[8,64,256]{2,1,0:T(8,128)(2,1)S(1)} %collective-permute-done.8.refs_4_), channel_id=1, source_target_pairs={{0,1},{1,0},{2,3},{3,2},{4,5},{5,4},{6,7},{7,6},{8,9},{9,8},{10,11... | collective-permute-start | bytes 786440 | tf_op jit(solution)/shard_map/ppermute | solution.py:357
  54.7 1.8 %collective-permute-start.10 = (bf16[8,64,256]{2,1,0:T(8,128)(2,1)S(1)}, bf16[8,64,256]{2,1,0:T(8,128)(2,1)S(1)}, u32[]{:S(2)}, u32[]{:S(2)}) collective-permute-start(bf16[8,64,256]{2,1,0:T(8,128)(2,1)S(1)} %collective-permute-done.3.refs_6_), channel_id=1, source_target_pairs={{0,1},{1,0},{2,3},{3,2},{4,5},{5,4},{6,7},{7,6},{8,9},{9,8},{10,11... | collective-permute-start | bytes 786440 | tf_op jit(solution)/shard_map/ppermute | solution.py:357

commit v5 on v4

--- a/solution.py
+++ b/solution.py
@@ -497,7 +497,7 @@
 
         return pl.pallas_call(
             fine_kernel,
-            in_specs=[SMEM] + [HBM] * 2 + [VMEM, HBM, ANY],
+            in_specs=[SMEM] + [HBM] * 2 + [VMEM, ANY, ANY],
             out_specs=HBM,
             out_shape=jax.ShapeDtypeStruct(queries.shape, jnp.bfloat16),
             scratch_shapes=[
@@ -511,7 +511,7 @@
             ],
             compiler_params=params(20),
             name="fine",
-        )(meta, queries, gate_weight, part, hbm(nearby), incoming)
+        )(meta, queries, gate_weight, part, nearby, incoming)
 
     rows = P(AXES, None)
     return jax.shard_map(

time: 78.2 us -> 78.1 us (level)
  waiting for transfers between devices: 4.41 us -> 5.22 us
    all_to_all x1, waiting for transfers between devices: 1.18 us -> 1.99 us  [per_device(): lax.all_to_all(copies, 'blk', split_axis=0, concat_axis=0, tiled=True)]
    unnamed x4 -> x2, local copies, waits for them, and re-layouts: 0.79 us -> 0.01 us
where the time goes in v5:
time: 78.1 us; the launch traced here: 77.6 us
  starting transfers between devices  37.4 us (48%)
  Pallas kernels  34.1 us (44%)
  waiting for transfers between devices  5.22 us (7%)
    pallas_call x1, Pallas kernels, per_device(): pl.pallas_call(coarse_kernel, in_specs=[SMEM] + [HBM] * 2 + [ANY] * 9, ou...  14.7 us
    ppermute x8, starting transfers between devices, cross(): return lax.ppermute(piece, AXES, swap)  11.2 us
    all_to_all x1, starting transfers between devices, per_device(): lax.all_to_all(copies, 'blk', split_axis=0, concat_axis=0, tiled=True)  8.99 us
    ppermute x6, starting transfers between devices, spread(): return [lax.ppermute(piece, AXES, path) for path in (up, down, across)]  8.64 us
    all_to_all x1, starting transfers between devices, per_device(): lax.all_to_all(outgoing, 'blk', split_axis=0, concat_axis=0, tiled=True)  7.96 us
    pallas_call x1, Pallas kernels, per_device(): pl.pallas_call(fine_kernel, in_specs=[SMEM] + [HBM] * 2 + [VMEM, ANY, ANY...  6.23 us
    pallas_call x1, Pallas kernels, per_device(): pl.pallas_call(window_kernel, in_specs=[SMEM] + [HBM] * 2 + [ANY] * 4, ou...  4.83 us
    pallas_call x1, Pallas kernels, per_device(): pl.pallas_call(compress_kernel, in_specs=[HBM] * 7, out_specs=VMEM, out_s...  4.12 us
  transfers between devices with their start and end apart: 17, of which 8 were waited for; matrix products, arithmetic and copies ran while one was open for 0% of the time, Pallas kernels for 34%

profile of v5, /device:TPU:129, one launch (start us, length us, event | category | flops | bytes accessed | tf_op | source)
XLA Modules:
  0.0 77.6 jit_solution(6100511490159525862)
XLA Ops:
  0.0 0.6 pad_add_fusion.ids
  0.6 1.8 %prep.1 = (bf16[512,256]{1,0:T(8,128)(2,1)S(1)}, s32[1,384]{1,0:T(1,128)S(1)}) custom-call(s32[2]{0:T(128)} %pad_add_fusion.ids, bf16[512,128]{1,0:T(8,128)(2,1)} %keys_ref.3, bf16[512,128]{1,0:T(8,128)(2,1)} %values_ref.3, s32[16,256]{1,0:T(8,128)} %bitcast.26), custom_call_target="tpu_custom_call" | custom-call | tf_op jit(solution)/shard_map/prep/pallas_call | solution.py:390
  2.4 0.0 copy-start
  2.4 0.7 collective-permute-start
  3.1 1.4 %collective-permute-start.1 = (bf16[8,64,256]{2,1,0:T(8,128)(2,1)S(1)}, bf16[8,64,256]{2,1,0:T(8,128)(2,1)S(1)}, u32[]{:S(2)}, u32[]{:S(2)}) collective-permute-start(bf16[8,64,256]{2,1,0:T(8,128)(2,1)S(1)} %bitcast.15), channel_id=1, source_target_pairs={{0,1},{1,0},{2,3},{3,2},{4,5},{5,4},{6,7},{7,6},{8,9},{9,8},{10,11... | collective-permute-start | bytes 786440 | tf_op jit(solution)/shard_map/ppermute | solution.py:357
  4.5 0.7 collective-permute-start.4
  5.2 0.0 copy-done
  5.2 4.7 %collective-permute-start.11 = (bf16[8,64,256]{2,1,0:T(8,128)(2,1)S(1)}, bf16[8,64,256]{2,1,0:T(8,128)(2,1)S(1)}, u32[]{:S(2)}, u32[]{:S(2)}) collective-permute-start(bf16[8,64,256]{2,1,0:T(8,128)(2,1)S(1)} %bitcast.17), channel_id=1, source_target_pairs={{0,4},{1,5},{2,6},{3,7},{4,0},{5,1},{6,2},{7,3},{8,12},{9,13},{10,... | collective-permute-start | bytes 786440 | tf_op jit(solution)/shard_map/ppermute | solution.py:360
  9.9 0.0 collective-permute-start.13
  9.9 4.1 %compress.1 = bf16[32,16,256]{2,1,0:T(8,128)(2,1)} custom-call(bf16[512,128]{1,0:T(8,128)(2,1)} %keys_ref.3, bf16[512,128]{1,0:T(8,128)(2,1)} %values_ref.3, bf16[2,32,128]{2,1,0:T(8,128)(2,1)} %pos_ref.1, bf16[4096,256]{1,0:T(8,128)(2,1)} %k_in.1, bf16[256,128]{1,0:T(8,128)(2,1)} %k_out.1, bf16[4096,256]{1,0:T(8,128)(2,1)} %v_in.1, bf16[256,128]{1,0:T(8,128)(2,1)} %v_out.1), custom_call_target="tpu_custom_call" | custom-call | tf_op jit(solution)/shard_map/compress/pallas_call | solution.py:407
  14.0 0.0 collective-permute-done
  14.0 0.0 collective-permute-done.1.refs_1_
  14.0 9.0 %all-to-all-start = ((bf16[32,16,256]{2,1,0:T(8,128)(2,1)}), bf16[32,16,256]{2,1,0:T(8,128)(2,1)S(1)}, u32[]{:S(2)}, u32[]{:S(2)}) async-start(bf16[32,16,256]{2,1,0:T(8,128)(2,1)} %compress.1), calls=%async_computation | async-start | bytes 524288 | tf_op jit(solution)/shard_map/all_to_all | solution.py:429
  23.0 0.4 collective-permute-done.4.refs_2_
  23.5 1.2 %collective-permute-start.5 = (bf16[8,64,256]{2,1,0:T(8,128)(2,1)S(1)}, bf16[8,64,256]{2,1,0:T(8,128)(2,1)S(1)}, u32[]{:S(2)}, u32[]{:S(2)}) collective-permute-start(bf16[8,64,256]{2,1,0:T(8,128)(2,1)S(1)} %collective-permute-done.4.refs_2_), channel_id=1, source_target_pairs={{0,1},{1,0},{2,3},{3,2},{4,5},{5,4},{6,7},{7,6},{8,9},{9,8},{10,11... | collective-permute-start | bytes 786440 | tf_op jit(solution)/shard_map/ppermute | solution.py:357
  24.7 0.0 collective-permute-done.11.refs_4_
  24.7 0.1 collective-permute-start.12
  24.8 0.0 collective-permute-done.13.refs_6_
  24.8 0.4 collective-permute-start.14
  25.2 0.6 collective-permute-done.5.refs_3_
  25.8 0.4 collective-permute-done.12.refs_5_
  26.2 0.4 collective-permute-done.14.refs_7_
  26.6 2.3 %pick.1 = (bf16[32,64,256]{2,1,0:T(8,128)(2,1)}, bf16[16,64,256]{2,1,0:T(8,128)(2,1)S(1)}) custom-call(s32[1,384]{1,0:T(1,128)} %copy-done, bf16[8,64,256]{2,1,0:T(8,128)(2,1)S(1)} %bitcast.19, bf16[8,64,256]{2,1,0:T(8,128)(2,1)S(1)} %collective-permute-done.1.refs_1_, bf16[8,64,256]{2,1,0:T(8,128)(2,1)S(1)} %collective-permute-done.4.refs_2_, ...), custom_call_target="tpu_custom_call" | custom-call | tf_op jit(solution)/shard_map/pick/pallas_call | solution.py:432
  28.9 2.0 %all-to-all-done = bf16[32,16,256]{2,1,0:T(8,128)(2,1)S(1)} async-done(((bf16[32,16,256]{2,1,0:T(8,128)(2,1)}), bf16[32,16,256]{2,1,0:T(8,128)(2,1)S(1)}, u32[]{:S(2)}, u32[]{:S(2)}) %all-to-all-start) | async-done | bytes 262176 | tf_op jit(solution)/shard_map/all_to_all | solution.py:429
  30.9 8.0 %all-to-all-start.1 = ((bf16[32,64,256]{2,1,0:T(8,128)(2,1)}), bf16[32,64,256]{2,1,0:T(8,128)(2,1)S(1)}, u32[]{:S(2)}, u32[]{:S(2)}) async-start(bf16[32,64,256]{2,1,0:T(8,128)(2,1)} %get-tuple-element.24), calls=%async_computation.1 | async-start | bytes 2097152 | tf_op jit(solution)/shard_map/all_to_all | solution.py:447
  38.9 1.4 %collective-permute-start.2 = (bf16[8,64,256]{2,1,0:T(8,128)(2,1)S(1)}, bf16[8,64,256]{2,1,0:T(8,128)(2,1)S(1)}, u32[]{:S(2)}, u32[]{:S(2)}) collective-permute-start(bf16[8,64,256]{2,1,0:T(8,128)(2,1)S(1)} %bitcast.9), channel_id=1, source_target_pairs={{0,2},{1,3},{2,4},{3,5},{4,6},{5,7},{6,0},{7,1},{8,10},{9,11},{10,... | collective-permute-start | bytes 786440 | tf_op jit(solution)/shard_map/ppermute | solution.py:360
  40.3 1.4 %collective-permute-start.3 = (bf16[8,64,256]{2,1,0:T(8,128)(2,1)S(1)}, bf16[8,64,256]{2,1,0:T(8,128)(2,1)S(1)}, u32[]{:S(2)}, u32[]{:S(2)}) collective-permute-start(bf16[8,64,256]{2,1,0:T(8,128)(2,1)S(1)} %bitcast.10), channel_id=1, source_target_pairs={{0,6},{1,7},{2,0},{3,1},{4,2},{5,3},{6,4},{7,5},{8,14},{9,15},{10,... | collective-permute-start | bytes 786440 | tf_op jit(solution)/shard_map/ppermute | solution.py:360
  41.7 0.5 collective-permute-start.8
  42.1 4.8 %window.1.local_in = f32[512,512]{1,0:T(8,128)S(1)} custom-call(s32[1,384]{1,0:T(1,128)} %copy-done, bf16[512,512]{1,0:T(8,128)(2,1)} %q_in.5, bf16[12,512]{1,0:T(8,128)(2,1)} %bitcast.23, bf16[512,256]{1,0:T(8,128)(2,1)S(1)} %get-tuple-element.16.kv_in, bf16[512,256]{1,0:T(8,128)(2,1)S(1)} %bitcast.20, bf16[512,256]{1,0:T(8,128)(2,1)S(1)} %bitcast.21, ...), custom_call_target="tpu_custom_call" | custom-call | tf_op jit(solution)/shard_map/window/pallas_call | solution.py:453
  47.0 3.2 %collective-permute-start.6 = (bf16[8,64,256]{2,1,0:T(8,128)(2,1)S(1)}, bf16[8,64,256]{2,1,0:T(8,128)(2,1)S(1)}, u32[]{:S(2)}, u32[]{:S(2)}) collective-permute-start(bf16[8,64,256]{2,1,0:T(8,128)(2,1)S(1)} %bitcast.12), channel_id=1, source_target_pairs={{0,1},{1,0},{2,3},{3,2},{4,5},{5,4},{6,7},{7,6},{8,9},{9,8},{10,11... | collective-permute-start | bytes 786440 | tf_op jit(solution)/shard_map/ppermute | solution.py:357
  50.2 0.0 collective-permute-done.2.refs_2_
  50.2 0.0 collective-permute-done.3.refs_6_
  50.2 4.3 %collective-permute-start.7 = (bf16[8,64,256]{2,1,0:T(8,128)(2,1)S(1)}, bf16[8,64,256]{2,1,0:T(8,128)(2,1)S(1)}, u32[]{:S(2)}, u32[]{:S(2)}) collective-permute-start(bf16[8,64,256]{2,1,0:T(8,128)(2,1)S(1)} %collective-permute-done.2.refs_2_), channel_id=1, source_target_pairs={{0,1},{1,0},{2,3},{3,2},{4,5},{5,4},{6,7},{7,6},{8,9},{9,8},{10,11... | collective-permute-start | bytes 786440 | tf_op jit(solution)/shard_map/ppermute | solution.py:357
  54.5 0.0 collective-permute-done.8.refs_4_
  54.5 0.1 collective-permute-start.9
  54.6 0.4 collective-permute-start.10
  55.1 0.0 collective-permute-done.6.refs_1_
  55.1 0.6 collective-permute-done.7.refs_3_
  55.7 0.4 collective-permute-done.9.refs_5_
  56.1 0.4 collective-permute-done.10.refs_7_
  56.5 14.7 %coarse.1.part_ref = f32[512,512]{1,0:T(8,128)S(1)} custom-call(s32[1,384]{1,0:T(1,128)} %copy-done, bf16[512,512]{1,0:T(8,128)(2,1)} %q_in.5, bf16[12,512]{1,0:T(8,128)(2,1)} %bitcast.24, f32[512,512]{1,0:T(8,128)S(1)} %window.1.local_in, bf16[8,64,256]{2,1,0:T(8,128)(2,1)S(1)} %bitcast.13, bf16[8,64,256]{2,1,0:T(8,128)(2,1)S(1)} %collective-permute-done.6.refs_1_, ...), custom_call_target="tpu_custom_call" | custom-call | tf_op jit(solution)/shard_map/coarse/pallas_call | solution.py:481
  71.2 0.0 all-to-all-done.1.incoming
  71.2 6.2 %fine.1 = bf16[512,512]{1,0:T(8,128)(2,1)} custom-call(s32[1,384]{1,0:T(1,128)} %copy-done, bf16[512,512]{1,0:T(8,128)(2,1)} %q_in.5, bf16[12,512]{1,0:T(8,128)(2,1)} %bitcast.25, f32[512,512]{1,0:T(8,128)S(1)} %coarse.1.part_ref, bf16[16,64,256]{2,1,0:T(8,128)(2,1)S(1)} %get-tuple-element.23.near_ref, bf16[32,64,256]{2,1,0:T(8,128)(2,1)S(1)} %all-to-all-done.1.incoming), custom_call_target="tpu_custom_call" | custom-call | tf_op jit(solution)/shard_map/fine/pallas_call | solution.py:498
Async XLA Ops:
  2.4 2.8 %copy-start = (s32[1,384]{1,0:T(1,128)}, s32[1,384]{1,0:T(1,128)S(1)}, u32[]{:S(2)}) copy-start(s32[1,384]{1,0:T(1,128)S(1)} %get-tuple-element.15.meta) | copy-start | bytes 4612
  2.4 11.6 %collective-permute-start = (bf16[8,64,256]{2,1,0:T(8,128)(2,1)S(1)}, bf16[8,64,256]{2,1,0:T(8,128)(2,1)S(1)}, u32[]{:S(2)}, u32[]{:S(2)}) collective-permute-start(bf16[8,64,256]{2,1,0:T(8,128)(2,1)S(1)} %bitcast.14), channel_id=1, source_target_pairs={{7,8},{15,16},{23,24},{31,32},{39,40},{47,48},{55,56},{63,64},{71,... | collective-permute-start | bytes 786440 | tf_op jit(solution)/shard_map/ppermute | solution.py:427
  3.1 10.9 %collective-permute-start.1 = (bf16[8,64,256]{2,1,0:T(8,128)(2,1)S(1)}, bf16[8,64,256]{2,1,0:T(8,128)(2,1)S(1)}, u32[]{:S(2)}, u32[]{:S(2)}) collective-permute-start(bf16[8,64,256]{2,1,0:T(8,128)(2,1)S(1)} %bitcast.15), channel_id=1, source_target_pairs={{0,1},{1,0},{2,3},{3,2},{4,5},{5,4},{6,7},{7,6},{8,9},{9,8},{10,11... | collective-permute-start | bytes 786440 | tf_op jit(solution)/shard_map/ppermute | solution.py:357
  4.5 19.0 %collective-permute-start.4 = (bf16[8,64,256]{2,1,0:T(8,128)(2,1)S(1)}, bf16[8,64,256]{2,1,0:T(8,128)(2,1)S(1)}, u32[]{:S(2)}, u32[]{:S(2)}) collective-permute-start(bf16[8,64,256]{2,1,0:T(8,128)(2,1)S(1)} %bitcast.16), channel_id=1, source_target_pairs={{0,2},{1,3},{2,4},{3,5},{4,6},{5,7},{6,0},{7,1},{8,10},{9,11},{10,... | collective-permute-start | bytes 786440 | tf_op jit(solution)/shard_map/ppermute | solution.py:360
  5.2 19.5 %collective-permute-start.11 = (bf16[8,64,256]{2,1,0:T(8,128)(2,1)S(1)}, bf16[8,64,256]{2,1,0:T(8,128)(2,1)S(1)}, u32[]{:S(2)}, u32[]{:S(2)}) collective-permute-start(bf16[8,64,256]{2,1,0:T(8,128)(2,1)S(1)} %bitcast.17), channel_id=1, source_target_pairs={{0,4},{1,5},{2,6},{3,7},{4,0},{5,1},{6,2},{7,3},{8,12},{9,13},{10,... | collective-permute-start | bytes 786440 | tf_op jit(solution)/shard_map/ppermute | solution.py:360
  9.9 14.9 %collective-permute-start.13 = (bf16[8,64,256]{2,1,0:T(8,128)(2,1)S(1)}, bf16[8,64,256]{2,1,0:T(8,128)(2,1)S(1)}, u32[]{:S(2)}, u32[]{:S(2)}) collective-permute-start(bf16[8,64,256]{2,1,0:T(8,128)(2,1)S(1)} %bitcast.18), channel_id=1, source_target_pairs={{0,6},{1,7},{2,0},{3,1},{4,2},{5,3},{6,4},{7,5},{8,14},{9,15},{10,... | collective-permute-start | bytes 786440 | tf_op jit(solution)/shard_map/ppermute | solution.py:360
  14.0 16.9 %all-to-all-start = ((bf16[32,16,256]{2,1,0:T(8,128)(2,1)}), bf16[32,16,256]{2,1,0:T(8,128)(2,1)S(1)}, u32[]{:S(2)}, u32[]{:S(2)}) async-start(bf16[32,16,256]{2,1,0:T(8,128)(2,1)} %compress.1), calls=%async_computation | async-start | bytes 524288 | tf_op jit(solution)/shard_map/all_to_all | solution.py:429
  23.5 2.4 %collective-permute-start.5 = (bf16[8,64,256]{2,1,0:T(8,128)(2,1)S(1)}, bf16[8,64,256]{2,1,0:T(8,128)(2,1)S(1)}, u32[]{:S(2)}, u32[]{:S(2)}) collective-permute-start(bf16[8,64,256]{2,1,0:T(8,128)(2,1)S(1)} %collective-permute-done.4.refs_2_), channel_id=1, source_target_pairs={{0,1},{1,0},{2,3},{3,2},{4,5},{5,4},{6,7},{7,6},{8,9},{9,8},{10,11... | collective-permute-start | bytes 786440 | tf_op jit(solution)/shard_map/ppermute | solution.py:357
  24.7 1.5 %collective-permute-start.12 = (bf16[8,64,256]{2,1,0:T(8,128)(2,1)S(1)}, bf16[8,64,256]{2,1,0:T(8,128)(2,1)S(1)}, u32[]{:S(2)}, u32[]{:S(2)}) collective-permute-start(bf16[8,64,256]{2,1,0:T(8,128)(2,1)S(1)} %collective-permute-done.11.refs_4_), channel_id=1, source_target_pairs={{0,1},{1,0},{2,3},{3,2},{4,5},{5,4},{6,7},{7,6},{8,9},{9,8},{10,11... | collective-permute-start | bytes 786440 | tf_op jit(solution)/shard_map/ppermute | solution.py:357
  24.8 1.8 %collective-permute-start.14 = (bf16[8,64,256]{2,1,0:T(8,128)(2,1)S(1)}, bf16[8,64,256]{2,1,0:T(8,128)(2,1)S(1)}, u32[]{:S(2)}, u32[]{:S(2)}) collective-permute-start(bf16[8,64,256]{2,1,0:T(8,128)(2,1)S(1)} %collective-permute-done.13.refs_6_), channel_id=1, source_target_pairs={{0,1},{1,0},{2,3},{3,2},{4,5},{5,4},{6,7},{7,6},{8,9},{9,8},{10,11... | collective-permute-start | bytes 786440 | tf_op jit(solution)/shard_map/ppermute | solution.py:357
  30.9 40.3 %all-to-all-start.1 = ((bf16[32,64,256]{2,1,0:T(8,128)(2,1)}), bf16[32,64,256]{2,1,0:T(8,128)(2,1)S(1)}, u32[]{:S(2)}, u32[]{:S(2)}) async-start(bf16[32,64,256]{2,1,0:T(8,128)(2,1)} %get-tuple-element.24), calls=%async_computation.1 | async-start | bytes 2097152 | tf_op jit(solution)/shard_map/all_to_all | solution.py:447
  38.9 11.3 %collective-permute-start.2 = (bf16[8,64,256]{2,1,0:T(8,128)(2,1)S(1)}, bf16[8,64,256]{2,1,0:T(8,128)(2,1)S(1)}, u32[]{:S(2)}, u32[]{:S(2)}) collective-permute-start(bf16[8,64,256]{2,1,0:T(8,128)(2,1)S(1)} %bitcast.9), channel_id=1, source_target_pairs={{0,2},{1,3},{2,4},{3,5},{4,6},{5,7},{6,0},{7,1},{8,10},{9,11},{10,... | collective-permute-start | bytes 786440 | tf_op jit(solution)/shard_map/ppermute | solution.py:360
  40.3 9.9 %collective-permute-start.3 = (bf16[8,64,256]{2,1,0:T(8,128)(2,1)S(1)}, bf16[8,64,256]{2,1,0:T(8,128)(2,1)S(1)}, u32[]{:S(2)}, u32[]{:S(2)}) collective-permute-start(bf16[8,64,256]{2,1,0:T(8,128)(2,1)S(1)} %bitcast.10), channel_id=1, source_target_pairs={{0,6},{1,7},{2,0},{3,1},{4,2},{5,3},{6,4},{7,5},{8,14},{9,15},{10,... | collective-permute-start | bytes 786440 | tf_op jit(solution)/shard_map/ppermute | solution.py:360
  41.7 12.9 %collective-permute-start.8 = (bf16[8,64,256]{2,1,0:T(8,128)(2,1)S(1)}, bf16[8,64,256]{2,1,0:T(8,128)(2,1)S(1)}, u32[]{:S(2)}, u32[]{:S(2)}) collective-permute-start(bf16[8,64,256]{2,1,0:T(8,128)(2,1)S(1)} %bitcast.11), channel_id=1, source_target_pairs={{0,4},{1,5},{2,6},{3,7},{4,0},{5,1},{6,2},{7,3},{8,12},{9,13},{10,... | collective-permute-start | bytes 786440 | tf_op jit(solution)/shard_map/ppermute | solution.py:360
  47.0 8.1 %collective-permute-start.6 = (bf16[8,64,256]{2,1,0:T(8,128)(2,1)S(1)}, bf16[8,64,256]{2,1,0:T(8,128)(2,1)S(1)}, u32[]{:S(2)}, u32[]{:S(2)}) collective-permute-start(bf16[8,64,256]{2,1,0:T(8,128)(2,1)S(1)} %bitcast.12), channel_id=1, source_target_pairs={{0,1},{1,0},{2,3},{3,2},{4,5},{5,4},{6,7},{7,6},{8,9},{9,8},{10,11... | collective-permute-start | bytes 786440 | tf_op jit(solution)/shard_map/ppermute | solution.py:357
  50.2 5.5 %collective-permute-start.7 = (bf16[8,64,256]{2,1,0:T(8,128)(2,1)S(1)}, bf16[8,64,256]{2,1,0:T(8,128)(2,1)S(1)}, u32[]{:S(2)}, u32[]{:S(2)}) collective-permute-start(bf16[8,64,256]{2,1,0:T(8,128)(2,1)S(1)} %collective-permute-done.2.refs_2_), channel_id=1, source_target_pairs={{0,1},{1,0},{2,3},{3,2},{4,5},{5,4},{6,7},{7,6},{8,9},{9,8},{10,11... | collective-permute-start | bytes 786440 | tf_op jit(solution)/shard_map/ppermute | solution.py:357
  54.5 1.5 %collective-permute-start.9 = (bf16[8,64,256]{2,1,0:T(8,128)(2,1)S(1)}, bf16[8,64,256]{2,1,0:T(8,128)(2,1)S(1)}, u32[]{:S(2)}, u32[]{:S(2)}) collective-permute-start(bf16[8,64,256]{2,1,0:T(8,128)(2,1)S(1)} %collective-permute-done.8.refs_4_), channel_id=1, source_target_pairs={{0,1},{1,0},{2,3},{3,2},{4,5},{5,4},{6,7},{7,6},{8,9},{9,8},{10,11... | collective-permute-start | bytes 786440 | tf_op jit(solution)/shard_map/ppermute | solution.py:357
  54.6 1.8 %collective-permute-start.10 = (bf16[8,64,256]{2,1,0:T(8,128)(2,1)S(1)}, bf16[8,64,256]{2,1,0:T(8,128)(2,1)S(1)}, u32[]{:S(2)}, u32[]{:S(2)}) collective-permute-start(bf16[8,64,256]{2,1,0:T(8,128)(2,1)S(1)} %collective-permute-done.3.refs_6_), channel_id=1, source_target_pairs={{0,1},{1,0},{2,3},{3,2},{4,5},{5,4},{6,7},{7,6},{8,9},{9,8},{10,11... | collective-permute-start | bytes 786440 | tf_op jit(solution)/shard_map/ppermute | solution.py:357
